TPU v7x, 256 devices: a whole 4x4x8 slice. The times are simulated.
256 devices in a mesh: pipe: 16 (over z, core), tensor: 16 (over y, x).
Axes of the slice: x: 4, y: 4, z: 8, core: 2. Of those that a mesh axis runs over, the one named last changes fastest.
Arguments:
- section_inputs: bfloat16 [16, 8, 128, 12288], P('pipe', None, None, 'tensor'), may hold values from -6 to 6
- out_grad: bfloat16 [8, 128, 12288], P(None, None, 'tensor'), may hold values from -6 to 6
- w_first: bfloat16 [16, 1, 96, 128, 128], P('pipe', None, 'tensor'), may hold values from -0.5 to 0.5
- w_second: bfloat16 [16, 1, 96, 128, 128], P('pipe', None, 'tensor'), may hold values from -0.5 to 0.5
- drop_flags: int32 [16, 1], P('pipe'), may hold values 0 or 1
- perm: int32 [16, 1, 12288], P('pipe'), may hold values from 0 to 12287, as said below
Outputs:
- input_grads: bfloat16 [16, 8, 128, 12288], P('pipe', None, None, 'tensor')
- grad_first: float32 [16, 1, 96, 128, 128], P('pipe', None, 'tensor')
- grad_second: float32 [16, 1, 96, 128, 128], P('pipe', None, 'tensor')
Inputs may be any that keep to these rules, and one draw needn't show every extreme that they name: For each section and layer, perm is a permutation of 0 to 12287, and for every two block groups g and h exactly 48 of the positions h * 768 to (h + 1) * 768 - 1 hold a feature of group g, that is a number from g * 768 to (g + 1) * 768 - 1.
All inputs are finite; a program needn't handle non-finite values. No bound on the sum of `drop_flags` on one device may be relied on, other than what follows from the above.
Results may differ from a plain program's by a relative error of at most 0.023.
Values may be sent and summed in bfloat16 or wider, within the bound.
No kernel may reach another device: no remote copies, remote signals or barrier semaphores. Data moves between devices by JAX's collectives and lax.ppermute only.
A program may use at most 128 MiB of HBM per device.

v0:
```python
import jax
import jax.numpy as jnp
from jax import lax
from jax.sharding import PartitionSpec as P

gelu_scale = 0.7978845608028654
gelu_cubic = 0.044715


def passed_along(block, axis, distance):
    devices = range(lax.axis_size(axis))
    route = [(i - distance, i) for i in devices if i - distance in devices]
    return lax.ppermute(block, axis, route)


def gelu_value(values):
    inner = gelu_scale * (values + gelu_cubic * values * values * values)
    return 0.5 * values * (1.0 + jnp.tanh(inner))


def gelu_slope(values):
    tangent = jnp.tanh(gelu_scale * (values + gelu_cubic * values * values * values))
    return 0.5 * (1.0 + tangent) + 0.5 * values * (1.0 - tangent * tangent) * gelu_scale * (
        1.0 + 3.0 * gelu_cubic * values * values
    )


def block_forward(values, weight):
    count = weight.shape[0]
    result = jnp.einsum(
        "tbi,bij->tbj",
        values.reshape(values.shape[0], count, -1),
        weight,
        preferred_element_type=jnp.float32,
    )
    return result.reshape(values.shape[0], -1)


def block_backward(values, weight):
    count = weight.shape[0]
    result = jnp.einsum(
        "tbj,bij->tbi",
        values.reshape(values.shape[0], count, -1),
        weight,
        preferred_element_type=jnp.float32,
    )
    return result.reshape(values.shape[0], -1)


def block_outer(left, right, count):
    left_blocks = left.reshape(left.shape[0], count, -1)
    right_blocks = right.reshape(right.shape[0], count, -1)
    return jnp.einsum("tbi,tbj->bij", left_blocks, right_blocks, preferred_element_type=jnp.float32)


def route_tables(source_row, group_index, group_count):
    feat_count = source_row.shape[0] // group_count
    per_peer = feat_count // group_count
    target_rows = source_row.reshape(group_count, feat_count)
    source_group = target_rows // feat_count
    position = jnp.arange(feat_count, dtype=jnp.int32)
    ranking = jnp.where(
        source_group == group_index, position[None, :], feat_count + position[None, :]
    )
    chosen = jnp.argsort(ranking, axis=1)[:, :per_peer]
    send_index = (
        jnp.take_along_axis(target_rows, chosen, axis=1) - group_index * feat_count
    ).reshape(-1)
    own_row = lax.dynamic_slice_in_dim(target_rows, group_index, 1, 0)[0]
    arrival = jnp.argsort(own_row // feat_count * feat_count + position)
    placing = jnp.argsort(arrival)
    gathering = jnp.argsort(send_index)
    return (send_index, arrival, placing, gathering)


def on_device(section_inputs, out_grad, w_first, w_second, drop_flags, perm):
    section_count = lax.axis_size("pipe")
    section_index = lax.axis_index("pipe")
    group_count = lax.axis_size("tensor")
    group_index = lax.axis_index("tensor")
    micro_count = section_inputs.shape[1]
    local_inputs = section_inputs[0]
    first_weights = w_first[0]
    second_weights = w_second[0]
    tables = [route_tables(perm[0, 0], group_index, group_count)]

    def mix_forward(hidden, layer_index):
        send_index, arrival, placing, gathering = tables[layer_index]
        outgoing = jnp.take(hidden, send_index, axis=1)
        mixed = jnp.take(
            lax.all_to_all(outgoing, "tensor", split_axis=1, concat_axis=1, tiled=True),
            placing,
            axis=1,
        )
        branch = block_forward(mixed, second_weights[layer_index])
        return (mixed, branch)

    def mix_backward(grad_mixed, layer_index):
        send_index, arrival, placing, gathering = tables[layer_index]
        returned = lax.all_to_all(
            jnp.take(grad_mixed, arrival, axis=1), "tensor", split_axis=1, concat_axis=1, tiled=True
        )
        return jnp.take(returned, gathering, axis=1)

    block_count = first_weights.shape[1]

    def layer_forward(current, layer_index):
        keep_factor = drop_flags[0, layer_index].astype(jnp.float32)
        before = block_forward(current, first_weights[layer_index])
        hidden = gelu_value(before).astype(jnp.bfloat16)
        mixed, branch = mix_forward(hidden, layer_index)
        following = (current.astype(jnp.float32) + keep_factor * branch).astype(jnp.bfloat16)
        return (following, before, mixed)

    def layer_backward(grad_now, current, before, mixed, layer_index):
        keep_factor = drop_flags[0, layer_index].astype(jnp.float32)
        grad_branch = (keep_factor * grad_now.astype(jnp.float32)).astype(jnp.bfloat16)
        second_part = block_outer(mixed, grad_branch, block_count)
        grad_mixed = block_backward(grad_branch, second_weights[layer_index]).astype(jnp.bfloat16)
        grad_hidden = mix_backward(grad_mixed, layer_index)
        grad_before = (grad_hidden.astype(jnp.float32) * gelu_slope(before)).astype(jnp.bfloat16)
        first_part = block_outer(current, grad_before, block_count)
        back_term = block_backward(grad_before, first_weights[layer_index])
        grad_prior = (grad_now.astype(jnp.float32) + back_term).astype(jnp.bfloat16)
        return (grad_prior, first_part, second_part)

    def run_section(first_input, cotangent):
        layer_inputs = [first_input]
        layer_index = 0
        current = layer_inputs[-1]
        following, before, mixed = layer_forward(current, layer_index)
        layer_inputs.append(following)
        saved_pairs = [(before, mixed)]
        grad_now = cotangent
        layer_index = 0
        current = layer_inputs[layer_index]
        before, mixed = saved_pairs[layer_index]
        grad_now, first_part, second_part = layer_backward(
            grad_now, current, before, mixed, layer_index
        )
        first_list = [first_part]
        second_list = [second_part]
        return (grad_now, jnp.stack(first_list[::-1]), jnp.stack(second_list[::-1]))

    def advance(step_index, carry):
        outgoing, buffer, sum_first, sum_second = carry
        incoming = passed_along(outgoing, "pipe", -1)
        micro_index = step_index - (section_count - 1 - section_index)
        live = (micro_index >= 0) & (micro_index < micro_count)
        clipped = jnp.clip(micro_index, 0, micro_count - 1)
        first_input = lax.dynamic_index_in_dim(local_inputs, clipped, 0, keepdims=False)
        last_grad = lax.dynamic_index_in_dim(out_grad, clipped, 0, keepdims=False)
        cotangent = jnp.where(section_index == section_count - 1, last_grad, incoming)
        grad_in, first_parts, second_parts = run_section(first_input, cotangent)
        previous = lax.dynamic_index_in_dim(buffer, clipped, 0, keepdims=False)
        buffer = lax.dynamic_update_index_in_dim(
            buffer, jnp.where(live, grad_in, previous), clipped, 0
        )
        sum_first = sum_first + jnp.where(live, first_parts, 0.0)
        sum_second = sum_second + jnp.where(live, second_parts, 0.0)
        return (grad_in, buffer, sum_first, sum_second)

    start = (
        jnp.zeros(local_inputs.shape[1:], jnp.bfloat16),
        jnp.zeros(local_inputs.shape, jnp.bfloat16),
        jnp.zeros(first_weights.shape, jnp.float32),
        jnp.zeros(second_weights.shape, jnp.float32),
    )
    step_count = micro_count + section_count - 1
    outgoing, buffer, sum_first, sum_second = lax.fori_loop(0, step_count, advance, start)
    return (buffer[None], sum_first[None], sum_second[None])


def solution(mesh):
    placed = (
        P("pipe", None, None, "tensor"),
        P(None, None, "tensor"),
        P("pipe", None, "tensor", None, None),
        P("pipe", None, "tensor", None, None),
        P("pipe", None),
        P("pipe", None, None),
    )
    return jax.shard_map(
        on_device,
        mesh=mesh,
        in_specs=placed,
        out_specs=(
            P("pipe", None, None, "tensor"),
            P("pipe", None, "tensor", None, None),
            P("pipe", None, "tensor", None, None),
        ),
        check_vma=False,
    )
```

profile of v0, /device:TPU:1, one launch (start us, length us, event | category | flops | bytes accessed | tf_op | source)
XLA Modules:
  0.0 966.8 jit_solution(11102775969191306429)
XLA Ops:
  23.5 6.3 gather_fusion.4
  36.4 922.6 %while.22 = (s32[]{:T(128)}, bf16[128,768]{0,1:T(8,128)(2,1)S(1)}, bf16[8,128,768]{2,1,0:T(8,128)(2,1)}, f32[1,6,128,128]{3,2,1,0:T(8,128)S(1)}, f32[1,6,128,128...) while((s32[]{:T(128)}, bf16[128,768]{0,1:T(8,128)(2,1)S(1)}, ...), condition=%wide.region_5.7_spmd.clone, body=%wide.region_4.6_spmd.clone.sunk | while | flops 130087944 | bytes 15419767 | solution.py:170
  47.8 6.8 all-to-all-start
  54.5 7.2 all-to-all-done
  71.6 6.0 all-to-all-done.1
  94.9 7.1 all-to-all-done
  135.0 7.1 all-to-all-done
  175.1 7.1 all-to-all-done
  215.3 7.1 all-to-all-done
  255.4 7.1 all-to-all-done
  295.6 7.1 all-to-all-done
  312.7 5.7 all-to-all-done.1
  335.7 7.1 all-to-all-done
  352.8 5.7 all-to-all-done.1
  375.8 7.1 all-to-all-done
  415.8 7.1 all-to-all-done
  432.9 5.7 all-to-all-done.1
  455.6 7.1 all-to-all-done
  495.1 7.1 all-to-all-done
  512.2 5.7 all-to-all-done.1
  534.2 7.1 all-to-all-done
  573.4 7.1 all-to-all-done
  590.4 5.7 all-to-all-done.1
  612.5 7.1 all-to-all-done
  652.7 7.1 all-to-all-done
  692.9 7.1 all-to-all-done
  733.0 7.1 all-to-all-done
  773.2 7.1 all-to-all-done
  813.4 7.1 all-to-all-done
  853.6 7.1 all-to-all-done
  893.8 7.1 all-to-all-done
  933.9 7.1 all-to-all-done
  (880 shorter events, 734.3 us)
Async XLA Ops:
  47.8 14.0 %all-to-all-start = ((bf16[128,16,48]{0,2,1:T(8,128)(2,1)}), bf16[128,16,48]{0,2,1:T(8,128)(2,1)S(1)}, u32[]{:S(2)}, u32[]{:S(2)}) async-start(bf16[128,16,48]{0,2,1:T(8,128)(2,1)} %bitcast.127), calls=%async_computation | async-start | bytes 393216 | tf_op jit(solution)/shard_map/while/body/eval_jaxpr/all_to_all | solution.py:100
  66.7 11.0 %all-to-all-start.1 = ((bf16[128,16,48]{0,2,1:T(8,128)(2,1)}), bf16[128,16,48]{0,2,1:T(8,128)(2,1)S(1)}, u32[]{:S(2)}, u32[]{:S(2)}) async-start(bf16[128,16,48]{0,2,1:T(8,128)(2,1)} %bitcast.130), calls=%async_computation.1 | async-start | bytes 393216 | tf_op jit(solution)/shard_map/while/body/eval_jaxpr/all_to_all | solution.py:91
  91.4 10.7 %all-to-all-start = ((bf16[128,16,48]{0,2,1:T(8,128)(2,1)}), bf16[128,16,48]{0,2,1:T(8,128)(2,1)S(1)}, u32[]{:S(2)}, u32[]{:S(2)}) async-start(bf16[128,16,48]{0,2,1:T(8,128)(2,1)} %bitcast.127), calls=%async_computation | async-start | bytes 393216 | tf_op jit(solution)/shard_map/while/body/eval_jaxpr/all_to_all | solution.py:100
  107.0 10.7 %all-to-all-start.1 = ((bf16[128,16,48]{0,2,1:T(8,128)(2,1)}), bf16[128,16,48]{0,2,1:T(8,128)(2,1)S(1)}, u32[]{:S(2)}, u32[]{:S(2)}) async-start(bf16[128,16,48]{0,2,1:T(8,128)(2,1)} %bitcast.130), calls=%async_computation.1 | async-start | bytes 393216 | tf_op jit(solution)/shard_map/while/body/eval_jaxpr/all_to_all | solution.py:91
  131.5 10.7 %all-to-all-start = ((bf16[128,16,48]{0,2,1:T(8,128)(2,1)}), bf16[128,16,48]{0,2,1:T(8,128)(2,1)S(1)}, u32[]{:S(2)}, u32[]{:S(2)}) async-start(bf16[128,16,48]{0,2,1:T(8,128)(2,1)} %bitcast.127), calls=%async_computation | async-start | bytes 393216 | tf_op jit(solution)/shard_map/while/body/eval_jaxpr/all_to_all | solution.py:100
  147.1 10.7 %all-to-all-start.1 = ((bf16[128,16,48]{0,2,1:T(8,128)(2,1)}), bf16[128,16,48]{0,2,1:T(8,128)(2,1)S(1)}, u32[]{:S(2)}, u32[]{:S(2)}) async-start(bf16[128,16,48]{0,2,1:T(8,128)(2,1)} %bitcast.130), calls=%async_computation.1 | async-start | bytes 393216 | tf_op jit(solution)/shard_map/while/body/eval_jaxpr/all_to_all | solution.py:91
  171.6 10.7 %all-to-all-start = ((bf16[128,16,48]{0,2,1:T(8,128)(2,1)}), bf16[128,16,48]{0,2,1:T(8,128)(2,1)S(1)}, u32[]{:S(2)}, u32[]{:S(2)}) async-start(bf16[128,16,48]{0,2,1:T(8,128)(2,1)} %bitcast.127), calls=%async_computation | async-start | bytes 393216 | tf_op jit(solution)/shard_map/while/body/eval_jaxpr/all_to_all | solution.py:100
  187.2 10.7 %all-to-all-start.1 = ((bf16[128,16,48]{0,2,1:T(8,128)(2,1)}), bf16[128,16,48]{0,2,1:T(8,128)(2,1)S(1)}, u32[]{:S(2)}, u32[]{:S(2)}) async-start(bf16[128,16,48]{0,2,1:T(8,128)(2,1)} %bitcast.130), calls=%async_computation.1 | async-start | bytes 393216 | tf_op jit(solution)/shard_map/while/body/eval_jaxpr/all_to_all | solution.py:91
  211.7 10.7 %all-to-all-start = ((bf16[128,16,48]{0,2,1:T(8,128)(2,1)}), bf16[128,16,48]{0,2,1:T(8,128)(2,1)S(1)}, u32[]{:S(2)}, u32[]{:S(2)}) async-start(bf16[128,16,48]{0,2,1:T(8,128)(2,1)} %bitcast.127), calls=%async_computation | async-start | bytes 393216 | tf_op jit(solution)/shard_map/while/body/eval_jaxpr/all_to_all | solution.py:100
  227.4 10.7 %all-to-all-start.1 = ((bf16[128,16,48]{0,2,1:T(8,128)(2,1)}), bf16[128,16,48]{0,2,1:T(8,128)(2,1)S(1)}, u32[]{:S(2)}, u32[]{:S(2)}) async-start(bf16[128,16,48]{0,2,1:T(8,128)(2,1)} %bitcast.130), calls=%async_computation.1 | async-start | bytes 393216 | tf_op jit(solution)/shard_map/while/body/eval_jaxpr/all_to_all | solution.py:91
  251.9 10.7 %all-to-all-start = ((bf16[128,16,48]{0,2,1:T(8,128)(2,1)}), bf16[128,16,48]{0,2,1:T(8,128)(2,1)S(1)}, u32[]{:S(2)}, u32[]{:S(2)}) async-start(bf16[128,16,48]{0,2,1:T(8,128)(2,1)} %bitcast.127), calls=%async_computation | async-start | bytes 393216 | tf_op jit(solution)/shard_map/while/body/eval_jaxpr/all_to_all | solution.py:100
  267.5 10.7 %all-to-all-start.1 = ((bf16[128,16,48]{0,2,1:T(8,128)(2,1)}), bf16[128,16,48]{0,2,1:T(8,128)(2,1)S(1)}, u32[]{:S(2)}, u32[]{:S(2)}) async-start(bf16[128,16,48]{0,2,1:T(8,128)(2,1)} %bitcast.130), calls=%async_computation.1 | async-start | bytes 393216 | tf_op jit(solution)/shard_map/while/body/eval_jaxpr/all_to_all | solution.py:91
  292.1 10.7 %all-to-all-start = ((bf16[128,16,48]{0,2,1:T(8,128)(2,1)}), bf16[128,16,48]{0,2,1:T(8,128)(2,1)S(1)}, u32[]{:S(2)}, u32[]{:S(2)}) async-start(bf16[128,16,48]{0,2,1:T(8,128)(2,1)} %bitcast.127), calls=%async_computation | async-start | bytes 393216 | tf_op jit(solution)/shard_map/while/body/eval_jaxpr/all_to_all | solution.py:100
  307.7 10.7 %all-to-all-start.1 = ((bf16[128,16,48]{0,2,1:T(8,128)(2,1)}), bf16[128,16,48]{0,2,1:T(8,128)(2,1)S(1)}, u32[]{:S(2)}, u32[]{:S(2)}) async-start(bf16[128,16,48]{0,2,1:T(8,128)(2,1)} %bitcast.130), calls=%async_computation.1 | async-start | bytes 393216 | tf_op jit(solution)/shard_map/while/body/eval_jaxpr/all_to_all | solution.py:91
  332.2 10.7 %all-to-all-start = ((bf16[128,16,48]{0,2,1:T(8,128)(2,1)}), bf16[128,16,48]{0,2,1:T(8,128)(2,1)S(1)}, u32[]{:S(2)}, u32[]{:S(2)}) async-start(bf16[128,16,48]{0,2,1:T(8,128)(2,1)} %bitcast.127), calls=%async_computation | async-start | bytes 393216 | tf_op jit(solution)/shard_map/while/body/eval_jaxpr/all_to_all | solution.py:100
  347.8 10.7 %all-to-all-start.1 = ((bf16[128,16,48]{0,2,1:T(8,128)(2,1)}), bf16[128,16,48]{0,2,1:T(8,128)(2,1)S(1)}, u32[]{:S(2)}, u32[]{:S(2)}) async-start(bf16[128,16,48]{0,2,1:T(8,128)(2,1)} %bitcast.130), calls=%async_computation.1 | async-start | bytes 393216 | tf_op jit(solution)/shard_map/while/body/eval_jaxpr/all_to_all | solution.py:91
  372.3 10.7 %all-to-all-start = ((bf16[128,16,48]{0,2,1:T(8,128)(2,1)}), bf16[128,16,48]{0,2,1:T(8,128)(2,1)S(1)}, u32[]{:S(2)}, u32[]{:S(2)}) async-start(bf16[128,16,48]{0,2,1:T(8,128)(2,1)} %bitcast.127), calls=%async_computation | async-start | bytes 393216 | tf_op jit(solution)/shard_map/while/body/eval_jaxpr/all_to_all | solution.py:100
  452.1 10.7 %all-to-all-start = ((bf16[128,16,48]{0,2,1:T(8,128)(2,1)}), bf16[128,16,48]{0,2,1:T(8,128)(2,1)S(1)}, u32[]{:S(2)}, u32[]{:S(2)}) async-start(bf16[128,16,48]{0,2,1:T(8,128)(2,1)} %bitcast.127), calls=%async_computation | async-start | bytes 393216 | tf_op jit(solution)/shard_map/while/body/eval_jaxpr/all_to_all | solution.py:100
  467.7 10.7 %all-to-all-start.1 = ((bf16[128,16,48]{0,2,1:T(8,128)(2,1)}), bf16[128,16,48]{0,2,1:T(8,128)(2,1)S(1)}, u32[]{:S(2)}, u32[]{:S(2)}) async-start(bf16[128,16,48]{0,2,1:T(8,128)(2,1)} %bitcast.130), calls=%async_computation.1 | async-start | bytes 393216 | tf_op jit(solution)/shard_map/while/body/eval_jaxpr/all_to_all | solution.py:91
  491.6 10.7 %all-to-all-start = ((bf16[128,16,48]{0,2,1:T(8,128)(2,1)}), bf16[128,16,48]{0,2,1:T(8,128)(2,1)S(1)}, u32[]{:S(2)}, u32[]{:S(2)}) async-start(bf16[128,16,48]{0,2,1:T(8,128)(2,1)} %bitcast.127), calls=%async_computation | async-start | bytes 393216 | tf_op jit(solution)/shard_map/while/body/eval_jaxpr/all_to_all | solution.py:100
  507.2 10.7 %all-to-all-start.1 = ((bf16[128,16,48]{0,2,1:T(8,128)(2,1)}), bf16[128,16,48]{0,2,1:T(8,128)(2,1)S(1)}, u32[]{:S(2)}, u32[]{:S(2)}) async-start(bf16[128,16,48]{0,2,1:T(8,128)(2,1)} %bitcast.130), calls=%async_computation.1 | async-start | bytes 393216 | tf_op jit(solution)/shard_map/while/body/eval_jaxpr/all_to_all | solution.py:91
  569.8 10.7 %all-to-all-start = ((bf16[128,16,48]{0,2,1:T(8,128)(2,1)}), bf16[128,16,48]{0,2,1:T(8,128)(2,1)S(1)}, u32[]{:S(2)}, u32[]{:S(2)}) async-start(bf16[128,16,48]{0,2,1:T(8,128)(2,1)} %bitcast.127), calls=%async_computation | async-start | bytes 393216 | tf_op jit(solution)/shard_map/while/body/eval_jaxpr/all_to_all | solution.py:100
  585.5 10.7 %all-to-all-start.1 = ((bf16[128,16,48]{0,2,1:T(8,128)(2,1)}), bf16[128,16,48]{0,2,1:T(8,128)(2,1)S(1)}, u32[]{:S(2)}, u32[]{:S(2)}) async-start(bf16[128,16,48]{0,2,1:T(8,128)(2,1)} %bitcast.130), calls=%async_computation.1 | async-start | bytes 393216 | tf_op jit(solution)/shard_map/while/body/eval_jaxpr/all_to_all | solution.py:91
  609.0 10.7 %all-to-all-start = ((bf16[128,16,48]{0,2,1:T(8,128)(2,1)}), bf16[128,16,48]{0,2,1:T(8,128)(2,1)S(1)}, u32[]{:S(2)}, u32[]{:S(2)}) async-start(bf16[128,16,48]{0,2,1:T(8,128)(2,1)} %bitcast.127), calls=%async_computation | async-start | bytes 393216 | tf_op jit(solution)/shard_map/while/body/eval_jaxpr/all_to_all | solution.py:100
  624.6 10.7 %all-to-all-start.1 = ((bf16[128,16,48]{0,2,1:T(8,128)(2,1)}), bf16[128,16,48]{0,2,1:T(8,128)(2,1)S(1)}, u32[]{:S(2)}, u32[]{:S(2)}) async-start(bf16[128,16,48]{0,2,1:T(8,128)(2,1)} %bitcast.130), calls=%async_computation.1 | async-start | bytes 393216 | tf_op jit(solution)/shard_map/while/body/eval_jaxpr/all_to_all | solution.py:91
  649.1 10.7 %all-to-all-start = ((bf16[128,16,48]{0,2,1:T(8,128)(2,1)}), bf16[128,16,48]{0,2,1:T(8,128)(2,1)S(1)}, u32[]{:S(2)}, u32[]{:S(2)}) async-start(bf16[128,16,48]{0,2,1:T(8,128)(2,1)} %bitcast.127), calls=%async_computation | async-start | bytes 393216 | tf_op jit(solution)/shard_map/while/body/eval_jaxpr/all_to_all | solution.py:100
  664.8 10.7 %all-to-all-start.1 = ((bf16[128,16,48]{0,2,1:T(8,128)(2,1)}), bf16[128,16,48]{0,2,1:T(8,128)(2,1)S(1)}, u32[]{:S(2)}, u32[]{:S(2)}) async-start(bf16[128,16,48]{0,2,1:T(8,128)(2,1)} %bitcast.130), calls=%async_computation.1 | async-start | bytes 393216 | tf_op jit(solution)/shard_map/while/body/eval_jaxpr/all_to_all | solution.py:91
  689.3 10.7 %all-to-all-start = ((bf16[128,16,48]{0,2,1:T(8,128)(2,1)}), bf16[128,16,48]{0,2,1:T(8,128)(2,1)S(1)}, u32[]{:S(2)}, u32[]{:S(2)}) async-start(bf16[128,16,48]{0,2,1:T(8,128)(2,1)} %bitcast.127), calls=%async_computation | async-start | bytes 393216 | tf_op jit(solution)/shard_map/while/body/eval_jaxpr/all_to_all | solution.py:100
  705.0 10.7 %all-to-all-start.1 = ((bf16[128,16,48]{0,2,1:T(8,128)(2,1)}), bf16[128,16,48]{0,2,1:T(8,128)(2,1)S(1)}, u32[]{:S(2)}, u32[]{:S(2)}) async-start(bf16[128,16,48]{0,2,1:T(8,128)(2,1)} %bitcast.130), calls=%async_computation.1 | async-start | bytes 393216 | tf_op jit(solution)/shard_map/while/body/eval_jaxpr/all_to_all | solution.py:91
  729.5 10.7 %all-to-all-start = ((bf16[128,16,48]{0,2,1:T(8,128)(2,1)}), bf16[128,16,48]{0,2,1:T(8,128)(2,1)S(1)}, u32[]{:S(2)}, u32[]{:S(2)}) async-start(bf16[128,16,48]{0,2,1:T(8,128)(2,1)} %bitcast.127), calls=%async_computation | async-start | bytes 393216 | tf_op jit(solution)/shard_map/while/body/eval_jaxpr/all_to_all | solution.py:100
  745.1 10.7 %all-to-all-start.1 = ((bf16[128,16,48]{0,2,1:T(8,128)(2,1)}), bf16[128,16,48]{0,2,1:T(8,128)(2,1)S(1)}, u32[]{:S(2)}, u32[]{:S(2)}) async-start(bf16[128,16,48]{0,2,1:T(8,128)(2,1)} %bitcast.130), calls=%async_computation.1 | async-start | bytes 393216 | tf_op jit(solution)/shard_map/while/body/eval_jaxpr/all_to_all | solution.py:91
  785.3 10.7 %all-to-all-start.1 = ((bf16[128,16,48]{0,2,1:T(8,128)(2,1)}), bf16[128,16,48]{0,2,1:T(8,128)(2,1)S(1)}, u32[]{:S(2)}, u32[]{:S(2)}) async-start(bf16[128,16,48]{0,2,1:T(8,128)(2,1)} %bitcast.130), calls=%async_computation.1 | async-start | bytes 393216 | tf_op jit(solution)/shard_map/while/body/eval_jaxpr/all_to_all | solution.py:91
  (42 other events, 369.4 us)
Sparse Core Ops, SparseCore 0:
  11.0 3.5 sort.69.cloned.1.call-done
  (1 shorter events, 0.0 us)
where the time goes:
time: 979 us; the launch traced here: 967 us
  waiting for transfers between devices  374 us (38%)
  local copies, waits for them, and re-layouts  258 us (26%)
  starting transfers between devices  213 us (22%)
  other arithmetic  73.8 us (8%)
  matrix products  27.5 us (3%)
  between operations  14.8 us (2%)
    all_to_all x23, waiting for transfers between devices, mix_backward(): lax.all_to_all(jnp.take(grad_mixed, arrival, axis=1), 'tensor', split_axi...  164 us
    all_to_all x23, waiting for transfers between devices, mix_forward(): lax.all_to_all(outgoing, 'tensor', split_axis=1, concat_axis=1, tiled=True)  131 us
    all_to_all x23, starting transfers between devices, mix_backward(): lax.all_to_all(jnp.take(grad_mixed, arrival, axis=1), 'tensor', split_axi...  84.3 us
    all_to_all x23, starting transfers between devices, mix_forward(): lax.all_to_all(outgoing, 'tensor', split_axis=1, concat_axis=1, tiled=True)  81 us
    ppermute x23, waiting for transfers between devices, passed_along(): return lax.ppermute(block, axis, route)  78.7 us
    ppermute x23, starting transfers between devices, passed_along(): return lax.ppermute(block, axis, route)  47.4 us
    gather x23, local copies, waits for them, and re-layouts, mix_forward(): outgoing = jnp.take(hidden, send_index, axis=1)  43.2 us
    gather x23, local copies, waits for them, and re-layouts, mix_backward(): jnp.take(grad_mixed, arrival, axis=1)  43.2 us
  transfers between devices with their start and end apart: 69, of which 69 were waited for; matrix products, arithmetic and copies ran while one was open for 10% of the time, Pallas kernels for 0%

commit v1 on v0

v1 whole, which is shorter than its diff:
```python
import functools

import jax
import jax.numpy as jnp
from jax import lax
from jax.experimental import pallas as pl
from jax.experimental.pallas import tpu as pltpu
from jax.sharding import PartitionSpec as P

gelu_scale = 0.7978845608028654
gelu_cubic = 0.044715
bf16 = jnp.bfloat16
f32 = jnp.float32


def dot(left, right, dims):
    return lax.dot_general(left, right, (dims, ((), ())), preferred_element_type=f32)


NN = ((1,), (0,))
NT = ((1,), (1,))
TN = ((0,), (0,))


def whole(space=pltpu.VMEM):
    return pl.BlockSpec(memory_space=space)


def prep_kernel(group_ref, drop_ref, perm_ref, w1_ref, w2_ref, w1d_ref, w2d_ref, pick_first_ref, pick_second_ref):
    groups, feats = perm_ref.shape
    blocks, size, _ = w1_ref.shape
    per_peer = feats // groups
    own_group = group_ref[0]
    keep = drop_ref[0].astype(f32)
    base = own_group * feats
    rows = lax.broadcasted_iota(jnp.int32, (feats, feats), 0)
    cols = lax.broadcasted_iota(jnp.int32, (feats, feats), 1)
    before = jnp.where(rows < cols, 1.0, 0.0).astype(bf16)
    perm = perm_ref[...]
    mine = (perm >= base) & (perm < base + feats)
    rank = dot(jnp.where(mine, 1.0, 0.0).astype(bf16), before, NN)
    rank = jnp.where(mine, rank, -1.0).astype(jnp.int32)
    local = (perm - base).astype(f32)
    counter = lax.broadcasted_iota(jnp.int32, (per_peer, feats), 0)
    lane = lax.broadcasted_iota(jnp.int32, (per_peer, feats), 1)
    for peer in range(groups):
        hit = counter == rank[peer : peer + 1, :]
        source = jnp.sum(jnp.where(hit, local[peer : peer + 1, :], 0.0), axis=1, keepdims=True)
        pick_first_ref[peer * per_peer : (peer + 1) * per_peer, :] = jnp.where(
            lane == source.astype(jnp.int32), 1.0, 0.0
        ).astype(bf16)
    own = perm_ref[pl.ds(own_group, 1), :]
    start = lax.broadcasted_iota(jnp.int32, (groups, feats), 0)
    from_group = (own >= start * feats) & (own < start * feats + feats)
    marks = jnp.where(from_group, 1.0, 0.0)
    place = dot(marks.astype(bf16), before, NN) + start.astype(f32) * per_peer
    slot = jnp.sum(marks * place, axis=0, keepdims=True).astype(jnp.int32)
    arrive = jnp.where(rows == slot, 1.0, 0.0)
    arrive_bf = arrive.astype(bf16)
    pick_second_ref[...] = jnp.transpose(arrive).astype(bf16)
    for block in range(blocks):
        span = slice(block * size, (block + 1) * size)
        w1d_ref[:, span] = dot(pick_first_ref[:, span], w1_ref[block], NT).astype(bf16)
        w2d_ref[:, span] = (keep * dot(arrive_bf[:, span], w2_ref[block], NN)).astype(bf16)


def forward_kernel(x_ref, w1d_ref, hidden_ref, slope_ref):
    groups, _, per_peer, tokens = hidden_ref.shape
    v = dot(w1d_ref[...], x_ref[0], NT)
    u = jnp.tanh(gelu_scale * (v + gelu_cubic * v * v * v))
    hidden = (0.5 * v * (1.0 + u)).astype(bf16)
    hidden_ref[...] = hidden.reshape(groups, 1, per_peer, tokens)
    slope_ref[0] = 0.5 * (1.0 + u) + 0.5 * v * (1.0 - u * u) * gelu_scale * (1.0 + 3.0 * gelu_cubic * v * v)


def send_kernel(step_ref, where_ref, incoming_ref, out_grad_ref, w2d_ref, gin_old, gin_ref, mixed_ref):
    del gin_old
    last = where_ref[1] == 1
    g = jnp.where(last, out_grad_ref[0], incoming_ref[...])
    gin_ref[0] = g
    groups, per_peer, tokens = mixed_ref.shape
    mixed_ref[...] = dot(w2d_ref[...], g, NT).astype(bf16).reshape(groups, per_peer, tokens)


def receive_kernel(step_ref, where_ref, returned_ref, slope_ref, w1d_ref, gin_ref, da_old, gout_old, da_ref, gout_ref, g_ref):
    del da_old, gout_old
    groups, per_peer, tokens = returned_ref.shape
    dh = returned_ref[...].reshape(groups * per_peer, tokens).astype(f32)
    da = jnp.transpose(dh * slope_ref[0]).astype(bf16)
    da_ref[0] = da
    g = (gin_ref[0].astype(f32) + dot(da, w1d_ref[...], NN)).astype(bf16)
    gout_ref[0] = g
    g_ref[...] = g


def grad_kernel(start_ref, drop_ref, x_ref, da_ref, z_ref, gin_ref, gout_ref, pick_first_ref, pick_second_ref, grads_ref, first_ref, second_ref):
    micro = pl.program_id(0)
    blocks, size, _ = first_ref.shape
    keep = drop_ref[0].astype(f32)
    grads_ref[0] = gout_ref[0]
    da = dot(da_ref[0], pick_first_ref[...], NN).astype(bf16)
    groups, _, per_peer, tokens = z_ref.shape
    z = dot(pick_second_ref[...], z_ref[...].reshape(groups * per_peer, tokens), NN).astype(bf16)
    x = x_ref[0]
    g = gin_ref[0]

    @pl.when(micro == 0)
    def _():
        first_ref[...] = jnp.zeros_like(first_ref)
        second_ref[...] = jnp.zeros_like(second_ref)

    for block in range(blocks):
        span = slice(block * size, (block + 1) * size)
        first_ref[block] += dot(x[:, span], da[:, span], TN)
        second_ref[block] += keep * dot(z[span, :], g[:, span], NN)


def on_device(section_inputs, out_grad, w_first, w_second, drop_flags, perm):
    sections = lax.axis_size("pipe")
    section = lax.axis_index("pipe").astype(jnp.int32)
    groups = lax.axis_size("tensor")
    group = lax.axis_index("tensor").astype(jnp.int32)
    x = section_inputs[0]
    micros, tokens, feats = x.shape
    blocks, size = w_first.shape[2], w_first.shape[3]
    per_peer = feats // groups
    steps = micros + sections - 1
    drop = drop_flags.reshape(1)
    sds = jax.ShapeDtypeStruct
    params = pltpu.CompilerParams(vmem_limit_bytes=24 * 1024 * 1024)

    w1d, w2d, pick_first, pick_second = pl.pallas_call(
        prep_kernel,
        in_specs=[whole(pltpu.SMEM), whole(pltpu.SMEM), whole(), whole(), whole()],
        out_specs=[whole()] * 4,
        out_shape=[sds((feats, feats), bf16)] * 4,
        compiler_params=params,
        name="prep",
    )(group.reshape(1), drop, perm.reshape(groups, feats), w_first[0, 0], w_second[0, 0])

    hidden, slope = pl.pallas_call(
        forward_kernel,
        grid=(micros,),
        in_specs=[
            pl.BlockSpec((1, tokens, feats), lambda m: (m, 0, 0)),
            pl.BlockSpec((feats, feats), lambda m: (0, 0)),
        ],
        out_specs=[
            pl.BlockSpec((groups, 1, per_peer, tokens), lambda m: (0, m, 0, 0)),
            pl.BlockSpec((1, feats, tokens), lambda m: (m, 0, 0)),
        ],
        out_shape=[sds((groups, micros, per_peer, tokens), bf16), sds((micros, feats, tokens), f32)],
        compiler_params=params,
        name="forward",
    )(x, w1d)
    z = lax.all_to_all(hidden, "tensor", 0, 0, tiled=True)

    where = jnp.stack([sections - 1 - section, (section == sections - 1).astype(jnp.int32)])

    def pick(k, w):
        return jnp.clip(k[0] - w[0], 0, micros - 1)

    send = pl.pallas_call(
        send_kernel,
        grid_spec=pltpu.PrefetchScalarGridSpec(
            num_scalar_prefetch=2,
            grid=(1,),
            in_specs=[
                pl.BlockSpec((tokens, feats), lambda i, k, w: (0, 0)),
                pl.BlockSpec((1, tokens, feats), lambda i, k, w: (pick(k, w), 0, 0)),
                pl.BlockSpec((feats, feats), lambda i, k, w: (0, 0)),
                whole(pl.ANY),
            ],
            out_specs=[
                pl.BlockSpec((1, tokens, feats), lambda i, k, w: (k[0], 0, 0)),
                pl.BlockSpec((groups, per_peer, tokens), lambda i, k, w: (0, 0, 0)),
            ],
        ),
        out_shape=[sds((steps, tokens, feats), bf16), sds((groups, per_peer, tokens), bf16)],
        input_output_aliases={5: 0},
        compiler_params=params,
        name="send",
    )
    receive = pl.pallas_call(
        receive_kernel,
        grid_spec=pltpu.PrefetchScalarGridSpec(
            num_scalar_prefetch=2,
            grid=(1,),
            in_specs=[
                pl.BlockSpec((groups, per_peer, tokens), lambda i, k, w: (0, 0, 0)),
                pl.BlockSpec((1, feats, tokens), lambda i, k, w: (pick(k, w), 0, 0)),
                pl.BlockSpec((feats, feats), lambda i, k, w: (0, 0)),
                pl.BlockSpec((1, tokens, feats), lambda i, k, w: (k[0], 0, 0)),
                whole(pl.ANY),
                whole(pl.ANY),
            ],
            out_specs=[
                pl.BlockSpec((1, tokens, feats), lambda i, k, w: (k[0], 0, 0)),
                pl.BlockSpec((1, tokens, feats), lambda i, k, w: (k[0], 0, 0)),
                pl.BlockSpec((tokens, feats), lambda i, k, w: (0, 0)),
            ],
        ),
        out_shape=[sds((steps, tokens, feats), bf16)] * 2 + [sds((tokens, feats), bf16)],
        input_output_aliases={6: 0, 7: 1},
        compiler_params=params,
        name="receive",
    )
    route = [(i, i - 1) for i in range(1, sections)]

    def advance(k, carry):
        g, gin, da, gout = carry
        at = jnp.full((1,), k, jnp.int32)
        incoming = lax.ppermute(g, "pipe", route)
        gin, outgoing = send(at, where, incoming, out_grad, w2d, gin)
        returned = lax.all_to_all(outgoing, "tensor", 0, 0, tiled=True)
        da, gout, g = receive(at, where, returned, slope, w1d, gin, da, gout)
        return (g, gin, da, gout)

    def blank():
        return jnp.zeros((steps, tokens, feats), bf16)

    _, gin, da, gout = lax.fori_loop(
        0, steps, advance, (jnp.zeros((tokens, feats), bf16), blank(), blank(), blank())
    )

    grads, first, second = pl.pallas_call(
        grad_kernel,
        grid_spec=pltpu.PrefetchScalarGridSpec(
            num_scalar_prefetch=2,
            grid=(micros,),
            in_specs=[
                pl.BlockSpec((1, tokens, feats), lambda m, w, d: (m, 0, 0)),
                pl.BlockSpec((1, tokens, feats), lambda m, w, d: (w[0] + m, 0, 0)),
                pl.BlockSpec((groups, 1, per_peer, tokens), lambda m, w, d: (0, m, 0, 0)),
                pl.BlockSpec((1, tokens, feats), lambda m, w, d: (w[0] + m, 0, 0)),
                pl.BlockSpec((1, tokens, feats), lambda m, w, d: (w[0] + m, 0, 0)),
                pl.BlockSpec((feats, feats), lambda m, w, d: (0, 0)),
                pl.BlockSpec((feats, feats), lambda m, w, d: (0, 0)),
            ],
            out_specs=[
                pl.BlockSpec((1, tokens, feats), lambda m, w, d: (m, 0, 0)),
                pl.BlockSpec((blocks, size, size), lambda m, w, d: (0, 0, 0)),
                pl.BlockSpec((blocks, size, size), lambda m, w, d: (0, 0, 0)),
            ],
        ),
        out_shape=[
            sds((micros, tokens, feats), bf16),
            sds((blocks, size, size), f32),
            sds((blocks, size, size), f32),
        ],
        compiler_params=params,
        name="grads",
    )(where, drop, x, da, z, gin, gout, pick_first, pick_second)
    return (grads[None], first[None, None], second[None, None])


def solution(mesh):
    placed = (
        P("pipe", None, None, "tensor"),
        P(None, None, "tensor"),
        P("pipe", None, "tensor", None, None),
        P("pipe", None, "tensor", None, None),
        P("pipe", None),
        P("pipe", None, None),
    )
    return jax.shard_map(
        on_device,
        mesh=mesh,
        in_specs=placed,
        out_specs=(
            P("pipe", None, None, "tensor"),
            P("pipe", None, "tensor", None, None),
            P("pipe", None, "tensor", None, None),
        ),
        check_vma=False,
    )
```

time: 979 us -> 644 us (0.66)
  the two profiles are of different devices: /device:TPU:1 before, /device:TPU:128 now
where the time goes in v1:
time: 644 us; the launch traced here: 640 us
  waiting for transfers between devices  286 us (44%)
  Pallas kernels  158 us (25%)
  starting transfers between devices  150 us (23%)
  blocking collectives  25.9 us (4%)
  local copies, waits for them, and re-layouts  16.1 us (3%)
    all_to_all x23, waiting for transfers between devices, advance(): returned = lax.all_to_all(outgoing, 'tensor', 0, 0, tiled=True)  213 us
    all_to_all x23, starting transfers between devices, advance(): returned = lax.all_to_all(outgoing, 'tensor', 0, 0, tiled=True)  84.5 us
    ppermute x23, waiting for transfers between devices, advance(): incoming = lax.ppermute(g, 'pipe', route)  72.8 us
    pallas_call x23, Pallas kernels, advance(): da, gout, g = receive(at, where, returned, slope, w1d, gin, da, gout)  69.1 us
    pallas_call x23, Pallas kernels, advance(): gin, outgoing = send(at, where, incoming, out_grad, w2d, gin)  68.4 us
    ppermute x23, starting transfers between devices, advance(): incoming = lax.ppermute(g, 'pipe', route)  65.6 us
    all_to_all x1, blocking collectives, on_device(): z = lax.all_to_all(hidden, 'tensor', 0, 0, tiled=True)  25.9 us
  transfers between devices with their start and end apart: 46, of which 46 were waited for; matrix products, arithmetic and copies ran while one was open for 0% of the time, Pallas kernels for 0%

profile of v1, /device:TPU:128, one launch (start us, length us, event | category | flops | bytes accessed | tf_op | source)
XLA Modules:
  0.0 639.8 jit_solution(825586948563787949)
XLA Ops:
  11.4 5.8 forward.1
  25.1 574.1 %while.19 = (s32[]{:T(128)}, bf16[128,768]{1,0:T(8,128)(2,1)S(1)}, bf16[23,128,768]{2,1,0:T(8,128)(2,1)}, bf16[23,128,768]{2,1,0:T(8,128)(2,1)}, bf16[23,128,768...) while((s32[]{:T(128)}, bf16[128,768]{1,0:T(8,128)(2,1)S(1)}, ...), condition=%wide.region_1.0_spmd, body=%wide.region_0.0_spmd.sunk | while | flops 2 | bytes 1376445 | solution.py:222
  33.3 7.0 %all-to-all-start = ((bf16[16,48,128]{2,1,0:T(8,128)(2,1)}), bf16[16,48,128]{2,1,0:T(8,128)(2,1)S(1)}, u32[]{:S(2)}, u32[]{:S(2)}) async-start(bf16[16,48,128]{2,1,0:T(8,128)(2,1)} %get-tuple-element.275), calls=%async_computation | async-start | bytes 393216 | tf_op jit(solution)/shard_map/while/body/eval_jaxpr/all_to_all | solution.py:215
  40.3 8.9 %all-to-all-done.returned_ref = bf16[16,48,128]{2,1,0:T(8,128)(2,1)S(1)} async-done(((bf16[16,48,128]{2,1,0:T(8,128)(2,1)}), bf16[16,48,128]{2,1,0:T(8,128)(2,1)S(1)}, u32[]{:S(2)}, u32[]{:S(2)}) %all-to-all-start) | async-done | bytes 196640 | tf_op jit(solution)/shard_map/while/body/eval_jaxpr/all_to_all | solution.py:215
  61.4 3.5 all-to-all-start
  64.9 9.2 %all-to-all-done.returned_ref = bf16[16,48,128]{2,1,0:T(8,128)(2,1)S(1)} async-done(((bf16[16,48,128]{2,1,0:T(8,128)(2,1)}), bf16[16,48,128]{2,1,0:T(8,128)(2,1)S(1)}, u32[]{:S(2)}, u32[]{:S(2)}) %all-to-all-start) | async-done | bytes 196640 | tf_op jit(solution)/shard_map/while/body/eval_jaxpr/all_to_all | solution.py:215
  89.8 9.3 %all-to-all-done.returned_ref = bf16[16,48,128]{2,1,0:T(8,128)(2,1)S(1)} async-done(((bf16[16,48,128]{2,1,0:T(8,128)(2,1)}), bf16[16,48,128]{2,1,0:T(8,128)(2,1)S(1)}, u32[]{:S(2)}, u32[]{:S(2)}) %all-to-all-start) | async-done | bytes 196640 | tf_op jit(solution)/shard_map/while/body/eval_jaxpr/all_to_all | solution.py:215
  111.1 3.5 all-to-all-start
  114.7 9.2 %all-to-all-done.returned_ref = bf16[16,48,128]{2,1,0:T(8,128)(2,1)S(1)} async-done(((bf16[16,48,128]{2,1,0:T(8,128)(2,1)}), bf16[16,48,128]{2,1,0:T(8,128)(2,1)S(1)}, u32[]{:S(2)}, u32[]{:S(2)}) %all-to-all-start) | async-done | bytes 196640 | tf_op jit(solution)/shard_map/while/body/eval_jaxpr/all_to_all | solution.py:215
  139.5 9.3 %all-to-all-done.returned_ref = bf16[16,48,128]{2,1,0:T(8,128)(2,1)S(1)} async-done(((bf16[16,48,128]{2,1,0:T(8,128)(2,1)}), bf16[16,48,128]{2,1,0:T(8,128)(2,1)S(1)}, u32[]{:S(2)}, u32[]{:S(2)}) %all-to-all-start) | async-done | bytes 196640 | tf_op jit(solution)/shard_map/while/body/eval_jaxpr/all_to_all | solution.py:215
  164.4 9.3 %all-to-all-done.returned_ref = bf16[16,48,128]{2,1,0:T(8,128)(2,1)S(1)} async-done(((bf16[16,48,128]{2,1,0:T(8,128)(2,1)}), bf16[16,48,128]{2,1,0:T(8,128)(2,1)S(1)}, u32[]{:S(2)}, u32[]{:S(2)}) %all-to-all-start) | async-done | bytes 196640 | tf_op jit(solution)/shard_map/while/body/eval_jaxpr/all_to_all | solution.py:215
  189.2 9.3 %all-to-all-done.returned_ref = bf16[16,48,128]{2,1,0:T(8,128)(2,1)S(1)} async-done(((bf16[16,48,128]{2,1,0:T(8,128)(2,1)}), bf16[16,48,128]{2,1,0:T(8,128)(2,1)S(1)}, u32[]{:S(2)}, u32[]{:S(2)}) %all-to-all-start) | async-done | bytes 196640 | tf_op jit(solution)/shard_map/while/body/eval_jaxpr/all_to_all | solution.py:215
  210.6 3.5 all-to-all-start
  214.1 9.3 %all-to-all-done.returned_ref = bf16[16,48,128]{2,1,0:T(8,128)(2,1)S(1)} async-done(((bf16[16,48,128]{2,1,0:T(8,128)(2,1)}), bf16[16,48,128]{2,1,0:T(8,128)(2,1)S(1)}, u32[]{:S(2)}, u32[]{:S(2)}) %all-to-all-start) | async-done | bytes 196640 | tf_op jit(solution)/shard_map/while/body/eval_jaxpr/all_to_all | solution.py:215
  235.4 3.5 all-to-all-start
  238.9 9.3 %all-to-all-done.returned_ref = bf16[16,48,128]{2,1,0:T(8,128)(2,1)S(1)} async-done(((bf16[16,48,128]{2,1,0:T(8,128)(2,1)}), bf16[16,48,128]{2,1,0:T(8,128)(2,1)S(1)}, u32[]{:S(2)}, u32[]{:S(2)}) %all-to-all-start) | async-done | bytes 196640 | tf_op jit(solution)/shard_map/while/body/eval_jaxpr/all_to_all | solution.py:215
  263.8 9.3 %all-to-all-done.returned_ref = bf16[16,48,128]{2,1,0:T(8,128)(2,1)S(1)} async-done(((bf16[16,48,128]{2,1,0:T(8,128)(2,1)}), bf16[16,48,128]{2,1,0:T(8,128)(2,1)S(1)}, u32[]{:S(2)}, u32[]{:S(2)}) %all-to-all-start) | async-done | bytes 196640 | tf_op jit(solution)/shard_map/while/body/eval_jaxpr/all_to_all | solution.py:215
  288.6 9.3 %all-to-all-done.returned_ref = bf16[16,48,128]{2,1,0:T(8,128)(2,1)S(1)} async-done(((bf16[16,48,128]{2,1,0:T(8,128)(2,1)}), bf16[16,48,128]{2,1,0:T(8,128)(2,1)S(1)}, u32[]{:S(2)}, u32[]{:S(2)}) %all-to-all-start) | async-done | bytes 196640 | tf_op jit(solution)/shard_map/while/body/eval_jaxpr/all_to_all | solution.py:215
  313.5 9.3 %all-to-all-done.returned_ref = bf16[16,48,128]{2,1,0:T(8,128)(2,1)S(1)} async-done(((bf16[16,48,128]{2,1,0:T(8,128)(2,1)}), bf16[16,48,128]{2,1,0:T(8,128)(2,1)S(1)}, u32[]{:S(2)}, u32[]{:S(2)}) %all-to-all-start) | async-done | bytes 196640 | tf_op jit(solution)/shard_map/while/body/eval_jaxpr/all_to_all | solution.py:215
  338.3 9.3 %all-to-all-done.returned_ref = bf16[16,48,128]{2,1,0:T(8,128)(2,1)S(1)} async-done(((bf16[16,48,128]{2,1,0:T(8,128)(2,1)}), bf16[16,48,128]{2,1,0:T(8,128)(2,1)S(1)}, u32[]{:S(2)}, u32[]{:S(2)}) %all-to-all-start) | async-done | bytes 196640 | tf_op jit(solution)/shard_map/while/body/eval_jaxpr/all_to_all | solution.py:215
  363.2 9.3 %all-to-all-done.returned_ref = bf16[16,48,128]{2,1,0:T(8,128)(2,1)S(1)} async-done(((bf16[16,48,128]{2,1,0:T(8,128)(2,1)}), bf16[16,48,128]{2,1,0:T(8,128)(2,1)S(1)}, u32[]{:S(2)}, u32[]{:S(2)}) %all-to-all-start) | async-done | bytes 196640 | tf_op jit(solution)/shard_map/while/body/eval_jaxpr/all_to_all | solution.py:215
  388.0 9.3 %all-to-all-done.returned_ref = bf16[16,48,128]{2,1,0:T(8,128)(2,1)S(1)} async-done(((bf16[16,48,128]{2,1,0:T(8,128)(2,1)}), bf16[16,48,128]{2,1,0:T(8,128)(2,1)S(1)}, u32[]{:S(2)}, u32[]{:S(2)}) %all-to-all-start) | async-done | bytes 196640 | tf_op jit(solution)/shard_map/while/body/eval_jaxpr/all_to_all | solution.py:215
  412.9 9.2 %all-to-all-done.returned_ref = bf16[16,48,128]{2,1,0:T(8,128)(2,1)S(1)} async-done(((bf16[16,48,128]{2,1,0:T(8,128)(2,1)}), bf16[16,48,128]{2,1,0:T(8,128)(2,1)S(1)}, u32[]{:S(2)}, u32[]{:S(2)}) %all-to-all-start) | async-done | bytes 196640 | tf_op jit(solution)/shard_map/while/body/eval_jaxpr/all_to_all | solution.py:215
  437.7 9.3 %all-to-all-done.returned_ref = bf16[16,48,128]{2,1,0:T(8,128)(2,1)S(1)} async-done(((bf16[16,48,128]{2,1,0:T(8,128)(2,1)}), bf16[16,48,128]{2,1,0:T(8,128)(2,1)S(1)}, u32[]{:S(2)}, u32[]{:S(2)}) %all-to-all-start) | async-done | bytes 196640 | tf_op jit(solution)/shard_map/while/body/eval_jaxpr/all_to_all | solution.py:215
  462.6 9.2 %all-to-all-done.returned_ref = bf16[16,48,128]{2,1,0:T(8,128)(2,1)S(1)} async-done(((bf16[16,48,128]{2,1,0:T(8,128)(2,1)}), bf16[16,48,128]{2,1,0:T(8,128)(2,1)S(1)}, u32[]{:S(2)}, u32[]{:S(2)}) %all-to-all-start) | async-done | bytes 196640 | tf_op jit(solution)/shard_map/while/body/eval_jaxpr/all_to_all | solution.py:215
  487.4 9.3 %all-to-all-done.returned_ref = bf16[16,48,128]{2,1,0:T(8,128)(2,1)S(1)} async-done(((bf16[16,48,128]{2,1,0:T(8,128)(2,1)}), bf16[16,48,128]{2,1,0:T(8,128)(2,1)S(1)}, u32[]{:S(2)}, u32[]{:S(2)}) %all-to-all-start) | async-done | bytes 196640 | tf_op jit(solution)/shard_map/while/body/eval_jaxpr/all_to_all | solution.py:215
  512.3 9.3 %all-to-all-done.returned_ref = bf16[16,48,128]{2,1,0:T(8,128)(2,1)S(1)} async-done(((bf16[16,48,128]{2,1,0:T(8,128)(2,1)}), bf16[16,48,128]{2,1,0:T(8,128)(2,1)S(1)}, u32[]{:S(2)}, u32[]{:S(2)}) %all-to-all-start) | async-done | bytes 196640 | tf_op jit(solution)/shard_map/while/body/eval_jaxpr/all_to_all | solution.py:215
  537.1 9.3 %all-to-all-done.returned_ref = bf16[16,48,128]{2,1,0:T(8,128)(2,1)S(1)} async-done(((bf16[16,48,128]{2,1,0:T(8,128)(2,1)}), bf16[16,48,128]{2,1,0:T(8,128)(2,1)S(1)}, u32[]{:S(2)}, u32[]{:S(2)}) %all-to-all-start) | async-done | bytes 196640 | tf_op jit(solution)/shard_map/while/body/eval_jaxpr/all_to_all | solution.py:215
  562.0 9.2 %all-to-all-done.returned_ref = bf16[16,48,128]{2,1,0:T(8,128)(2,1)S(1)} async-done(((bf16[16,48,128]{2,1,0:T(8,128)(2,1)}), bf16[16,48,128]{2,1,0:T(8,128)(2,1)S(1)}, u32[]{:S(2)}, u32[]{:S(2)}) %all-to-all-start) | async-done | bytes 196640 | tf_op jit(solution)/shard_map/while/body/eval_jaxpr/all_to_all | solution.py:215
  586.9 9.3 %all-to-all-done.returned_ref = bf16[16,48,128]{2,1,0:T(8,128)(2,1)S(1)} async-done(((bf16[16,48,128]{2,1,0:T(8,128)(2,1)}), bf16[16,48,128]{2,1,0:T(8,128)(2,1)S(1)}, u32[]{:S(2)}, u32[]{:S(2)}) %all-to-all-start) | async-done | bytes 196640 | tf_op jit(solution)/shard_map/while/body/eval_jaxpr/all_to_all | solution.py:215
  599.2 25.9 %all_to_all.11.z_ref = bf16[16,8,48,128]{3,2,1,0:T(8,128)(2,1)S(1)} all-to-all(bf16[16,8,48,128]{3,2,1,0:T(8,128)(2,1)S(1)} %get-tuple-element.181), channel_id=1, replica_groups=mesh['pipe'=16,'tensor'=16] {'tensor'}, dimensions={0} | all-to-all | bytes 3145728 | tf_op jit(solution)/shard_map/all_to_all | solution.py:156
  627.7 12.1 %grads.1 = (bf16[8,128,768]{2,1,0:T(8,128)(2,1)}, f32[6,128,128]{2,1,0:T(8,128)}, f32[6,128,128]{2,1,0:T(8,128)}) custom-call(s32[2]{0:T(128)S(1)} %get-tuple-element.316, s32[1]{0:T(128)} %bitcast.14.drop_ref, bf16[8,128,768]{2,1,0:T(8,128)(2,1)S(1)} %bitcast.16, bf16[23,128,768]{2,1,0:T(8,128)(2,1)} %get-tuple-element.180.da_ref, ...), custom_call_target="tpu_custom_call" | custom-call | tf_op jit(solution)/shard_map/grads/pallas_call | solution.py:226
  (137 shorter events, 359.9 us)
Async XLA Ops:
  33.3 15.9 %all-to-all-start = ((bf16[16,48,128]{2,1,0:T(8,128)(2,1)}), bf16[16,48,128]{2,1,0:T(8,128)(2,1)S(1)}, u32[]{:S(2)}, u32[]{:S(2)}) async-start(bf16[16,48,128]{2,1,0:T(8,128)(2,1)} %get-tuple-element.275), calls=%async_computation | async-start | bytes 393216 | tf_op jit(solution)/shard_map/while/body/eval_jaxpr/all_to_all | solution.py:215
  52.2 6.2 collective-permute-start
  61.4 12.8 %all-to-all-start = ((bf16[16,48,128]{2,1,0:T(8,128)(2,1)}), bf16[16,48,128]{2,1,0:T(8,128)(2,1)S(1)}, u32[]{:S(2)}, u32[]{:S(2)}) async-start(bf16[16,48,128]{2,1,0:T(8,128)(2,1)} %get-tuple-element.275), calls=%async_computation | async-start | bytes 393216 | tf_op jit(solution)/shard_map/while/body/eval_jaxpr/all_to_all | solution.py:215
  77.2 6.1 collective-permute-start
  86.3 12.9 %all-to-all-start = ((bf16[16,48,128]{2,1,0:T(8,128)(2,1)}), bf16[16,48,128]{2,1,0:T(8,128)(2,1)S(1)}, u32[]{:S(2)}, u32[]{:S(2)}) async-start(bf16[16,48,128]{2,1,0:T(8,128)(2,1)} %get-tuple-element.275), calls=%async_computation | async-start | bytes 393216 | tf_op jit(solution)/shard_map/while/body/eval_jaxpr/all_to_all | solution.py:215
  111.1 12.8 %all-to-all-start = ((bf16[16,48,128]{2,1,0:T(8,128)(2,1)}), bf16[16,48,128]{2,1,0:T(8,128)(2,1)S(1)}, u32[]{:S(2)}, u32[]{:S(2)}) async-start(bf16[16,48,128]{2,1,0:T(8,128)(2,1)} %get-tuple-element.275), calls=%async_computation | async-start | bytes 393216 | tf_op jit(solution)/shard_map/while/body/eval_jaxpr/all_to_all | solution.py:215
  126.9 6.1 collective-permute-start
  136.0 12.9 %all-to-all-start = ((bf16[16,48,128]{2,1,0:T(8,128)(2,1)}), bf16[16,48,128]{2,1,0:T(8,128)(2,1)S(1)}, u32[]{:S(2)}, u32[]{:S(2)}) async-start(bf16[16,48,128]{2,1,0:T(8,128)(2,1)} %get-tuple-element.275), calls=%async_computation | async-start | bytes 393216 | tf_op jit(solution)/shard_map/while/body/eval_jaxpr/all_to_all | solution.py:215
  160.8 12.8 %all-to-all-start = ((bf16[16,48,128]{2,1,0:T(8,128)(2,1)}), bf16[16,48,128]{2,1,0:T(8,128)(2,1)S(1)}, u32[]{:S(2)}, u32[]{:S(2)}) async-start(bf16[16,48,128]{2,1,0:T(8,128)(2,1)} %get-tuple-element.275), calls=%async_computation | async-start | bytes 393216 | tf_op jit(solution)/shard_map/while/body/eval_jaxpr/all_to_all | solution.py:215
  176.6 6.1 collective-permute-start
  185.7 12.8 %all-to-all-start = ((bf16[16,48,128]{2,1,0:T(8,128)(2,1)}), bf16[16,48,128]{2,1,0:T(8,128)(2,1)S(1)}, u32[]{:S(2)}, u32[]{:S(2)}) async-start(bf16[16,48,128]{2,1,0:T(8,128)(2,1)} %get-tuple-element.275), calls=%async_computation | async-start | bytes 393216 | tf_op jit(solution)/shard_map/while/body/eval_jaxpr/all_to_all | solution.py:215
  210.6 12.8 %all-to-all-start = ((bf16[16,48,128]{2,1,0:T(8,128)(2,1)}), bf16[16,48,128]{2,1,0:T(8,128)(2,1)S(1)}, u32[]{:S(2)}, u32[]{:S(2)}) async-start(bf16[16,48,128]{2,1,0:T(8,128)(2,1)} %get-tuple-element.275), calls=%async_computation | async-start | bytes 393216 | tf_op jit(solution)/shard_map/while/body/eval_jaxpr/all_to_all | solution.py:215
  235.4 12.8 %all-to-all-start = ((bf16[16,48,128]{2,1,0:T(8,128)(2,1)}), bf16[16,48,128]{2,1,0:T(8,128)(2,1)S(1)}, u32[]{:S(2)}, u32[]{:S(2)}) async-start(bf16[16,48,128]{2,1,0:T(8,128)(2,1)} %get-tuple-element.275), calls=%async_computation | async-start | bytes 393216 | tf_op jit(solution)/shard_map/while/body/eval_jaxpr/all_to_all | solution.py:215
  260.3 12.8 %all-to-all-start = ((bf16[16,48,128]{2,1,0:T(8,128)(2,1)}), bf16[16,48,128]{2,1,0:T(8,128)(2,1)S(1)}, u32[]{:S(2)}, u32[]{:S(2)}) async-start(bf16[16,48,128]{2,1,0:T(8,128)(2,1)} %get-tuple-element.275), calls=%async_computation | async-start | bytes 393216 | tf_op jit(solution)/shard_map/while/body/eval_jaxpr/all_to_all | solution.py:215
  285.1 12.8 %all-to-all-start = ((bf16[16,48,128]{2,1,0:T(8,128)(2,1)}), bf16[16,48,128]{2,1,0:T(8,128)(2,1)S(1)}, u32[]{:S(2)}, u32[]{:S(2)}) async-start(bf16[16,48,128]{2,1,0:T(8,128)(2,1)} %get-tuple-element.275), calls=%async_computation | async-start | bytes 393216 | tf_op jit(solution)/shard_map/while/body/eval_jaxpr/all_to_all | solution.py:215
  310.0 12.8 %all-to-all-start = ((bf16[16,48,128]{2,1,0:T(8,128)(2,1)}), bf16[16,48,128]{2,1,0:T(8,128)(2,1)S(1)}, u32[]{:S(2)}, u32[]{:S(2)}) async-start(bf16[16,48,128]{2,1,0:T(8,128)(2,1)} %get-tuple-element.275), calls=%async_computation | async-start | bytes 393216 | tf_op jit(solution)/shard_map/while/body/eval_jaxpr/all_to_all | solution.py:215
  334.8 12.8 %all-to-all-start = ((bf16[16,48,128]{2,1,0:T(8,128)(2,1)}), bf16[16,48,128]{2,1,0:T(8,128)(2,1)S(1)}, u32[]{:S(2)}, u32[]{:S(2)}) async-start(bf16[16,48,128]{2,1,0:T(8,128)(2,1)} %get-tuple-element.275), calls=%async_computation | async-start | bytes 393216 | tf_op jit(solution)/shard_map/while/body/eval_jaxpr/all_to_all | solution.py:215
  359.7 12.8 %all-to-all-start = ((bf16[16,48,128]{2,1,0:T(8,128)(2,1)}), bf16[16,48,128]{2,1,0:T(8,128)(2,1)S(1)}, u32[]{:S(2)}, u32[]{:S(2)}) async-start(bf16[16,48,128]{2,1,0:T(8,128)(2,1)} %get-tuple-element.275), calls=%async_computation | async-start | bytes 393216 | tf_op jit(solution)/shard_map/while/body/eval_jaxpr/all_to_all | solution.py:215
  375.4 6.1 collective-permute-start
  384.5 12.9 %all-to-all-start = ((bf16[16,48,128]{2,1,0:T(8,128)(2,1)}), bf16[16,48,128]{2,1,0:T(8,128)(2,1)S(1)}, u32[]{:S(2)}, u32[]{:S(2)}) async-start(bf16[16,48,128]{2,1,0:T(8,128)(2,1)} %get-tuple-element.275), calls=%async_computation | async-start | bytes 393216 | tf_op jit(solution)/shard_map/while/body/eval_jaxpr/all_to_all | solution.py:215
  409.4 12.8 %all-to-all-start = ((bf16[16,48,128]{2,1,0:T(8,128)(2,1)}), bf16[16,48,128]{2,1,0:T(8,128)(2,1)S(1)}, u32[]{:S(2)}, u32[]{:S(2)}) async-start(bf16[16,48,128]{2,1,0:T(8,128)(2,1)} %get-tuple-element.275), calls=%async_computation | async-start | bytes 393216 | tf_op jit(solution)/shard_map/while/body/eval_jaxpr/all_to_all | solution.py:215
  425.1 6.1 collective-permute-start
  434.2 12.9 %all-to-all-start = ((bf16[16,48,128]{2,1,0:T(8,128)(2,1)}), bf16[16,48,128]{2,1,0:T(8,128)(2,1)S(1)}, u32[]{:S(2)}, u32[]{:S(2)}) async-start(bf16[16,48,128]{2,1,0:T(8,128)(2,1)} %get-tuple-element.275), calls=%async_computation | async-start | bytes 393216 | tf_op jit(solution)/shard_map/while/body/eval_jaxpr/all_to_all | solution.py:215
  459.1 12.8 %all-to-all-start = ((bf16[16,48,128]{2,1,0:T(8,128)(2,1)}), bf16[16,48,128]{2,1,0:T(8,128)(2,1)S(1)}, u32[]{:S(2)}, u32[]{:S(2)}) async-start(bf16[16,48,128]{2,1,0:T(8,128)(2,1)} %get-tuple-element.275), calls=%async_computation | async-start | bytes 393216 | tf_op jit(solution)/shard_map/while/body/eval_jaxpr/all_to_all | solution.py:215
  474.8 6.1 collective-permute-start
  483.9 12.9 %all-to-all-start = ((bf16[16,48,128]{2,1,0:T(8,128)(2,1)}), bf16[16,48,128]{2,1,0:T(8,128)(2,1)S(1)}, u32[]{:S(2)}, u32[]{:S(2)}) async-start(bf16[16,48,128]{2,1,0:T(8,128)(2,1)} %get-tuple-element.275), calls=%async_computation | async-start | bytes 393216 | tf_op jit(solution)/shard_map/while/body/eval_jaxpr/all_to_all | solution.py:215
  508.7 12.8 %all-to-all-start = ((bf16[16,48,128]{2,1,0:T(8,128)(2,1)}), bf16[16,48,128]{2,1,0:T(8,128)(2,1)S(1)}, u32[]{:S(2)}, u32[]{:S(2)}) async-start(bf16[16,48,128]{2,1,0:T(8,128)(2,1)} %get-tuple-element.275), calls=%async_computation | async-start | bytes 393216 | tf_op jit(solution)/shard_map/while/body/eval_jaxpr/all_to_all | solution.py:215
  524.6 6.1 collective-permute-start
  533.6 12.8 %all-to-all-start = ((bf16[16,48,128]{2,1,0:T(8,128)(2,1)}), bf16[16,48,128]{2,1,0:T(8,128)(2,1)S(1)}, u32[]{:S(2)}, u32[]{:S(2)}) async-start(bf16[16,48,128]{2,1,0:T(8,128)(2,1)} %get-tuple-element.275), calls=%async_computation | async-start | bytes 393216 | tf_op jit(solution)/shard_map/while/body/eval_jaxpr/all_to_all | solution.py:215
  558.5 12.8 %all-to-all-start = ((bf16[16,48,128]{2,1,0:T(8,128)(2,1)}), bf16[16,48,128]{2,1,0:T(8,128)(2,1)S(1)}, u32[]{:S(2)}, u32[]{:S(2)}) async-start(bf16[16,48,128]{2,1,0:T(8,128)(2,1)} %get-tuple-element.275), calls=%async_computation | async-start | bytes 393216 | tf_op jit(solution)/shard_map/while/body/eval_jaxpr/all_to_all | solution.py:215
  574.3 6.1 collective-permute-start
  583.3 12.9 %all-to-all-start = ((bf16[16,48,128]{2,1,0:T(8,128)(2,1)}), bf16[16,48,128]{2,1,0:T(8,128)(2,1)S(1)}, u32[]{:S(2)}, u32[]{:S(2)}) async-start(bf16[16,48,128]{2,1,0:T(8,128)(2,1)} %get-tuple-element.275), calls=%async_computation | async-start | bytes 393216 | tf_op jit(solution)/shard_map/while/body/eval_jaxpr/all_to_all | solution.py:215
  (23 other events, 707.5 us)

commit v2 on v1

v2 whole, which is shorter than its diff:
```python
import jax
import jax.numpy as jnp
from jax import lax
from jax.experimental import pallas as pl
from jax.experimental.pallas import tpu as pltpu
from jax.sharding import PartitionSpec as P

MEMBERS = 2
CHUNKS = 2

gelu_scale = 0.7978845608028654
gelu_cubic = 0.044715
bf16 = jnp.bfloat16
f32 = jnp.float32
i32 = jnp.int32
sds = jax.ShapeDtypeStruct

NN = ((1,), (0,))
NT = ((1,), (1,))
LANES = 128


def dot(left, right, dims):
    return lax.dot_general(left, right, (dims, ((), ())), preferred_element_type=f32)


def whole(space=pltpu.VMEM):
    return pl.BlockSpec(memory_space=space)


def prep_kernel(group_ref, drop_ref, perm_ref, w1_ref, w2_ref, packed_ref, first_ref, second_ref):
    groups, feats = perm_ref.shape
    blocks, size, _ = w1_ref.shape
    per_peer = feats // groups
    own_group = group_ref[0]
    keep = drop_ref[0].astype(f32)
    base = own_group * feats
    rows = lax.broadcasted_iota(i32, (feats, feats), 0)
    cols = lax.broadcasted_iota(i32, (feats, feats), 1)
    before = jnp.where(rows < cols, 1.0, 0.0).astype(bf16)
    perm = perm_ref[...]
    mine = (perm >= base) & (perm < base + feats)
    rank = dot(jnp.where(mine, 1.0, 0.0).astype(bf16), before, NN)
    rank = jnp.where(mine, rank, -1.0).astype(i32)
    local = (perm - base).astype(f32)
    counter = lax.broadcasted_iota(i32, (per_peer, feats), 0)
    lane = lax.broadcasted_iota(i32, (per_peer, feats), 1)
    parts = []
    for peer in range(groups):
        hit = counter == rank[peer : peer + 1, :]
        source = jnp.sum(jnp.where(hit, local[peer : peer + 1, :], 0.0), axis=1, keepdims=True)
        parts.append(jnp.where(lane == source.astype(i32), 1.0, 0.0))
    leave = jnp.concatenate(parts, axis=0)
    own = perm_ref[pl.ds(own_group, 1), :]
    start = lax.broadcasted_iota(i32, (groups, feats), 0)
    from_group = (own >= start * feats) & (own < start * feats + feats)
    marks = jnp.where(from_group, 1.0, 0.0)
    place = dot(marks.astype(bf16), before, NN) + start.astype(f32) * per_peer
    slot = jnp.sum(marks * place, axis=0, keepdims=True).astype(i32)
    arrive = jnp.where(rows == slot, 1.0, 0.0)
    first_ref[...] = jnp.transpose(leave).astype(bf16)
    second_ref[...] = jnp.transpose(arrive).astype(bf16)
    leave = leave.astype(bf16)
    arrive = arrive.astype(bf16)
    part1 = jnp.zeros((feats, size), f32)
    part2 = jnp.zeros((feats, size), f32)
    for block in range(blocks):
        span = slice(block * size, (block + 1) * size)
        part1 += dot(leave[:, span], w1_ref[block], NT)
        part2 += dot(arrive[:, span], w2_ref[block], NN)
    owner = lax.broadcasted_iota(i32, (feats, LANES), 0) // size
    column = lax.broadcasted_iota(i32, (feats, LANES), 1)
    where1 = jnp.where(column == owner, 1.0, 0.0).astype(bf16)
    where2 = jnp.where(column == owner + 8, 1.0, 0.0).astype(bf16)
    packed_ref[:, 0:size] = part1.astype(bf16)
    packed_ref[:, size : 2 * size] = (keep * part2).astype(bf16)
    packed_ref[:, 2 * size :] = (dot(leave, where1, NN) + dot(arrive, where2, NN)).astype(bf16)


def forward_kernel(x_ref, packed_ref, hidden_ref, slope_ref, *dense_refs):
    groups, _, per_peer, tokens = hidden_ref.shape
    section = pl.program_id(0)
    members = len(dense_refs) // 2
    feats = packed_ref.shape[1]
    blocks = feats // LANES
    packed = packed_ref[0].astype(f32)
    w1 = packed[:, :LANES]
    w2 = packed[:, LANES : 2 * LANES]
    dense1 = jnp.concatenate([w1 * packed[:, 2 * LANES + b : 2 * LANES + b + 1] for b in range(blocks)], axis=1)
    dense2 = jnp.concatenate([w2 * packed[:, 2 * LANES + 8 + b : 2 * LANES + 9 + b] for b in range(blocks)], axis=1)
    dense1 = dense1.astype(bf16)
    dense2 = dense2.astype(bf16)
    for member in range(members):

        @pl.when(section == member)
        def _():
            dense_refs[member][...] = dense1
            dense_refs[members + member][...] = dense2

    v = dot(dense1, x_ref[0], NT)
    u = jnp.tanh(gelu_scale * (v + gelu_cubic * v * v * v))
    hidden_ref[...] = (0.5 * v * (1.0 + u)).astype(bf16).reshape(groups, 1, per_peer, tokens)
    slope_ref[0] = 0.5 * (1.0 + u) + 0.5 * v * (1.0 - u * u) * gelu_scale * (1.0 + 3.0 * gelu_cubic * v * v)


def mix(w2_ref, g, mixed_ref):
    mixed_ref[...] = dot(w2_ref[...], g, NT).astype(bf16).reshape(mixed_ref.shape)


def head_kernel(step_ref, where_ref, incoming_ref, out_grad_ref, w2_ref, old_ref, stored_ref, g_ref, mixed_ref):
    del old_ref
    g = jnp.where(where_ref[1] == 1, out_grad_ref[0], incoming_ref[...])
    stored_ref[0, 0] = g
    g_ref[...] = g
    mix(w2_ref, g, mixed_ref)


def back_kernel(has_next, *refs):
    step_ref, where_ref, returned_ref, g_in_ref, slope_ref, w1_ref = refs[:6]
    refs = refs[6:]
    if has_next:
        w2_ref, refs = refs[0], refs[1:]
    _, _, da_ref, stored_ref, g_ref = refs[:5]
    groups, per_peer, tokens = returned_ref.shape
    dh = returned_ref[...].reshape(groups * per_peer, tokens).astype(f32)
    da = dh * slope_ref[0]
    da_ref[0, 0] = da.astype(bf16)
    g = g_in_ref[...].astype(f32) + dot(jnp.transpose(da).astype(bf16), w1_ref[...], NN)
    g = g.astype(bf16)
    stored_ref[0, 0] = g
    g_ref[...] = g
    if has_next:
        mix(w2_ref, g, refs[5])


def partial_kernel(where_ref, da_ref, cot_ref, out_ref, x_ref, z_ref, mask_ref, first_ref, second_ref, grads_ref):
    feats = da_ref.shape[2]
    blocks = feats // LANES
    groups, _, per_peer, tokens = z_ref.shape
    grads_ref[0] = out_ref[0, 0]
    mask = mask_ref[0].astype(f32)
    one = dot(da_ref[0, 0], x_ref[0], NN)
    two = dot(z_ref[...].reshape(groups * per_peer, tokens), cot_ref[0, 0], NN)
    one = sum(one[:, b * LANES : (b + 1) * LANES] * mask[:, b : b + 1] for b in range(blocks))
    two = sum(two[:, b * LANES : (b + 1) * LANES] * mask[:, 8 + b : 9 + b] for b in range(blocks))

    @pl.when(pl.program_id(1) == 0)
    def _():
        first_ref[0] = one
        second_ref[0] = two

    @pl.when(pl.program_id(1) != 0)
    def _():
        first_ref[0] += one
        second_ref[0] += two


def unpick(pick, values):
    high = values.astype(bf16)
    rest = values - high.astype(f32)
    middle = rest.astype(bf16)
    low = (rest - middle.astype(f32)).astype(bf16)
    return dot(pick, high, NN) + dot(pick, middle, NN) + dot(pick, low, NN)


def final_kernel(drop_ref, one_ref, two_ref, pick1_ref, pick2_ref, first_ref, second_ref):
    blocks, size, _ = first_ref.shape
    keep = drop_ref[0].astype(f32)
    one = unpick(pick1_ref[...], jnp.sum(one_ref[...], axis=0))
    two = keep * unpick(pick2_ref[...], jnp.sum(two_ref[...], axis=0))
    for block in range(blocks):
        span = slice(block * size, (block + 1) * size)
        first_ref[block] = jnp.transpose(one[span, :])
        second_ref[block] = two[span, :]


def on_device(section_inputs, out_grad, w_first, w_second, drop_flags, perm):
    J, M = MEMBERS, CHUNKS
    rows = lax.axis_size("pipe")
    row = lax.axis_index("pipe").astype(i32)
    stages = rows // J
    stage, member = row // J, row % J
    groups = lax.axis_size("tensor")
    group = lax.axis_index("tensor").astype(i32)
    micros, micro_tokens, feats = section_inputs.shape[1:]
    total = micros * micro_tokens
    n = total // J
    c = n // M
    blocks, size = w_first.shape[2], w_first.shape[3]
    per_peer = feats // groups
    steps = M + stages - 1
    drop = drop_flags.reshape(1)
    params = pltpu.CompilerParams(vmem_limit_bytes=58 * 1024 * 1024)
    index_groups = [[s * J + j for j in range(J)] for s in range(stages)]

    def by_source(mine, other):
        return jnp.stack([jnp.where(member == 0, mine, other), jnp.where(member == 0, other, mine)])

    def partner(value):
        return lax.ppermute(value, "pipe", [(i, i ^ 1) for i in range(rows)])

    def exchange(value):
        if J == 2:
            mine = lax.dynamic_index_in_dim(value, member, 0, keepdims=False)
            other = lax.dynamic_index_in_dim(value, 1 - member, 0, keepdims=False)
            return by_source(mine, partner(other))
        return lax.all_to_all(value, "pipe", 0, 0, tiled=True, axis_index_groups=index_groups)

    def collect(value):
        if J == 2:
            return by_source(value, partner(value))
        return lax.all_gather(value, "pipe", axis_index_groups=index_groups)

    xs = exchange(section_inputs.reshape(J, n, feats))
    packed, pick1, pick2 = pl.pallas_call(
        prep_kernel,
        in_specs=[whole(pltpu.SMEM), whole(pltpu.SMEM), whole(), whole(), whole()],
        out_specs=[whole()] * 3,
        out_shape=[sds((feats, 3 * LANES), bf16)] + [sds((feats, feats), bf16)] * 2,
        compiler_params=params,
        name="prep",
    )(group.reshape(1), drop, perm.reshape(groups, feats), w_first[0, 0], w_second[0, 0])
    packed = collect(packed)

    outs = pl.pallas_call(
        forward_kernel,
        grid=(J,),
        in_specs=[
            pl.BlockSpec((1, n, feats), lambda j: (j, 0, 0)),
            pl.BlockSpec((1, feats, 3 * LANES), lambda j: (j, 0, 0)),
        ],
        out_specs=[
            pl.BlockSpec((groups, 1, per_peer, n), lambda j: (0, j, 0, 0)),
            pl.BlockSpec((1, feats, n), lambda j: (j, 0, 0)),
        ]
        + [pl.BlockSpec((feats, feats), lambda j: (0, 0))] * (2 * J),
        out_shape=[sds((groups, J, per_peer, n), bf16), sds((J, feats, n), f32)]
        + [sds((feats, feats), bf16)] * (2 * J),
        compiler_params=params,
        name="forward",
    )(xs, packed)
    hidden, slope = outs[:2]
    dense1, dense2 = outs[2 : 2 + J], outs[2 + J :]
    z = lax.all_to_all(hidden, "tensor", 0, 0, tiled=True)

    where = jnp.stack([stages - 1 - stage, (stage == stages - 1).astype(i32), member * M])
    chunks = out_grad.reshape(J * M, c, feats)

    def pick(k, w):
        return jnp.clip(k[0] - w[0], 0, M - 1)

    value_spec = pl.BlockSpec((c, feats), lambda i, k, w: (0, 0))
    mixed_spec = pl.BlockSpec((groups, per_peer, c), lambda i, k, w: (0, 0, 0))
    stored_shape = sds((steps, J + 1, c, feats), bf16)
    da_shape = sds((steps, J, feats, c), bf16)
    value_shape = sds((c, feats), bf16)
    mixed_shape = sds((groups, per_peer, c), bf16)

    def stored_spec(j):
        return pl.BlockSpec((1, 1, c, feats), lambda i, k, w: (k[0], j, 0, 0))

    head = pl.pallas_call(
        head_kernel,
        grid_spec=pltpu.PrefetchScalarGridSpec(
            num_scalar_prefetch=2,
            grid=(1,),
            in_specs=[
                value_spec,
                pl.BlockSpec((1, c, feats), lambda i, k, w: (w[2] + pick(k, w), 0, 0)),
                whole(),
                whole(pl.ANY),
            ],
            out_specs=[stored_spec(J), value_spec, mixed_spec],
        ),
        out_shape=[stored_shape, value_shape, mixed_shape],
        input_output_aliases={5: 0},
        compiler_params=params,
        name="head",
    )

    def back(j):
        has_next = j > 0
        extra = 1 if has_next else 0

        def body(*refs):
            back_kernel(has_next, *refs)

        return pl.pallas_call(
            body,
            grid_spec=pltpu.PrefetchScalarGridSpec(
                num_scalar_prefetch=2,
                grid=(1,),
                in_specs=[
                    mixed_spec,
                    value_spec,
                    pl.BlockSpec((1, feats, c), lambda i, k, w: (j, 0, pick(k, w))),
                    whole(),
                ]
                + [whole()] * extra
                + [whole(pl.ANY)] * 2,
                out_specs=[
                    pl.BlockSpec((1, 1, feats, c), lambda i, k, w: (k[0], j, 0, 0)),
                    stored_spec(j),
                    value_spec,
                ]
                + [mixed_spec] * extra,
            ),
            out_shape=[da_shape, stored_shape, value_shape] + [mixed_shape] * extra,
            input_output_aliases={6 + extra: 0, 7 + extra: 1},
            compiler_params=params,
            name="back",
        )

    backs = [back(j) for j in range(J)]
    route = [(i, i - J) for i in range(J, rows)]

    def advance(k, carry):
        g, stored, da = carry
        at = jnp.full((1,), k, i32)
        if stages > 1:
            g = lax.ppermute(g, "pipe", route)
        stored, g, mixed = head(at, where, g, chunks, dense2[J - 1], stored)
        for j in reversed(range(J)):
            returned = lax.all_to_all(mixed, "tensor", 0, 0, tiled=True)
            if j > 0:
                da, stored, g, mixed = backs[j](at, where, returned, g, slope, dense1[j], dense2[j - 1], da, stored)
            else:
                da, stored, g = backs[j](at, where, returned, g, slope, dense1[j], da, stored)
        return (g, stored, da)

    carry = (
        jnp.zeros((c, feats), bf16),
        jnp.zeros(stored_shape.shape, bf16),
        jnp.zeros(da_shape.shape, bf16),
    )
    _, stored, da = lax.fori_loop(0, steps, advance, carry)

    one, two, grads = pl.pallas_call(
        partial_kernel,
        grid_spec=pltpu.PrefetchScalarGridSpec(
            num_scalar_prefetch=1,
            grid=(J, M),
            in_specs=[
                pl.BlockSpec((1, 1, feats, c), lambda j, m, w: (w[0] + m, j, 0, 0)),
                pl.BlockSpec((1, 1, c, feats), lambda j, m, w: (w[0] + m, j + 1, 0, 0)),
                pl.BlockSpec((1, 1, c, feats), lambda j, m, w: (w[0] + m, j, 0, 0)),
                pl.BlockSpec((1, c, feats), lambda j, m, w: (j, m, 0)),
                pl.BlockSpec((groups, 1, per_peer, c), lambda j, m, w: (0, j, 0, m)),
                pl.BlockSpec((1, feats, LANES), lambda j, m, w: (j, 0, 2)),
            ],
            out_specs=[
                pl.BlockSpec((1, feats, LANES), lambda j, m, w: (j, 0, 0)),
                pl.BlockSpec((1, feats, LANES), lambda j, m, w: (j, 0, 0)),
                pl.BlockSpec((1, c, feats), lambda j, m, w: (j, m, 0)),
            ],
        ),
        out_shape=[sds((J, feats, LANES), f32), sds((J, feats, LANES), f32), sds((J, n, feats), bf16)],
        compiler_params=params,
        name="partial",
    )(where, da, stored, stored, xs, z, packed)

    grads = exchange(grads)
    one = exchange(one)
    two = exchange(two)
    first, second = pl.pallas_call(
        final_kernel,
        in_specs=[whole(pltpu.SMEM)] + [whole()] * 4,
        out_specs=[whole()] * 2,
        out_shape=[sds((blocks, size, size), f32)] * 2,
        compiler_params=params,
        name="final",
    )(drop, one, two, pick1, pick2)
    return (grads.reshape(section_inputs.shape), first[None, None], second[None, None])


def solution(mesh):
    placed = (
        P("pipe", None, None, "tensor"),
        P(None, None, "tensor"),
        P("pipe", None, "tensor", None, None),
        P("pipe", None, "tensor", None, None),
        P("pipe", None),
        P("pipe", None, None),
    )
    return jax.shard_map(
        on_device,
        mesh=mesh,
        in_specs=placed,
        out_specs=(
            P("pipe", None, None, "tensor"),
            P("pipe", None, "tensor", None, None),
            P("pipe", None, "tensor", None, None),
        ),
        check_vma=False,
    )
```

time: 644 us -> 531 us (0.82)
  the two profiles are of different devices: /device:TPU:128 before, /device:TPU:1 now
where the time goes in v2:
time: 531 us; the launch traced here: 525 us
  waiting for transfers between devices  158 us (30%)
  blocking collectives  133 us (25%)
  Pallas kernels  120 us (23%)
  starting transfers between devices  77.7 us (15%)
  local copies, waits for them, and re-layouts  28 us (5%)
  other arithmetic  7.08 us (1%)
    all_to_all x9, blocking collectives, advance(): returned = lax.all_to_all(mixed, 'tensor', 0, 0, tiled=True)  114 us
    ppermute x9, waiting for transfers between devices, advance(): g = lax.ppermute(g, 'pipe', route)  80.5 us
    all_to_all x9, waiting for transfers between devices, advance(): returned = lax.all_to_all(mixed, 'tensor', 0, 0, tiled=True)  75.4 us
    ppermute x5, starting transfers between devices, partner(): return lax.ppermute(value, 'pipe', [(i, i ^ 1) for i in range(rows)])  34.2 us
    all_to_all x9, starting transfers between devices, advance(): returned = lax.all_to_all(mixed, 'tensor', 0, 0, tiled=True)  32 us
    pallas_call x9, Pallas kernels, advance(): stored, g, mixed = head(at, where, g, chunks, dense2[J - 1], stored)  31.3 us
    pallas_call x9, Pallas kernels, advance(): backs[j](at, where, returned, g, slope, dense1[j], da, stored)  31.3 us
    pallas_call x9, Pallas kernels, advance(): backs[j]  30.3 us
  transfers between devices with their start and end apart: 23, of which 21 were waited for; matrix products, arithmetic and copies ran while one was open for 1% of the time, Pallas kernels for 1%

profile of v2, /device:TPU:1, one launch (start us, length us, event | category | flops | bytes accessed | tf_op | source)
XLA Modules:
  0.0 524.9 jit_solution(15648899836138613493)
XLA Ops:
  17.0 9.0 %forward.1 = (bf16[16,2,48,512]{3,2,1,0:T(8,128)(2,1)}, f32[2,768,512]{2,1,0:T(8,128)S(1)}, bf16[768,768]{1,0:T(8,128)(2,1)}, bf16[768,768]{1,0:T(8,128)(2,1)}, ...) custom-call(bf16[2,512,768]{2,1,0:T(8,128)(2,1)} %pad_maximum_fusion.x_ref, ...), custom_call_target="tpu_custom_call" | custom-call | tf_op jit(solution)/shard_map/forward/pallas_call | solution.py:225
  35.6 420.0 %while.17 = (s32[]{:T(128)}, bf16[256,768]{1,0:T(8,128)(2,1)}, bf16[9,3,256,768]{3,2,1,0:T(8,128)(2,1)}, bf16[9,2,768,256]{3,2,1,0:T(8,128)(2,1)}, s32[3]{0:T(12...) while((s32[]{:T(128)}, bf16[256,768]{1,0:T(8,128)(2,1)}, ...), condition=%wide.region_1.2_spmd, body=%wide.region_0.1_spmd.sunk | while | flops 2 | bytes 16122165 | solution.py:336
  36.9 11.1 %collective-permute-done.incoming_ref = bf16[256,768]{1,0:T(8,128)(2,1)S(1)} collective-permute-done((bf16[256,768]{1,0:T(8,128)(2,1)}, bf16[256,768]{1,0:T(8,128)(2,1)S(1)}, u32[]{:S(2)}, u32[]{:S(2)}) %collective-permute-start) | collective-permute-done | bytes 393248 | tf_op jit(solution)/shard_map/while/body/eval_jaxpr/ppermute | solution.py:321
  52.3 14.4 %all_to_all.18.refs_2_ = bf16[16,48,256]{2,1,0:T(8,128)(2,1)} all-to-all(bf16[16,48,256]{2,1,0:T(8,128)(2,1)} %get-tuple-element.325), channel_id=1, replica_groups=mesh['pipe'=16,'tensor'=16] {'tensor'}, dimensions={0} | all-to-all | bytes 786432 | tf_op jit(solution)/shard_map/while/body/eval_jaxpr/all_to_all | solution.py:324
  73.5 8.4 %all-to-all-done.1.refs_2_ = bf16[16,48,256]{2,1,0:T(8,128)(2,1)S(1)} async-done(((bf16[16,48,256]{2,1,0:T(8,128)(2,1)}), bf16[16,48,256]{2,1,0:T(8,128)(2,1)S(1)}, u32[]{:S(2)}, u32[]{:S(2)}) %all-to-all-start.1) | async-done | bytes 393248 | tf_op jit(solution)/shard_map/while/body/eval_jaxpr/all_to_all | solution.py:324
  87.4 8.7 %collective-permute-done.incoming_ref = bf16[256,768]{1,0:T(8,128)(2,1)S(1)} collective-permute-done((bf16[256,768]{1,0:T(8,128)(2,1)}, bf16[256,768]{1,0:T(8,128)(2,1)S(1)}, u32[]{:S(2)}, u32[]{:S(2)}) %collective-permute-start) | collective-permute-done | bytes 393248 | tf_op jit(solution)/shard_map/while/body/eval_jaxpr/ppermute | solution.py:321
  100.4 12.5 %all_to_all.18.refs_2_ = bf16[16,48,256]{2,1,0:T(8,128)(2,1)} all-to-all(bf16[16,48,256]{2,1,0:T(8,128)(2,1)} %get-tuple-element.325), channel_id=1, replica_groups=mesh['pipe'=16,'tensor'=16] {'tensor'}, dimensions={0} | all-to-all | bytes 786432 | tf_op jit(solution)/shard_map/while/body/eval_jaxpr/all_to_all | solution.py:324
  119.8 8.2 %all-to-all-done.1.refs_2_ = bf16[16,48,256]{2,1,0:T(8,128)(2,1)S(1)} async-done(((bf16[16,48,256]{2,1,0:T(8,128)(2,1)}), bf16[16,48,256]{2,1,0:T(8,128)(2,1)S(1)}, u32[]{:S(2)}, u32[]{:S(2)}) %all-to-all-start.1) | async-done | bytes 393248 | tf_op jit(solution)/shard_map/while/body/eval_jaxpr/all_to_all | solution.py:324
  133.5 7.6 %collective-permute-done.incoming_ref = bf16[256,768]{1,0:T(8,128)(2,1)S(1)} collective-permute-done((bf16[256,768]{1,0:T(8,128)(2,1)}, bf16[256,768]{1,0:T(8,128)(2,1)S(1)}, u32[]{:S(2)}, u32[]{:S(2)}) %collective-permute-start) | collective-permute-done | bytes 393248 | tf_op jit(solution)/shard_map/while/body/eval_jaxpr/ppermute | solution.py:321
  145.3 12.5 %all_to_all.18.refs_2_ = bf16[16,48,256]{2,1,0:T(8,128)(2,1)} all-to-all(bf16[16,48,256]{2,1,0:T(8,128)(2,1)} %get-tuple-element.325), channel_id=1, replica_groups=mesh['pipe'=16,'tensor'=16] {'tensor'}, dimensions={0} | all-to-all | bytes 786432 | tf_op jit(solution)/shard_map/while/body/eval_jaxpr/all_to_all | solution.py:324
  164.7 8.2 %all-to-all-done.1.refs_2_ = bf16[16,48,256]{2,1,0:T(8,128)(2,1)S(1)} async-done(((bf16[16,48,256]{2,1,0:T(8,128)(2,1)}), bf16[16,48,256]{2,1,0:T(8,128)(2,1)S(1)}, u32[]{:S(2)}, u32[]{:S(2)}) %all-to-all-start.1) | async-done | bytes 393248 | tf_op jit(solution)/shard_map/while/body/eval_jaxpr/all_to_all | solution.py:324
  178.4 9.0 %collective-permute-done.incoming_ref = bf16[256,768]{1,0:T(8,128)(2,1)S(1)} collective-permute-done((bf16[256,768]{1,0:T(8,128)(2,1)}, bf16[256,768]{1,0:T(8,128)(2,1)S(1)}, u32[]{:S(2)}, u32[]{:S(2)}) %collective-permute-start) | collective-permute-done | bytes 393248 | tf_op jit(solution)/shard_map/while/body/eval_jaxpr/ppermute | solution.py:321
  191.7 12.5 %all_to_all.18.refs_2_ = bf16[16,48,256]{2,1,0:T(8,128)(2,1)} all-to-all(bf16[16,48,256]{2,1,0:T(8,128)(2,1)} %get-tuple-element.325), channel_id=1, replica_groups=mesh['pipe'=16,'tensor'=16] {'tensor'}, dimensions={0} | all-to-all | bytes 786432 | tf_op jit(solution)/shard_map/while/body/eval_jaxpr/all_to_all | solution.py:324
  211.1 8.2 %all-to-all-done.1.refs_2_ = bf16[16,48,256]{2,1,0:T(8,128)(2,1)S(1)} async-done(((bf16[16,48,256]{2,1,0:T(8,128)(2,1)}), bf16[16,48,256]{2,1,0:T(8,128)(2,1)S(1)}, u32[]{:S(2)}, u32[]{:S(2)}) %all-to-all-start.1) | async-done | bytes 393248 | tf_op jit(solution)/shard_map/while/body/eval_jaxpr/all_to_all | solution.py:324
  224.8 8.3 %collective-permute-done.incoming_ref = bf16[256,768]{1,0:T(8,128)(2,1)S(1)} collective-permute-done((bf16[256,768]{1,0:T(8,128)(2,1)}, bf16[256,768]{1,0:T(8,128)(2,1)S(1)}, u32[]{:S(2)}, u32[]{:S(2)}) %collective-permute-start) | collective-permute-done | bytes 393248 | tf_op jit(solution)/shard_map/while/body/eval_jaxpr/ppermute | solution.py:321
  237.3 12.5 %all_to_all.18.refs_2_ = bf16[16,48,256]{2,1,0:T(8,128)(2,1)} all-to-all(bf16[16,48,256]{2,1,0:T(8,128)(2,1)} %get-tuple-element.325), channel_id=1, replica_groups=mesh['pipe'=16,'tensor'=16] {'tensor'}, dimensions={0} | all-to-all | bytes 786432 | tf_op jit(solution)/shard_map/while/body/eval_jaxpr/all_to_all | solution.py:324
  256.7 9.1 %all-to-all-done.1.refs_2_ = bf16[16,48,256]{2,1,0:T(8,128)(2,1)S(1)} async-done(((bf16[16,48,256]{2,1,0:T(8,128)(2,1)}), bf16[16,48,256]{2,1,0:T(8,128)(2,1)S(1)}, u32[]{:S(2)}, u32[]{:S(2)}) %all-to-all-start.1) | async-done | bytes 393248 | tf_op jit(solution)/shard_map/while/body/eval_jaxpr/all_to_all | solution.py:324
  271.2 9.3 %collective-permute-done.incoming_ref = bf16[256,768]{1,0:T(8,128)(2,1)S(1)} collective-permute-done((bf16[256,768]{1,0:T(8,128)(2,1)}, bf16[256,768]{1,0:T(8,128)(2,1)S(1)}, u32[]{:S(2)}, u32[]{:S(2)}) %collective-permute-start) | collective-permute-done | bytes 393248 | tf_op jit(solution)/shard_map/while/body/eval_jaxpr/ppermute | solution.py:321
  284.8 12.5 %all_to_all.18.refs_2_ = bf16[16,48,256]{2,1,0:T(8,128)(2,1)} all-to-all(bf16[16,48,256]{2,1,0:T(8,128)(2,1)} %get-tuple-element.325), channel_id=1, replica_groups=mesh['pipe'=16,'tensor'=16] {'tensor'}, dimensions={0} | all-to-all | bytes 786432 | tf_op jit(solution)/shard_map/while/body/eval_jaxpr/all_to_all | solution.py:324
  304.2 8.7 %all-to-all-done.1.refs_2_ = bf16[16,48,256]{2,1,0:T(8,128)(2,1)S(1)} async-done(((bf16[16,48,256]{2,1,0:T(8,128)(2,1)}), bf16[16,48,256]{2,1,0:T(8,128)(2,1)S(1)}, u32[]{:S(2)}, u32[]{:S(2)}) %all-to-all-start.1) | async-done | bytes 393248 | tf_op jit(solution)/shard_map/while/body/eval_jaxpr/all_to_all | solution.py:324
  318.4 8.8 %collective-permute-done.incoming_ref = bf16[256,768]{1,0:T(8,128)(2,1)S(1)} collective-permute-done((bf16[256,768]{1,0:T(8,128)(2,1)}, bf16[256,768]{1,0:T(8,128)(2,1)S(1)}, u32[]{:S(2)}, u32[]{:S(2)}) %collective-permute-start) | collective-permute-done | bytes 393248 | tf_op jit(solution)/shard_map/while/body/eval_jaxpr/ppermute | solution.py:321
  331.4 12.5 %all_to_all.18.refs_2_ = bf16[16,48,256]{2,1,0:T(8,128)(2,1)} all-to-all(bf16[16,48,256]{2,1,0:T(8,128)(2,1)} %get-tuple-element.325), channel_id=1, replica_groups=mesh['pipe'=16,'tensor'=16] {'tensor'}, dimensions={0} | all-to-all | bytes 786432 | tf_op jit(solution)/shard_map/while/body/eval_jaxpr/all_to_all | solution.py:324
  350.8 8.2 %all-to-all-done.1.refs_2_ = bf16[16,48,256]{2,1,0:T(8,128)(2,1)S(1)} async-done(((bf16[16,48,256]{2,1,0:T(8,128)(2,1)}), bf16[16,48,256]{2,1,0:T(8,128)(2,1)S(1)}, u32[]{:S(2)}, u32[]{:S(2)}) %all-to-all-start.1) | async-done | bytes 393248 | tf_op jit(solution)/shard_map/while/body/eval_jaxpr/all_to_all | solution.py:324
  364.5 9.2 %collective-permute-done.incoming_ref = bf16[256,768]{1,0:T(8,128)(2,1)S(1)} collective-permute-done((bf16[256,768]{1,0:T(8,128)(2,1)}, bf16[256,768]{1,0:T(8,128)(2,1)S(1)}, u32[]{:S(2)}, u32[]{:S(2)}) %collective-permute-start) | collective-permute-done | bytes 393248 | tf_op jit(solution)/shard_map/while/body/eval_jaxpr/ppermute | solution.py:321
  378.0 12.5 %all_to_all.18.refs_2_ = bf16[16,48,256]{2,1,0:T(8,128)(2,1)} all-to-all(bf16[16,48,256]{2,1,0:T(8,128)(2,1)} %get-tuple-element.325), channel_id=1, replica_groups=mesh['pipe'=16,'tensor'=16] {'tensor'}, dimensions={0} | all-to-all | bytes 786432 | tf_op jit(solution)/shard_map/while/body/eval_jaxpr/all_to_all | solution.py:324
  397.4 8.2 %all-to-all-done.1.refs_2_ = bf16[16,48,256]{2,1,0:T(8,128)(2,1)S(1)} async-done(((bf16[16,48,256]{2,1,0:T(8,128)(2,1)}), bf16[16,48,256]{2,1,0:T(8,128)(2,1)S(1)}, u32[]{:S(2)}, u32[]{:S(2)}) %all-to-all-start.1) | async-done | bytes 393248 | tf_op jit(solution)/shard_map/while/body/eval_jaxpr/all_to_all | solution.py:324
  411.1 8.5 %collective-permute-done.incoming_ref = bf16[256,768]{1,0:T(8,128)(2,1)S(1)} collective-permute-done((bf16[256,768]{1,0:T(8,128)(2,1)}, bf16[256,768]{1,0:T(8,128)(2,1)S(1)}, u32[]{:S(2)}, u32[]{:S(2)}) %collective-permute-start) | collective-permute-done | bytes 393248 | tf_op jit(solution)/shard_map/while/body/eval_jaxpr/ppermute | solution.py:321
  423.9 12.5 %all_to_all.18.refs_2_ = bf16[16,48,256]{2,1,0:T(8,128)(2,1)} all-to-all(bf16[16,48,256]{2,1,0:T(8,128)(2,1)} %get-tuple-element.325), channel_id=1, replica_groups=mesh['pipe'=16,'tensor'=16] {'tensor'}, dimensions={0} | all-to-all | bytes 786432 | tf_op jit(solution)/shard_map/while/body/eval_jaxpr/all_to_all | solution.py:324
  443.2 8.2 %all-to-all-done.1.refs_2_ = bf16[16,48,256]{2,1,0:T(8,128)(2,1)S(1)} async-done(((bf16[16,48,256]{2,1,0:T(8,128)(2,1)}), bf16[16,48,256]{2,1,0:T(8,128)(2,1)S(1)}, u32[]{:S(2)}, u32[]{:S(2)}) %all-to-all-start.1) | async-done | bytes 393248 | tf_op jit(solution)/shard_map/while/body/eval_jaxpr/all_to_all | solution.py:324
  455.7 19.1 %all_to_all.17.z_ref = bf16[16,2,48,512]{3,2,1,0:T(8,128)(2,1)} all-to-all(bf16[16,2,48,512]{3,2,1,0:T(8,128)(2,1)} %get-tuple-element.206), channel_id=1, replica_groups=mesh['pipe'=16,'tensor'=16] {'tensor'}, dimensions={0} | all-to-all | bytes 3145728 | tf_op jit(solution)/shard_map/all_to_all | solution.py:244
  474.8 8.1 %partial.1 = (f32[2,768,128]{2,1,0:T(8,128)}, f32[2,768,128]{2,1,0:T(8,128)}, bf16[2,512,768]{2,1,0:T(8,128)(2,1)}) custom-call(s32[3]{0:T(128)S(1)} %get-tuple-element.386, bf16[9,2,768,256]{3,2,1,0:T(8,128)(2,1)} %get-tuple-element.204.da_ref, bf16[9,3,256,768]{3,2,1,0:T(8,128)(2,1)} %get-tuple-element.205.cot_ref.out_ref, ...), custom_call_target="tpu_custom_call" | custom-call | tf_op jit(solution)/shard_map/partial/pallas_call | solution.py:338
  484.1 30.2 %collective-permute-start.5 = (f32[768,128]{1,0:T(8,128)S(1)}, f32[768,128]{1,0:T(8,128)S(1)}, u32[]{:S(2)}, u32[]{:S(2)}) collective-permute-start(f32[768,128]{1,0:T(8,128)S(1)} %dynamic-slice_bitcast_fusion.2), channel_id=1, source_target_pairs={{0,16},{16,0},{32,48},{48,32},{64,80},{80,64},{96,112},{112,96},{1... | collective-permute-start | bytes 1179656 | tf_op jit(solution)/shard_map/ppermute | solution.py:200
  (158 shorter events, 186.9 us)
Async XLA Ops:
  8.6 5.0 collective-permute-start.2
  13.0 2.4 collective-permute-start.1
  35.6 12.4 %collective-permute-start = (bf16[256,768]{1,0:T(8,128)(2,1)}, bf16[256,768]{1,0:T(8,128)(2,1)S(1)}, u32[]{:S(2)}, u32[]{:S(2)}) collective-permute-start(bf16[256,768]{1,0:T(8,128)(2,1)} %get-tuple-element.348), channel_id=1, source_target_pairs={{32,0},{48,16},{64,32},{80,48},{96,64},{112,80},{128,96},{144,112}... | collective-permute-start | bytes 1179656 | tf_op jit(solution)/shard_map/while/body/eval_jaxpr/ppermute | solution.py:321
  48.8 17.9 %copy-start.1 = (bf16[768,768]{1,0:T(8,128)(2,1)S(1)}, bf16[768,768]{1,0:T(8,128)(2,1)}, u32[]{:S(2)}) copy-start(bf16[768,768]{1,0:T(8,128)(2,1)} %get-tuple-element.367.refs_5_) | copy-start | bytes 3538948 | tf_op jit(solution)/shard_map/while
  48.8 17.9 %copy-start.2 = (bf16[768,768]{1,0:T(8,128)(2,1)S(1)}, bf16[768,768]{1,0:T(8,128)(2,1)}, u32[]{:S(2)}) copy-start(bf16[768,768]{1,0:T(8,128)(2,1)} %get-tuple-element.368.refs_6_) | copy-start | bytes 3538948 | tf_op jit(solution)/shard_map/while
  70.0 11.9 %all-to-all-start.1 = ((bf16[16,48,256]{2,1,0:T(8,128)(2,1)}), bf16[16,48,256]{2,1,0:T(8,128)(2,1)S(1)}, u32[]{:S(2)}, u32[]{:S(2)}) async-start(bf16[16,48,256]{2,1,0:T(8,128)(2,1)} %get-tuple-element.328), calls=%async_computation.1 | async-start | bytes 786432 | tf_op jit(solution)/shard_map/while/body/eval_jaxpr/all_to_all | solution.py:324
  86.2 10.0 %collective-permute-start = (bf16[256,768]{1,0:T(8,128)(2,1)}, bf16[256,768]{1,0:T(8,128)(2,1)S(1)}, u32[]{:S(2)}, u32[]{:S(2)}) collective-permute-start(bf16[256,768]{1,0:T(8,128)(2,1)} %get-tuple-element.348), channel_id=1, source_target_pairs={{32,0},{48,16},{64,32},{80,48},{96,64},{112,80},{128,96},{144,112}... | collective-permute-start | bytes 1179656 | tf_op jit(solution)/shard_map/while/body/eval_jaxpr/ppermute | solution.py:321
  96.9 16.0 %copy-start.1 = (bf16[768,768]{1,0:T(8,128)(2,1)S(1)}, bf16[768,768]{1,0:T(8,128)(2,1)}, u32[]{:S(2)}) copy-start(bf16[768,768]{1,0:T(8,128)(2,1)} %get-tuple-element.367.refs_5_) | copy-start | bytes 3538948 | tf_op jit(solution)/shard_map/while
  96.9 16.0 %copy-start.2 = (bf16[768,768]{1,0:T(8,128)(2,1)S(1)}, bf16[768,768]{1,0:T(8,128)(2,1)}, u32[]{:S(2)}) copy-start(bf16[768,768]{1,0:T(8,128)(2,1)} %get-tuple-element.368.refs_6_) | copy-start | bytes 3538948 | tf_op jit(solution)/shard_map/while
  116.2 11.8 %all-to-all-start.1 = ((bf16[16,48,256]{2,1,0:T(8,128)(2,1)}), bf16[16,48,256]{2,1,0:T(8,128)(2,1)S(1)}, u32[]{:S(2)}, u32[]{:S(2)}) async-start(bf16[16,48,256]{2,1,0:T(8,128)(2,1)} %get-tuple-element.328), calls=%async_computation.1 | async-start | bytes 786432 | tf_op jit(solution)/shard_map/while/body/eval_jaxpr/all_to_all | solution.py:324
  132.2 8.8 %collective-permute-start = (bf16[256,768]{1,0:T(8,128)(2,1)}, bf16[256,768]{1,0:T(8,128)(2,1)S(1)}, u32[]{:S(2)}, u32[]{:S(2)}) collective-permute-start(bf16[256,768]{1,0:T(8,128)(2,1)} %get-tuple-element.348), channel_id=1, source_target_pairs={{32,0},{48,16},{64,32},{80,48},{96,64},{112,80},{128,96},{144,112}... | collective-permute-start | bytes 1179656 | tf_op jit(solution)/shard_map/while/body/eval_jaxpr/ppermute | solution.py:321
  161.1 11.8 %all-to-all-start.1 = ((bf16[16,48,256]{2,1,0:T(8,128)(2,1)}), bf16[16,48,256]{2,1,0:T(8,128)(2,1)S(1)}, u32[]{:S(2)}, u32[]{:S(2)}) async-start(bf16[16,48,256]{2,1,0:T(8,128)(2,1)} %get-tuple-element.328), calls=%async_computation.1 | async-start | bytes 786432 | tf_op jit(solution)/shard_map/while/body/eval_jaxpr/all_to_all | solution.py:324
  177.1 10.3 %collective-permute-start = (bf16[256,768]{1,0:T(8,128)(2,1)}, bf16[256,768]{1,0:T(8,128)(2,1)S(1)}, u32[]{:S(2)}, u32[]{:S(2)}) collective-permute-start(bf16[256,768]{1,0:T(8,128)(2,1)} %get-tuple-element.348), channel_id=1, source_target_pairs={{32,0},{48,16},{64,32},{80,48},{96,64},{112,80},{128,96},{144,112}... | collective-permute-start | bytes 1179656 | tf_op jit(solution)/shard_map/while/body/eval_jaxpr/ppermute | solution.py:321
  188.2 15.9 %copy-start.2 = (bf16[768,768]{1,0:T(8,128)(2,1)S(1)}, bf16[768,768]{1,0:T(8,128)(2,1)}, u32[]{:S(2)}) copy-start(bf16[768,768]{1,0:T(8,128)(2,1)} %get-tuple-element.368.refs_6_) | copy-start | bytes 3538948 | tf_op jit(solution)/shard_map/while
  207.5 11.8 %all-to-all-start.1 = ((bf16[16,48,256]{2,1,0:T(8,128)(2,1)}), bf16[16,48,256]{2,1,0:T(8,128)(2,1)S(1)}, u32[]{:S(2)}, u32[]{:S(2)}) async-start(bf16[16,48,256]{2,1,0:T(8,128)(2,1)} %get-tuple-element.328), calls=%async_computation.1 | async-start | bytes 786432 | tf_op jit(solution)/shard_map/while/body/eval_jaxpr/all_to_all | solution.py:324
  223.5 9.5 %collective-permute-start = (bf16[256,768]{1,0:T(8,128)(2,1)}, bf16[256,768]{1,0:T(8,128)(2,1)S(1)}, u32[]{:S(2)}, u32[]{:S(2)}) collective-permute-start(bf16[256,768]{1,0:T(8,128)(2,1)} %get-tuple-element.348), channel_id=1, source_target_pairs={{32,0},{48,16},{64,32},{80,48},{96,64},{112,80},{128,96},{144,112}... | collective-permute-start | bytes 1179656 | tf_op jit(solution)/shard_map/while/body/eval_jaxpr/ppermute | solution.py:321
  233.8 15.9 %copy-start.2 = (bf16[768,768]{1,0:T(8,128)(2,1)S(1)}, bf16[768,768]{1,0:T(8,128)(2,1)}, u32[]{:S(2)}) copy-start(bf16[768,768]{1,0:T(8,128)(2,1)} %get-tuple-element.368.refs_6_) | copy-start | bytes 3538948 | tf_op jit(solution)/shard_map/while
  253.1 12.6 %all-to-all-start.1 = ((bf16[16,48,256]{2,1,0:T(8,128)(2,1)}), bf16[16,48,256]{2,1,0:T(8,128)(2,1)S(1)}, u32[]{:S(2)}, u32[]{:S(2)}) async-start(bf16[16,48,256]{2,1,0:T(8,128)(2,1)} %get-tuple-element.328), calls=%async_computation.1 | async-start | bytes 786432 | tf_op jit(solution)/shard_map/while/body/eval_jaxpr/all_to_all | solution.py:324
  270.0 10.6 %collective-permute-start = (bf16[256,768]{1,0:T(8,128)(2,1)}, bf16[256,768]{1,0:T(8,128)(2,1)S(1)}, u32[]{:S(2)}, u32[]{:S(2)}) collective-permute-start(bf16[256,768]{1,0:T(8,128)(2,1)} %get-tuple-element.348), channel_id=1, source_target_pairs={{32,0},{48,16},{64,32},{80,48},{96,64},{112,80},{128,96},{144,112}... | collective-permute-start | bytes 1179656 | tf_op jit(solution)/shard_map/while/body/eval_jaxpr/ppermute | solution.py:321
  300.6 12.3 %all-to-all-start.1 = ((bf16[16,48,256]{2,1,0:T(8,128)(2,1)}), bf16[16,48,256]{2,1,0:T(8,128)(2,1)S(1)}, u32[]{:S(2)}, u32[]{:S(2)}) async-start(bf16[16,48,256]{2,1,0:T(8,128)(2,1)} %get-tuple-element.328), calls=%async_computation.1 | async-start | bytes 786432 | tf_op jit(solution)/shard_map/while/body/eval_jaxpr/all_to_all | solution.py:324
  317.1 10.1 %collective-permute-start = (bf16[256,768]{1,0:T(8,128)(2,1)}, bf16[256,768]{1,0:T(8,128)(2,1)S(1)}, u32[]{:S(2)}, u32[]{:S(2)}) collective-permute-start(bf16[256,768]{1,0:T(8,128)(2,1)} %get-tuple-element.348), channel_id=1, source_target_pairs={{32,0},{48,16},{64,32},{80,48},{96,64},{112,80},{128,96},{144,112}... | collective-permute-start | bytes 1179656 | tf_op jit(solution)/shard_map/while/body/eval_jaxpr/ppermute | solution.py:321
  347.3 11.8 %all-to-all-start.1 = ((bf16[16,48,256]{2,1,0:T(8,128)(2,1)}), bf16[16,48,256]{2,1,0:T(8,128)(2,1)S(1)}, u32[]{:S(2)}, u32[]{:S(2)}) async-start(bf16[16,48,256]{2,1,0:T(8,128)(2,1)} %get-tuple-element.328), calls=%async_computation.1 | async-start | bytes 786432 | tf_op jit(solution)/shard_map/while/body/eval_jaxpr/all_to_all | solution.py:324
  363.2 10.5 %collective-permute-start = (bf16[256,768]{1,0:T(8,128)(2,1)}, bf16[256,768]{1,0:T(8,128)(2,1)S(1)}, u32[]{:S(2)}, u32[]{:S(2)}) collective-permute-start(bf16[256,768]{1,0:T(8,128)(2,1)} %get-tuple-element.348), channel_id=1, source_target_pairs={{32,0},{48,16},{64,32},{80,48},{96,64},{112,80},{128,96},{144,112}... | collective-permute-start | bytes 1179656 | tf_op jit(solution)/shard_map/while/body/eval_jaxpr/ppermute | solution.py:321
  374.5 15.9 %copy-start.2 = (bf16[768,768]{1,0:T(8,128)(2,1)S(1)}, bf16[768,768]{1,0:T(8,128)(2,1)}, u32[]{:S(2)}) copy-start(bf16[768,768]{1,0:T(8,128)(2,1)} %get-tuple-element.368.refs_6_) | copy-start | bytes 3538948 | tf_op jit(solution)/shard_map/while
  393.8 11.8 %all-to-all-start.1 = ((bf16[16,48,256]{2,1,0:T(8,128)(2,1)}), bf16[16,48,256]{2,1,0:T(8,128)(2,1)S(1)}, u32[]{:S(2)}, u32[]{:S(2)}) async-start(bf16[16,48,256]{2,1,0:T(8,128)(2,1)} %get-tuple-element.328), calls=%async_computation.1 | async-start | bytes 786432 | tf_op jit(solution)/shard_map/while/body/eval_jaxpr/all_to_all | solution.py:324
  409.8 9.8 %collective-permute-start = (bf16[256,768]{1,0:T(8,128)(2,1)}, bf16[256,768]{1,0:T(8,128)(2,1)S(1)}, u32[]{:S(2)}, u32[]{:S(2)}) collective-permute-start(bf16[256,768]{1,0:T(8,128)(2,1)} %get-tuple-element.348), channel_id=1, source_target_pairs={{32,0},{48,16},{64,32},{80,48},{96,64},{112,80},{128,96},{144,112}... | collective-permute-start | bytes 1179656 | tf_op jit(solution)/shard_map/while/body/eval_jaxpr/ppermute | solution.py:321
  439.7 11.8 %all-to-all-start.1 = ((bf16[16,48,256]{2,1,0:T(8,128)(2,1)}), bf16[16,48,256]{2,1,0:T(8,128)(2,1)S(1)}, u32[]{:S(2)}, u32[]{:S(2)}) async-start(bf16[16,48,256]{2,1,0:T(8,128)(2,1)} %get-tuple-element.328), calls=%async_computation.1 | async-start | bytes 786432 | tf_op jit(solution)/shard_map/while/body/eval_jaxpr/all_to_all | solution.py:324
  482.9 32.5 %copy-start.5 = (bf16[2,512,768]{2,1,0:T(8,128)(2,1)S(1)}, bf16[2,512,768]{2,1,0:T(8,128)(2,1)}, u32[]{:S(2)}) copy-start(bf16[2,512,768]{2,1,0:T(8,128)(2,1)} %get-tuple-element.207) | copy-start | bytes 4718596
  482.9 33.2 %copy-start.7 = (f32[2,768,128]{2,1,0:T(8,128)S(1)}, f32[2,768,128]{2,1,0:T(8,128)}, u32[]{:S(2)}) copy-start(f32[2,768,128]{2,1,0:T(8,128)} %get-tuple-element.209) | copy-start | bytes 2359300
  484.1 32.0 %collective-permute-start.5 = (f32[768,128]{1,0:T(8,128)S(1)}, f32[768,128]{1,0:T(8,128)S(1)}, u32[]{:S(2)}, u32[]{:S(2)}) collective-permute-start(f32[768,128]{1,0:T(8,128)S(1)} %dynamic-slice_bitcast_fusion.2), channel_id=1, source_target_pairs={{0,16},{16,0},{32,48},{48,32},{64,80},{80,64},{96,112},{112,96},{1... | collective-permute-start | bytes 1179656 | tf_op jit(solution)/shard_map/ppermute | solution.py:200
  515.3 1.8 collective-permute-start.4
  515.5 8.0 %collective-permute-start.3 = (bf16[512,768]{1,0:T(8,128)(2,1)S(1)}, bf16[512,768]{1,0:T(8,128)(2,1)S(1)}, u32[]{:S(2)}, u32[]{:S(2)}) collective-permute-start(bf16[512,768]{1,0:T(8,128)(2,1)S(1)} %dynamic-slice_bitcast_fusion), channel_id=1, source_target_pairs={{0,16},{16,0},{32,48},{48,32},{64,80},{80,64},{96,112},{112,96},{1... | collective-permute-start | bytes 2359304 | tf_op jit(solution)/shard_map/ppermute | solution.py:200
  (32 other events, 197.5 us)

commit v3 on v1

v3 whole, which is shorter than its diff:
```python
import jax
import jax.numpy as jnp
from jax import lax
from jax.experimental import pallas as pl
from jax.experimental.pallas import tpu as pltpu
from jax.sharding import PartitionSpec as P

gelu_scale = 0.7978845608028654
gelu_cubic = 0.044715
bf16 = jnp.bfloat16
f32 = jnp.float32
i32 = jnp.int32
sds = jax.ShapeDtypeStruct

NN = ((1,), (0,))
NT = ((1,), (1,))
LANES = 128
IDS = 64


def dot(left, right, dims):
    return lax.dot_general(left, right, (dims, ((), ())), preferred_element_type=f32)


def whole(space=pltpu.VMEM):
    return pl.BlockSpec(memory_space=space)


def gelu_pair(v):
    u = jnp.tanh(gelu_scale * (v + gelu_cubic * v * v * v))
    value = 0.5 * v * (1.0 + u)
    slope = 0.5 * (1.0 + u) + 0.5 * v * (1.0 - u * u) * gelu_scale * (1.0 + 3.0 * gelu_cubic * v * v)
    return value, slope


def prep_kernel(group_ref, drop_ref, perm_ref, w1_ref, w2_ref, packed_ref, w1d_ref, w2d_ref, pick1_ref, pick2_ref):
    groups, feats = perm_ref.shape
    blocks, size, _ = w1_ref.shape
    per_peer = feats // groups
    half = per_peer // 2
    own_group = group_ref[0]
    keep = drop_ref[0].astype(f32)
    base = own_group * feats
    rows = lax.broadcasted_iota(i32, (feats, feats), 0)
    cols = lax.broadcasted_iota(i32, (feats, feats), 1)
    before = jnp.where(rows < cols, 1.0, 0.0).astype(bf16)
    perm = perm_ref[...]
    mine = (perm >= base) & (perm < base + feats)
    rank = dot(jnp.where(mine, 1.0, 0.0).astype(bf16), before, NN)
    rank = jnp.where(mine, rank, -1.0).astype(i32)
    local = (perm - base).astype(f32)
    counter = lax.broadcasted_iota(i32, (half, feats), 0)
    lane = lax.broadcasted_iota(i32, (half, feats), 1)
    parts = []
    for part in range(2):
        for peer in range(groups):
            hit = counter + part * half == rank[peer : peer + 1, :]
            source = jnp.sum(jnp.where(hit, local[peer : peer + 1, :], 0.0), axis=1, keepdims=True)
            parts.append(jnp.where(lane == source.astype(i32), 1.0, 0.0))
    leave = jnp.concatenate(parts, axis=0).astype(bf16)
    own = perm_ref[pl.ds(own_group, 1), :]
    start = lax.broadcasted_iota(i32, (groups, feats), 0)
    from_group = (own >= start * feats) & (own < start * feats + feats)
    marks = jnp.where(from_group, 1.0, 0.0)
    place = dot(marks.astype(bf16), before, NN)
    place = place + jnp.where(place >= half, groups * half - half, 0.0) + start.astype(f32) * half
    slot = jnp.sum(marks * place, axis=0, keepdims=True).astype(i32)
    arrive = jnp.where(rows == slot, 1.0, 0.0)
    pick1_ref[...] = leave
    pick2_ref[...] = jnp.transpose(arrive).astype(bf16)
    arrive = arrive.astype(bf16)
    part1 = jnp.zeros((feats, size), f32)
    part2 = jnp.zeros((feats, size), f32)
    for block in range(blocks):
        span = slice(block * size, (block + 1) * size)
        one = dot(leave[:, span], w1_ref[block], NT)
        two = keep * dot(arrive[:, span], w2_ref[block], NN)
        w1d_ref[:, span] = one.astype(bf16)
        w2d_ref[:, span] = two.astype(bf16)
        part1 += one
        part2 += two
    packed_ref[0:feats, :] = part1.astype(bf16)
    packed_ref[feats : 2 * feats, :] = part2.astype(bf16)
    line = lax.broadcasted_iota(i32, (8, feats), 0)
    owner = (lax.broadcasted_iota(i32, (8, feats), 1) // size).astype(f32)
    ids = dot(jnp.where(line == 0, owner, 0.0).astype(bf16), leave, NT)
    ids += dot(jnp.where(line == 1, owner, 0.0).astype(bf16), arrive, NT)
    pieces = [ids[:, b * LANES : (b + 1) * LANES] for b in range(feats // LANES)]
    pieces.append(jnp.zeros((IDS - 8 * len(pieces), LANES), f32))
    packed_ref[2 * feats :, :] = jnp.concatenate(pieces, axis=0).astype(bf16)


def to_payload(values, ref):
    groups, _, parts, half, tokens = ref.shape
    for part in range(parts):
        span = values[part * groups * half : (part + 1) * groups * half]
        ref[:, 0, part] = span.reshape(groups, half, tokens).astype(bf16)


def from_payload(ref):
    groups, _, parts, half, tokens = ref.shape
    return jnp.concatenate(
        [ref[:, 0, part].astype(f32).reshape(groups * half, tokens) for part in range(parts)], axis=0
    )


def forward_kernel(x_ref, w1d_ref, hidden_ref, slope_ref):
    value, slope = gelu_pair(dot(w1d_ref[...], x_ref[0], NT))
    to_payload(value, hidden_ref)
    slope_ref[0] = slope


def settle_kernel(z_ref, x_ref, pick2_ref, z_out, x_out):
    z_out[0] = dot(pick2_ref[...], from_payload(z_ref).astype(bf16), NN).astype(bf16)
    x_out[0] = jnp.transpose(x_ref[0].astype(f32)).astype(bf16)


def expand_kernel(step_ref, first_ref, second_ref, x_ref, w1_ref, w2_ref, slope_ref):
    del step_ref
    feats = x_ref.shape[2]
    blocks = feats // LANES

    def owners(ref):
        ids = ref[0, 2 * feats :, :].astype(f32)
        return jnp.transpose(jnp.concatenate([ids[8 * b : 8 * b + 8] for b in range(blocks)], axis=1))

    one = first_ref[0, 0:feats, :].astype(f32)
    two = second_ref[0, feats : 2 * feats, :].astype(f32)
    own1 = owners(first_ref)[:, 0:1]
    own2 = owners(second_ref)[:, 1:2]
    for b in range(blocks):
        span = slice(b * LANES, (b + 1) * LANES)
        w1_ref[:, span] = jnp.where(own1 == b, one, 0.0).astype(bf16)
        w2_ref[:, span] = jnp.where(own2 == b, two, 0.0).astype(bf16)
    v = dot(x_ref[0], w1_ref[...], NT)
    _, slope = gelu_pair(jnp.concatenate([v[:, : feats // 2], v[:, feats // 2 :]], axis=0))
    slope_ref[...] = slope


def mix(g, w2_ref, mixed_ref):
    feats = g.shape[1]
    s = dot(g, w2_ref[...], NT)
    s = jnp.concatenate([s[:, : feats // 2], s[:, feats // 2 :]], axis=0)
    mixed_ref[...] = jnp.transpose(s).reshape(mixed_ref.shape).astype(bf16)


def start_kernel(g_ref, packed_ref, stored_ref, mixed_ref, w2_ref):
    feats = g_ref.shape[1]
    blocks = feats // LANES
    ids = packed_ref[0, 2 * feats :, :].astype(f32)
    own = jnp.transpose(jnp.concatenate([ids[8 * b : 8 * b + 8] for b in range(blocks)], axis=1))[:, 1:2]
    two = packed_ref[0, feats : 2 * feats, :].astype(f32)
    for b in range(blocks):
        w2_ref[:, b * LANES : (b + 1) * LANES] = jnp.where(own == b, two, 0.0).astype(bf16)
    g = g_ref[...]
    stored_ref[0] = g
    mix(g, w2_ref, mixed_ref)


def relay_kernel(step_ref, returned_ref, g_in_ref, slope_ref, w1_ref, w2_ref, old_ref, stored_ref, g_ref, mixed_ref):
    del step_ref, old_ref
    groups, half, lanes = returned_ref.shape
    tokens = lanes // 2
    dh = returned_ref[...].astype(f32).reshape(groups * half, lanes)
    da = (jnp.transpose(dh) * slope_ref[...]).astype(bf16)
    g = g_in_ref[...].astype(f32)
    g = g + (dot(da[:tokens], w1_ref[: groups * half], NN) + dot(da[tokens:], w1_ref[groups * half :], NN))
    g = g.astype(bf16)
    stored_ref[0] = g
    g_ref[...] = g
    mix(g, w2_ref, mixed_ref)


def owner_send_kernel(g_ref, w2d_ref, mixed_ref):
    to_payload(dot(w2d_ref[...], g_ref[0], NT), mixed_ref)


def owner_kernel(drop_ref, returned_ref, slope_ref, pick1_ref, w1_ref, x_ref, z_ref, g_ref, grads_ref, first_ref, second_ref):
    blocks, size, _ = first_ref.shape
    keep = drop_ref[0].astype(f32)
    da = jnp.transpose(from_payload(returned_ref) * slope_ref[0]).astype(bf16)
    da = dot(da, pick1_ref[...], NN).astype(bf16)

    @pl.when(pl.program_id(0) == 0)
    def _():
        first_ref[...] = jnp.zeros_like(first_ref)
        second_ref[...] = jnp.zeros_like(second_ref)

    for block in range(blocks):
        span = slice(block * size, (block + 1) * size)
        g = g_ref[0, :, span]
        grads_ref[0, :, span] = (g.astype(f32) + dot(da[:, span], w1_ref[block], NT)).astype(bf16)
        first_ref[block] += dot(x_ref[0, span, :], da[:, span], NN)
        second_ref[block] += keep * dot(z_ref[0, span, :], g, NN)


def on_device(section_inputs, out_grad, w_first, w_second, drop_flags, perm):
    sections = lax.axis_size("pipe")
    row = lax.axis_index("pipe").astype(i32)
    groups = lax.axis_size("tensor")
    group = lax.axis_index("tensor").astype(i32)
    x = section_inputs[0]
    micros, tokens, feats = x.shape
    share = micros * tokens // sections
    blocks, size = w_first.shape[2], w_first.shape[3]
    half = feats // groups // 2
    drop = drop_flags.reshape(1)
    params = pltpu.CompilerParams(vmem_limit_bytes=60 * 1024 * 1024)
    square = sds((feats, feats), bf16)

    xs = lax.all_to_all(x.reshape(sections, share, feats), "pipe", 0, 0, tiled=True)

    packed, w1d, w2d, pick1, pick2 = pl.pallas_call(
        prep_kernel,
        in_specs=[whole(pltpu.SMEM), whole(pltpu.SMEM), whole(), whole(), whole()],
        out_specs=[whole()] * 5,
        out_shape=[sds((2 * feats + IDS, LANES), bf16)] + [square] * 4,
        compiler_params=params,
        name="prep",
    )(group.reshape(1), drop, perm.reshape(groups, feats), w_first[0, 0], w_second[0, 0])
    packed = lax.all_gather(packed, "pipe")

    payload = sds((groups, micros, 2, half, tokens), bf16)
    payload_spec = pl.BlockSpec((groups, 1, 2, half, tokens), lambda m: (0, m, 0, 0, 0))
    token_spec = pl.BlockSpec((1, tokens, feats), lambda m: (m, 0, 0))
    feature_spec = pl.BlockSpec((1, feats, tokens), lambda m: (m, 0, 0))
    square_spec = pl.BlockSpec((feats, feats), lambda m: (0, 0))
    weight_spec = pl.BlockSpec((blocks, size, size), lambda m: (0, 0, 0))

    hidden, slope = pl.pallas_call(
        forward_kernel,
        grid=(micros,),
        in_specs=[token_spec, square_spec],
        out_specs=[payload_spec, feature_spec],
        out_shape=[payload, sds((micros, feats, tokens), f32)],
        compiler_params=params,
        name="forward",
    )(x, w1d)
    hidden, xs = lax.optimization_barrier((hidden, xs))
    z = lax.all_to_all(hidden, "tensor", 0, 0, tiled=True)

    mixed_shape = sds((groups, half, 2 * share), bf16)
    value_shape = sds((share, feats), bf16)
    stored_shape = sds((sections, share, feats), bf16)
    pack_rows = 2 * feats + IDS
    own_grad = lax.dynamic_index_in_dim(out_grad.reshape(sections, share, feats), row, 0, keepdims=False)
    own_grad, z = lax.optimization_barrier((own_grad, z))
    g = own_grad
    stored, mixed = pl.pallas_call(
        start_kernel,
        grid=(1,),
        in_specs=[
            pl.BlockSpec((share, feats), lambda i: (0, 0)),
            pl.BlockSpec((1, pack_rows, LANES), lambda i: (sections - 1, 0, 0)),
        ],
        out_specs=[
            pl.BlockSpec((1, share, feats), lambda i: (sections - 1, 0, 0)),
            pl.BlockSpec((groups, half, 2 * share), lambda i: (0, 0, 0)),
        ],
        out_shape=[stored_shape, mixed_shape],
        scratch_shapes=[pltpu.VMEM((feats, feats), bf16)],
        compiler_params=params,
        name="start",
    )(g, packed)

    expand = pl.pallas_call(
        expand_kernel,
        grid_spec=pltpu.PrefetchScalarGridSpec(
            num_scalar_prefetch=1,
            grid=(1,),
            in_specs=[
                pl.BlockSpec((1, pack_rows, LANES), lambda i, s: (s[0], 0, 0)),
                pl.BlockSpec((1, pack_rows, LANES), lambda i, s: (s[0] - 1, 0, 0)),
                pl.BlockSpec((1, share, feats), lambda i, s: (s[0], 0, 0)),
            ],
            out_specs=[
                pl.BlockSpec((feats, feats), lambda i, s: (0, 0)),
                pl.BlockSpec((feats, feats), lambda i, s: (0, 0)),
                pl.BlockSpec((2 * share, feats // 2), lambda i, s: (0, 0)),
            ],
        ),
        out_shape=[square, square, sds((2 * share, feats // 2), f32)],
        compiler_params=params,
        name="expand",
    )
    relay = pl.pallas_call(
        relay_kernel,
        grid_spec=pltpu.PrefetchScalarGridSpec(
            num_scalar_prefetch=1,
            grid=(1,),
            in_specs=[whole()] * 5 + [whole(pl.ANY)],
            out_specs=[
                pl.BlockSpec((1, share, feats), lambda i, s: (s[0] - 1, 0, 0)),
                whole(),
                whole(),
            ],
        ),
        out_shape=[stored_shape, value_shape, mixed_shape],
        input_output_aliases={6: 0},
        compiler_params=params,
        name="relay",
    )

    def advance(k, carry):
        g, mixed, stored = carry
        at = jnp.full((1,), sections - 1 - k, i32)
        returned = lax.all_to_all(mixed, "tensor", 0, 0, tiled=True)
        w1, w2, scale = expand(at, packed, packed, xs)
        stored, g, mixed = relay(at, returned, g, scale, w1, w2, stored)
        return (g, mixed, stored)

    _, _, stored = lax.fori_loop(0, sections - 1, advance, (g, mixed, stored))
    stored, z = lax.optimization_barrier((stored, z))
    cotangent = lax.all_to_all(stored, "pipe", 0, 0, tiled=True)
    cotangent = cotangent.reshape(micros, tokens, feats)
    z, x_turned = pl.pallas_call(
        settle_kernel,
        grid=(micros,),
        in_specs=[payload_spec, token_spec, square_spec],
        out_specs=[feature_spec, feature_spec],
        out_shape=[sds((micros, feats, tokens), bf16)] * 2,
        compiler_params=params,
        name="settle",
    )(z, x, pick2)

    mixed = pl.pallas_call(
        owner_send_kernel,
        grid=(micros,),
        in_specs=[token_spec, square_spec],
        out_specs=payload_spec,
        out_shape=payload,
        compiler_params=params,
        name="owner_send",
    )(cotangent, w2d)
    returned = lax.all_to_all(mixed, "tensor", 0, 0, tiled=True)
    grads, first, second = pl.pallas_call(
        owner_kernel,
        grid=(micros,),
        in_specs=[
            whole(pltpu.SMEM),
            payload_spec,
            feature_spec,
            square_spec,
            weight_spec,
            feature_spec,
            feature_spec,
            token_spec,
        ],
        out_specs=[token_spec, weight_spec, weight_spec],
        out_shape=[sds(x.shape, bf16), sds((blocks, size, size), f32), sds((blocks, size, size), f32)],
        compiler_params=params,
        name="owner",
    )(drop, returned, slope, pick1, w_first[0, 0], x_turned, z, cotangent)
    return (grads[None], first[None, None], second[None, None])


def solution(mesh):
    placed = (
        P("pipe", None, None, "tensor"),
        P(None, None, "tensor"),
        P("pipe", None, "tensor", None, None),
        P("pipe", None, "tensor", None, None),
        P("pipe", None),
        P("pipe", None, None),
    )
    return jax.shard_map(
        on_device,
        mesh=mesh,
        in_specs=placed,
        out_specs=(
            P("pipe", None, None, "tensor"),
            P("pipe", None, "tensor", None, None),
            P("pipe", None, "tensor", None, None),
        ),
        check_vma=False,
    )
```

time: 644 us -> 458 us (0.71)
  the two profiles are of different devices: /device:TPU:128 before, /device:TPU:1 now
where the time goes in v3:
time: 458 us; the launch traced here: 455 us
  Pallas kernels  154 us (34%)
  waiting for transfers between devices  120 us (26%)
  starting transfers between devices  88.4 us (19%)
  blocking collectives  55 us (12%)
  local copies, waits for them, and re-layouts  22.4 us (5%)
  between operations  14.8 us (3%)
    all_to_all x15, starting transfers between devices, advance(): returned = lax.all_to_all(mixed, 'tensor', 0, 0, tiled=True)  67.7 us
    pallas_call x15, Pallas kernels, advance(): w1, w2, scale = expand(at, packed, packed, xs)  59.6 us
    all_to_all x1, blocking collectives, on_device(): cotangent = lax.all_to_all(stored, 'pipe', 0, 0, tiled=True)  55 us
    pallas_call x15, Pallas kernels, advance(): stored, g, mixed = relay(at, returned, g, scale, w1, w2, stored)  50.7 us
    all_to_all x1, waiting for transfers between devices, on_device(): lax.all_to_all(x.reshape(sections, share, feats), 'pipe', 0, 0, tiled=True)  44 us
    all_to_all x15, waiting for transfers between devices, advance(): returned = lax.all_to_all(mixed, 'tensor', 0, 0, tiled=True)  31.1 us
    all_to_all x1, waiting for transfers between devices, on_device(): z = lax.all_to_all(hidden, 'tensor', 0, 0, tiled=True)  26 us
    while x45, local copies, waits for them, and re-layouts  18.9 us
  transfers between devices with their start and end apart: 19, of which 18 were waited for; matrix products, arithmetic and copies ran while one was open for 2% of the time, Pallas kernels for 17%

profile of v3, /device:TPU:1, one launch (start us, length us, event | category | flops | bytes accessed | tf_op | source)
XLA Modules:
  0.0 455.3 jit_solution(9855433225581781988)
XLA Ops:
  10.7 5.0 %prep.1 = (bf16[1600,128]{1,0:T(8,128)(2,1)}, bf16[768,768]{1,0:T(8,128)(2,1)}, bf16[768,768]{1,0:T(8,128)(2,1)}, bf16[768,768]{1,0:T(8,128)(2,1)}, bf16[768,768]{1,0:T(8,128)(2,1)}) custom-call(s32[1]{0:T(128)} %bitcast.5.group_ref, s32[1]{0:T(128)} %bitcast.17.drop_ref, s32[16,768]{1,0:T(8,128)} %reshape.24.perm_ref, bf16[6,128,128]{2,1,0:T(8,128)(2,1)} %bitcast.27, ...), custom_call_target="tpu_custom_call" | custom-call | tf_op jit(solution)/shard_map/prep/pallas_call | solution.py:213
  15.7 10.0 %all-to-all-start.1 = ((bf16[16,64,768]{2,1,0:T(8,128)(2,1)}), bf16[16,64,768]{2,1,0:T(8,128)(2,1)S(1)}, u32[]{:S(2)}, u32[]{:S(2)}) async-start(bf16[16,64,768]{2,1,0:T(8,128)(2,1)} %bitcast.22), calls=%async_computation.1 | async-start | bytes 3145728 | tf_op jit(solution)/shard_map/all_to_all | solution.py:211
  25.7 8.5 %forward.1 = (bf16[16,8,2,24,128]{4,3,2,1,0:T(8,128)(2,1)}, f32[8,768,128]{2,1,0:T(8,128)}) custom-call(bf16[8,128,768]{2,1,0:T(8,128)(2,1)} %bitcast.23, bf16[768,768]{1,0:T(8,128)(2,1)} %get-tuple-element.134.w1d_ref), custom_call_target="tpu_custom_call" | custom-call | tf_op jit(solution)/shard_map/forward/pallas_call | solution.py:230
  34.2 44.0 %all-to-all-done.1 = bf16[16,64,768]{2,1,0:T(8,128)(2,1)S(1)} async-done(((bf16[16,64,768]{2,1,0:T(8,128)(2,1)}), bf16[16,64,768]{2,1,0:T(8,128)(2,1)S(1)}, u32[]{:S(2)}, u32[]{:S(2)}) %all-to-all-start.1) | async-done | bytes 1572896 | tf_op jit(solution)/shard_map/all_to_all | solution.py:211
  79.4 7.0 %all-to-all-start.2 = ((bf16[16,8,2,24,128]{4,3,2,1,0:T(8,128)(2,1)}), bf16[16,8,2,24,128]{4,3,2,1,0:T(8,128)(2,1)}, u32[]{:S(2)}, u32[]{:S(2)}) async-start(bf16[16,8,2,24,128]{4,3,2,1,0:T(8,128)(2,1)} %get-tuple-element.136), calls=%async_computation.2 | async-start | bytes 3145728 | tf_op jit(solution)/shard_map/all_to_all | solution.py:240
  86.4 26.0 %all-to-all-done.2.z_ref = bf16[16,8,2,24,128]{4,3,2,1,0:T(8,128)(2,1)} async-done(((bf16[16,8,2,24,128]{4,3,2,1,0:T(8,128)(2,1)}), bf16[16,8,2,24,128]{4,3,2,1,0:T(8,128)(2,1)}, u32[]{:S(2)}, u32[]{:S(2)}) %all-to-all-start.2) | async-done | bytes 1572896 | tf_op jit(solution)/shard_map/all_to_all | solution.py:240
  115.3 228.2 %while.17 = (s32[]{:T(128)}, bf16[64,768]{1,0:T(8,128)(2,1)S(1)}, bf16[16,24,128]{2,1,0:T(8,128)(2,1)}, bf16[16,64,768]{2,1,0:T(8,128)(2,1)S(1)}, bf16[16,1600,1...) while((s32[]{:T(128)}, bf16[64,768]{1,0:T(8,128)(2,1)S(1)}, ...), condition=%wide.region_1.2_spmd, body=%wide.region_0.1_spmd.sunk | while | flops 3 | bytes 884893 | solution.py:312
  119.4 4.0 expand.5
  129.7 4.3 all-to-all-start
  144.7 4.6 %all-to-all-start = ((bf16[16,24,128]{2,1,0:T(8,128)(2,1)}), bf16[16,24,128]{2,1,0:T(8,128)(2,1)S(1)}, u32[]{:S(2)}, u32[]{:S(2)}) async-start(bf16[16,24,128]{2,1,0:T(8,128)(2,1)} %get-tuple-element.226), calls=%async_computation | async-start | bytes 196608 | tf_op jit(solution)/shard_map/while/body/eval_jaxpr/all_to_all | solution.py:307
  150.0 4.0 expand.5
  160.0 4.6 %all-to-all-start = ((bf16[16,24,128]{2,1,0:T(8,128)(2,1)}), bf16[16,24,128]{2,1,0:T(8,128)(2,1)S(1)}, u32[]{:S(2)}, u32[]{:S(2)}) async-start(bf16[16,24,128]{2,1,0:T(8,128)(2,1)} %get-tuple-element.226), calls=%async_computation | async-start | bytes 196608 | tf_op jit(solution)/shard_map/while/body/eval_jaxpr/all_to_all | solution.py:307
  175.3 4.6 %all-to-all-start = ((bf16[16,24,128]{2,1,0:T(8,128)(2,1)}), bf16[16,24,128]{2,1,0:T(8,128)(2,1)S(1)}, u32[]{:S(2)}, u32[]{:S(2)}) async-start(bf16[16,24,128]{2,1,0:T(8,128)(2,1)} %get-tuple-element.226), calls=%async_computation | async-start | bytes 196608 | tf_op jit(solution)/shard_map/while/body/eval_jaxpr/all_to_all | solution.py:307
  190.6 4.6 %all-to-all-start = ((bf16[16,24,128]{2,1,0:T(8,128)(2,1)}), bf16[16,24,128]{2,1,0:T(8,128)(2,1)S(1)}, u32[]{:S(2)}, u32[]{:S(2)}) async-start(bf16[16,24,128]{2,1,0:T(8,128)(2,1)} %get-tuple-element.226), calls=%async_computation | async-start | bytes 196608 | tf_op jit(solution)/shard_map/while/body/eval_jaxpr/all_to_all | solution.py:307
  195.8 4.0 expand.5
  205.9 4.6 %all-to-all-start = ((bf16[16,24,128]{2,1,0:T(8,128)(2,1)}), bf16[16,24,128]{2,1,0:T(8,128)(2,1)S(1)}, u32[]{:S(2)}, u32[]{:S(2)}) async-start(bf16[16,24,128]{2,1,0:T(8,128)(2,1)} %get-tuple-element.226), calls=%async_computation | async-start | bytes 196608 | tf_op jit(solution)/shard_map/while/body/eval_jaxpr/all_to_all | solution.py:307
  221.2 4.6 %all-to-all-start = ((bf16[16,24,128]{2,1,0:T(8,128)(2,1)}), bf16[16,24,128]{2,1,0:T(8,128)(2,1)S(1)}, u32[]{:S(2)}, u32[]{:S(2)}) async-start(bf16[16,24,128]{2,1,0:T(8,128)(2,1)} %get-tuple-element.226), calls=%async_computation | async-start | bytes 196608 | tf_op jit(solution)/shard_map/while/body/eval_jaxpr/all_to_all | solution.py:307
  226.4 4.0 expand.5
  236.5 4.6 %all-to-all-start = ((bf16[16,24,128]{2,1,0:T(8,128)(2,1)}), bf16[16,24,128]{2,1,0:T(8,128)(2,1)S(1)}, u32[]{:S(2)}, u32[]{:S(2)}) async-start(bf16[16,24,128]{2,1,0:T(8,128)(2,1)} %get-tuple-element.226), calls=%async_computation | async-start | bytes 196608 | tf_op jit(solution)/shard_map/while/body/eval_jaxpr/all_to_all | solution.py:307
  251.8 4.6 %all-to-all-start = ((bf16[16,24,128]{2,1,0:T(8,128)(2,1)}), bf16[16,24,128]{2,1,0:T(8,128)(2,1)S(1)}, u32[]{:S(2)}, u32[]{:S(2)}) async-start(bf16[16,24,128]{2,1,0:T(8,128)(2,1)} %get-tuple-element.226), calls=%async_computation | async-start | bytes 196608 | tf_op jit(solution)/shard_map/while/body/eval_jaxpr/all_to_all | solution.py:307
  257.0 4.0 expand.5
  267.1 4.6 %all-to-all-start = ((bf16[16,24,128]{2,1,0:T(8,128)(2,1)}), bf16[16,24,128]{2,1,0:T(8,128)(2,1)S(1)}, u32[]{:S(2)}, u32[]{:S(2)}) async-start(bf16[16,24,128]{2,1,0:T(8,128)(2,1)} %get-tuple-element.226), calls=%async_computation | async-start | bytes 196608 | tf_op jit(solution)/shard_map/while/body/eval_jaxpr/all_to_all | solution.py:307
  272.3 4.0 expand.5
  282.3 4.6 %all-to-all-start = ((bf16[16,24,128]{2,1,0:T(8,128)(2,1)}), bf16[16,24,128]{2,1,0:T(8,128)(2,1)S(1)}, u32[]{:S(2)}, u32[]{:S(2)}) async-start(bf16[16,24,128]{2,1,0:T(8,128)(2,1)} %get-tuple-element.226), calls=%async_computation | async-start | bytes 196608 | tf_op jit(solution)/shard_map/while/body/eval_jaxpr/all_to_all | solution.py:307
  297.6 4.6 %all-to-all-start = ((bf16[16,24,128]{2,1,0:T(8,128)(2,1)}), bf16[16,24,128]{2,1,0:T(8,128)(2,1)S(1)}, u32[]{:S(2)}, u32[]{:S(2)}) async-start(bf16[16,24,128]{2,1,0:T(8,128)(2,1)} %get-tuple-element.226), calls=%async_computation | async-start | bytes 196608 | tf_op jit(solution)/shard_map/while/body/eval_jaxpr/all_to_all | solution.py:307
  312.9 4.6 %all-to-all-start = ((bf16[16,24,128]{2,1,0:T(8,128)(2,1)}), bf16[16,24,128]{2,1,0:T(8,128)(2,1)S(1)}, u32[]{:S(2)}, u32[]{:S(2)}) async-start(bf16[16,24,128]{2,1,0:T(8,128)(2,1)} %get-tuple-element.226), calls=%async_computation | async-start | bytes 196608 | tf_op jit(solution)/shard_map/while/body/eval_jaxpr/all_to_all | solution.py:307
  328.2 4.6 %all-to-all-start = ((bf16[16,24,128]{2,1,0:T(8,128)(2,1)}), bf16[16,24,128]{2,1,0:T(8,128)(2,1)S(1)}, u32[]{:S(2)}, u32[]{:S(2)}) async-start(bf16[16,24,128]{2,1,0:T(8,128)(2,1)} %get-tuple-element.226), calls=%async_computation | async-start | bytes 196608 | tf_op jit(solution)/shard_map/while/body/eval_jaxpr/all_to_all | solution.py:307
  343.5 55.0 %all_to_all.26 = bf16[16,64,768]{2,1,0:T(8,128)(2,1)} all-to-all(bf16[16,64,768]{2,1,0:T(8,128)(2,1)S(1)} %get-tuple-element.144), channel_id=1, replica_groups=mesh['pipe'=16,'tensor'=16] {'pipe'}, dimensions={0} | all-to-all | bytes 3145728 | tf_op jit(solution)/shard_map/all_to_all | solution.py:314
  398.5 7.6 %owner_send.1 = bf16[16,8,2,24,128]{4,3,2,1,0:T(8,128)(2,1)} custom-call(bf16[8,128,768]{2,1,0:T(8,128)(2,1)} %bitcast.25, bf16[768,768]{1,0:T(8,128)(2,1)} %get-tuple-element.145.w2d_ref), custom_call_target="tpu_custom_call" | custom-call | tf_op jit(solution)/shard_map/owner_send/pallas_call | solution.py:326
  409.9 8.2 %settle.1 = (bf16[8,768,128]{2,1,0:T(8,128)(2,1)}, bf16[8,768,128]{2,1,0:T(8,128)(2,1)}) custom-call(bf16[16,8,2,24,128]{4,3,2,1,0:T(8,128)(2,1)} %all-to-all-done.2.z_ref, bf16[8,128,768]{2,1,0:T(8,128)(2,1)} %bitcast.24, bf16[768,768]{1,0:T(8,128)(2,1)} %get-tuple-element.149.pick2_ref), custom_call_target="tpu_custom_call" | custom-call | tf_op jit(solution)/shard_map/settle/pallas_call | solution.py:316
  418.0 18.3 %all-to-all-done.4.returned_ref = bf16[16,8,2,24,128]{4,3,2,1,0:T(8,128)(2,1)S(1)} async-done(((bf16[16,8,2,24,128]{4,3,2,1,0:T(8,128)(2,1)}), bf16[16,8,2,24,128]{4,3,2,1,0:T(8,128)(2,1)S(1)}, u32[]{:S(2)}, u32[]{:S(2)}) %all-to-all-start.4) | async-done | bytes 1572896 | tf_op jit(solution)/shard_map/all_to_all | solution.py:335
  437.5 11.0 %owner.1 = (bf16[8,128,768]{2,1,0:T(8,128)(2,1)}, f32[6,128,128]{2,1,0:T(8,128)}, f32[6,128,128]{2,1,0:T(8,128)}) custom-call(s32[1]{0:T(128)} %bitcast.18.drop_ref, bf16[16,8,2,24,128]{4,3,2,1,0:T(8,128)(2,1)} %copy-done.3, f32[8,768,128]{2,1,0:T(8,128)} %get-tuple-element.146.slope_ref, bf16[768,768]{1,0:T(8,128)(2,1)} %get-tuple-element.147.pick1_ref, ...), custom_call_target="tpu_custom_call" | custom-call | tf_op jit(solution)/shard_map/owner/pallas_call | solution.py:336
  (100 shorter events, 151.7 us)
Async XLA Ops:
  7.2 79.2 %copy-start = (bf16[8,128,768]{2,1,0:T(8,128)(2,1)S(1)}, bf16[8,128,768]{2,1,0:T(8,128)(2,1)}, u32[]{:S(2)}) copy-start(bf16[8,128,768]{2,1,0:T(8,128)(2,1)} %param.9) | copy-start | bytes 4718596
  7.2 105.3 %all-gather.3.cloned.1.call-start = ((), (), s32[]{:S(2)}) async-start(), calls=%async_computation.5 | async-start | bytes 6963200 | tf_op jit(solution)/shard_map/all_gather | solution.py:221
  15.7 62.5 %all-to-all-start.1 = ((bf16[16,64,768]{2,1,0:T(8,128)(2,1)}), bf16[16,64,768]{2,1,0:T(8,128)(2,1)S(1)}, u32[]{:S(2)}, u32[]{:S(2)}) async-start(bf16[16,64,768]{2,1,0:T(8,128)(2,1)} %bitcast.22), calls=%async_computation.1 | async-start | bytes 3145728 | tf_op jit(solution)/shard_map/all_to_all | solution.py:211
  78.2 1.1 copy-start.1
  79.4 33.1 %all-to-all-start.2 = ((bf16[16,8,2,24,128]{4,3,2,1,0:T(8,128)(2,1)}), bf16[16,8,2,24,128]{4,3,2,1,0:T(8,128)(2,1)}, u32[]{:S(2)}, u32[]{:S(2)}) async-start(bf16[16,8,2,24,128]{4,3,2,1,0:T(8,128)(2,1)} %get-tuple-element.136), calls=%async_computation.2 | async-start | bytes 3145728 | tf_op jit(solution)/shard_map/all_to_all | solution.py:240
  115.3 10.4 %all-to-all-start = ((bf16[16,24,128]{2,1,0:T(8,128)(2,1)}), bf16[16,24,128]{2,1,0:T(8,128)(2,1)S(1)}, u32[]{:S(2)}, u32[]{:S(2)}) async-start(bf16[16,24,128]{2,1,0:T(8,128)(2,1)} %get-tuple-element.226), calls=%async_computation | async-start | bytes 196608 | tf_op jit(solution)/shard_map/while/body/eval_jaxpr/all_to_all | solution.py:307
  125.7 0.6 copy-start.2
  129.7 11.0 %all-to-all-start = ((bf16[16,24,128]{2,1,0:T(8,128)(2,1)}), bf16[16,24,128]{2,1,0:T(8,128)(2,1)S(1)}, u32[]{:S(2)}, u32[]{:S(2)}) async-start(bf16[16,24,128]{2,1,0:T(8,128)(2,1)} %get-tuple-element.226), calls=%async_computation | async-start | bytes 196608 | tf_op jit(solution)/shard_map/while/body/eval_jaxpr/all_to_all | solution.py:307
  140.7 0.6 copy-start.2
  144.7 11.3 %all-to-all-start = ((bf16[16,24,128]{2,1,0:T(8,128)(2,1)}), bf16[16,24,128]{2,1,0:T(8,128)(2,1)S(1)}, u32[]{:S(2)}, u32[]{:S(2)}) async-start(bf16[16,24,128]{2,1,0:T(8,128)(2,1)} %get-tuple-element.226), calls=%async_computation | async-start | bytes 196608 | tf_op jit(solution)/shard_map/while/body/eval_jaxpr/all_to_all | solution.py:307
  156.0 0.6 copy-start.2
  160.0 11.3 %all-to-all-start = ((bf16[16,24,128]{2,1,0:T(8,128)(2,1)}), bf16[16,24,128]{2,1,0:T(8,128)(2,1)S(1)}, u32[]{:S(2)}, u32[]{:S(2)}) async-start(bf16[16,24,128]{2,1,0:T(8,128)(2,1)} %get-tuple-element.226), calls=%async_computation | async-start | bytes 196608 | tf_op jit(solution)/shard_map/while/body/eval_jaxpr/all_to_all | solution.py:307
  175.3 11.3 %all-to-all-start = ((bf16[16,24,128]{2,1,0:T(8,128)(2,1)}), bf16[16,24,128]{2,1,0:T(8,128)(2,1)S(1)}, u32[]{:S(2)}, u32[]{:S(2)}) async-start(bf16[16,24,128]{2,1,0:T(8,128)(2,1)} %get-tuple-element.226), calls=%async_computation | async-start | bytes 196608 | tf_op jit(solution)/shard_map/while/body/eval_jaxpr/all_to_all | solution.py:307
  186.6 0.6 copy-start.2
  190.6 11.3 %all-to-all-start = ((bf16[16,24,128]{2,1,0:T(8,128)(2,1)}), bf16[16,24,128]{2,1,0:T(8,128)(2,1)S(1)}, u32[]{:S(2)}, u32[]{:S(2)}) async-start(bf16[16,24,128]{2,1,0:T(8,128)(2,1)} %get-tuple-element.226), calls=%async_computation | async-start | bytes 196608 | tf_op jit(solution)/shard_map/while/body/eval_jaxpr/all_to_all | solution.py:307
  201.9 0.6 copy-start.2
  205.9 11.3 %all-to-all-start = ((bf16[16,24,128]{2,1,0:T(8,128)(2,1)}), bf16[16,24,128]{2,1,0:T(8,128)(2,1)S(1)}, u32[]{:S(2)}, u32[]{:S(2)}) async-start(bf16[16,24,128]{2,1,0:T(8,128)(2,1)} %get-tuple-element.226), calls=%async_computation | async-start | bytes 196608 | tf_op jit(solution)/shard_map/while/body/eval_jaxpr/all_to_all | solution.py:307
  221.2 11.3 %all-to-all-start = ((bf16[16,24,128]{2,1,0:T(8,128)(2,1)}), bf16[16,24,128]{2,1,0:T(8,128)(2,1)S(1)}, u32[]{:S(2)}, u32[]{:S(2)}) async-start(bf16[16,24,128]{2,1,0:T(8,128)(2,1)} %get-tuple-element.226), calls=%async_computation | async-start | bytes 196608 | tf_op jit(solution)/shard_map/while/body/eval_jaxpr/all_to_all | solution.py:307
  232.5 0.6 copy-start.2
  236.5 11.3 %all-to-all-start = ((bf16[16,24,128]{2,1,0:T(8,128)(2,1)}), bf16[16,24,128]{2,1,0:T(8,128)(2,1)S(1)}, u32[]{:S(2)}, u32[]{:S(2)}) async-start(bf16[16,24,128]{2,1,0:T(8,128)(2,1)} %get-tuple-element.226), calls=%async_computation | async-start | bytes 196608 | tf_op jit(solution)/shard_map/while/body/eval_jaxpr/all_to_all | solution.py:307
  251.8 11.3 %all-to-all-start = ((bf16[16,24,128]{2,1,0:T(8,128)(2,1)}), bf16[16,24,128]{2,1,0:T(8,128)(2,1)S(1)}, u32[]{:S(2)}, u32[]{:S(2)}) async-start(bf16[16,24,128]{2,1,0:T(8,128)(2,1)} %get-tuple-element.226), calls=%async_computation | async-start | bytes 196608 | tf_op jit(solution)/shard_map/while/body/eval_jaxpr/all_to_all | solution.py:307
  263.0 0.6 copy-start.2
  267.1 11.3 %all-to-all-start = ((bf16[16,24,128]{2,1,0:T(8,128)(2,1)}), bf16[16,24,128]{2,1,0:T(8,128)(2,1)S(1)}, u32[]{:S(2)}, u32[]{:S(2)}) async-start(bf16[16,24,128]{2,1,0:T(8,128)(2,1)} %get-tuple-element.226), calls=%async_computation | async-start | bytes 196608 | tf_op jit(solution)/shard_map/while/body/eval_jaxpr/all_to_all | solution.py:307
  282.3 11.3 %all-to-all-start = ((bf16[16,24,128]{2,1,0:T(8,128)(2,1)}), bf16[16,24,128]{2,1,0:T(8,128)(2,1)S(1)}, u32[]{:S(2)}, u32[]{:S(2)}) async-start(bf16[16,24,128]{2,1,0:T(8,128)(2,1)} %get-tuple-element.226), calls=%async_computation | async-start | bytes 196608 | tf_op jit(solution)/shard_map/while/body/eval_jaxpr/all_to_all | solution.py:307
  293.6 0.6 copy-start.2
  297.6 11.3 %all-to-all-start = ((bf16[16,24,128]{2,1,0:T(8,128)(2,1)}), bf16[16,24,128]{2,1,0:T(8,128)(2,1)S(1)}, u32[]{:S(2)}, u32[]{:S(2)}) async-start(bf16[16,24,128]{2,1,0:T(8,128)(2,1)} %get-tuple-element.226), calls=%async_computation | async-start | bytes 196608 | tf_op jit(solution)/shard_map/while/body/eval_jaxpr/all_to_all | solution.py:307
  308.9 0.6 copy-start.2
  312.9 11.3 %all-to-all-start = ((bf16[16,24,128]{2,1,0:T(8,128)(2,1)}), bf16[16,24,128]{2,1,0:T(8,128)(2,1)S(1)}, u32[]{:S(2)}, u32[]{:S(2)}) async-start(bf16[16,24,128]{2,1,0:T(8,128)(2,1)} %get-tuple-element.226), calls=%async_computation | async-start | bytes 196608 | tf_op jit(solution)/shard_map/while/body/eval_jaxpr/all_to_all | solution.py:307
  328.2 11.3 %all-to-all-start = ((bf16[16,24,128]{2,1,0:T(8,128)(2,1)}), bf16[16,24,128]{2,1,0:T(8,128)(2,1)S(1)}, u32[]{:S(2)}, u32[]{:S(2)}) async-start(bf16[16,24,128]{2,1,0:T(8,128)(2,1)} %get-tuple-element.226), calls=%async_computation | async-start | bytes 196608 | tf_op jit(solution)/shard_map/while/body/eval_jaxpr/all_to_all | solution.py:307
  339.5 0.6 copy-start.2
  406.1 30.2 %all-to-all-start.4 = ((bf16[16,8,2,24,128]{4,3,2,1,0:T(8,128)(2,1)}), bf16[16,8,2,24,128]{4,3,2,1,0:T(8,128)(2,1)S(1)}, u32[]{:S(2)}, u32[]{:S(2)}) async-start(bf16[16,8,2,24,128]{4,3,2,1,0:T(8,128)(2,1)} %owner_send.1), calls=%async_computation.4 | async-start | bytes 3145728 | tf_op jit(solution)/shard_map/all_to_all | solution.py:335
  436.3 1.2 copy-start.3
  (5 other events, 3.2 us)
Sparse Core Ops, SparseCore 0:
  15.8 80.0 all-gather.2

commit v4 on v3

--- a/solution.py
+++ b/solution.py
@@ -33,8 +33,9 @@
     return value, slope
 
 
-def prep_kernel(group_ref, drop_ref, perm_ref, w1_ref, w2_ref, packed_ref, w1d_ref, w2d_ref, pick1_ref, pick2_ref):
-    groups, feats = perm_ref.shape
+def prep_kernel(group_ref, drop_ref, perm_ref, w1_ref, w2_ref, packed1_ref, packed2_ref, w1d_ref, w2d_ref, pick1_ref, pick2_ref):
+    feats = pick1_ref.shape[0]
+    groups = perm_ref.shape[1] // feats
     blocks, size, _ = w1_ref.shape
     per_peer = feats // groups
     half = per_peer // 2
@@ -44,7 +45,7 @@
     rows = lax.broadcasted_iota(i32, (feats, feats), 0)
     cols = lax.broadcasted_iota(i32, (feats, feats), 1)
     before = jnp.where(rows < cols, 1.0, 0.0).astype(bf16)
-    perm = perm_ref[...]
+    perm = jnp.concatenate([perm_ref[:, g * feats : (g + 1) * feats] for g in range(groups)], axis=0)
     mine = (perm >= base) & (perm < base + feats)
     rank = dot(jnp.where(mine, 1.0, 0.0).astype(bf16), before, NN)
     rank = jnp.where(mine, rank, -1.0).astype(i32)
@@ -58,8 +59,8 @@
             source = jnp.sum(jnp.where(hit, local[peer : peer + 1, :], 0.0), axis=1, keepdims=True)
             parts.append(jnp.where(lane == source.astype(i32), 1.0, 0.0))
     leave = jnp.concatenate(parts, axis=0).astype(bf16)
-    own = perm_ref[pl.ds(own_group, 1), :]
     start = lax.broadcasted_iota(i32, (groups, feats), 0)
+    own = jnp.sum(jnp.where(start == own_group, perm, 0), axis=0, keepdims=True)
     from_group = (own >= start * feats) & (own < start * feats + feats)
     marks = jnp.where(from_group, 1.0, 0.0)
     place = dot(marks.astype(bf16), before, NN)
@@ -79,15 +80,16 @@
         w2d_ref[:, span] = two.astype(bf16)
         part1 += one
         part2 += two
-    packed_ref[0:feats, :] = part1.astype(bf16)
-    packed_ref[feats : 2 * feats, :] = part2.astype(bf16)
+    packed1_ref[0:feats, :] = part1.astype(bf16)
+    packed2_ref[0:feats, :] = part2.astype(bf16)
     line = lax.broadcasted_iota(i32, (8, feats), 0)
     owner = (lax.broadcasted_iota(i32, (8, feats), 1) // size).astype(f32)
-    ids = dot(jnp.where(line == 0, owner, 0.0).astype(bf16), leave, NT)
-    ids += dot(jnp.where(line == 1, owner, 0.0).astype(bf16), arrive, NT)
-    pieces = [ids[:, b * LANES : (b + 1) * LANES] for b in range(feats // LANES)]
-    pieces.append(jnp.zeros((IDS - 8 * len(pieces), LANES), f32))
-    packed_ref[2 * feats :, :] = jnp.concatenate(pieces, axis=0).astype(bf16)
+    owner = jnp.where(line == 0, owner, 0.0).astype(bf16)
+    for ref, chosen in ((packed1_ref, leave), (packed2_ref, arrive)):
+        ids = dot(owner, chosen, NT)
+        pieces = [ids[:, b * LANES : (b + 1) * LANES] for b in range(feats // LANES)]
+        pieces.append(jnp.zeros((IDS - 8 * len(pieces), LANES), f32))
+        ref[feats:, :] = jnp.concatenate(pieces, axis=0).astype(bf16)
 
 
 def to_payload(values, ref):
@@ -115,60 +117,67 @@
     x_out[0] = jnp.transpose(x_ref[0].astype(f32)).astype(bf16)
 
 
+def spread(packed_ref, dense_ref):
+    feats = dense_ref.shape[0]
+    blocks = feats // LANES
+    ids = packed_ref[0, feats:, :].astype(f32)
+    own = jnp.transpose(jnp.concatenate([ids[8 * b : 8 * b + 8] for b in range(blocks)], axis=1))[:, 0:1]
+    values = packed_ref[0, 0:feats, :].astype(f32)
+    for b in range(blocks):
+        dense_ref[:, b * LANES : (b + 1) * LANES] = jnp.where(own == b, values, 0.0).astype(bf16)
+
+
 def expand_kernel(step_ref, first_ref, second_ref, x_ref, w1_ref, w2_ref, slope_ref):
     del step_ref
     feats = x_ref.shape[2]
-    blocks = feats // LANES
-
-    def owners(ref):
-        ids = ref[0, 2 * feats :, :].astype(f32)
-        return jnp.transpose(jnp.concatenate([ids[8 * b : 8 * b + 8] for b in range(blocks)], axis=1))
-
-    one = first_ref[0, 0:feats, :].astype(f32)
-    two = second_ref[0, feats : 2 * feats, :].astype(f32)
-    own1 = owners(first_ref)[:, 0:1]
-    own2 = owners(second_ref)[:, 1:2]
-    for b in range(blocks):
-        span = slice(b * LANES, (b + 1) * LANES)
-        w1_ref[:, span] = jnp.where(own1 == b, one, 0.0).astype(bf16)
-        w2_ref[:, span] = jnp.where(own2 == b, two, 0.0).astype(bf16)
+    spread(first_ref, w1_ref)
+    spread(second_ref, w2_ref)
     v = dot(x_ref[0], w1_ref[...], NT)
     _, slope = gelu_pair(jnp.concatenate([v[:, : feats // 2], v[:, feats // 2 :]], axis=0))
     slope_ref[...] = slope
 
 
-def mix(g, w2_ref, mixed_ref):
+def mix(g, w2_ref, mixed_ref, ready=(None, None)):
     feats = g.shape[1]
-    s = dot(g, w2_ref[...], NT)
-    s = jnp.concatenate([s[:, : feats // 2], s[:, feats // 2 :]], axis=0)
+    pieces = []
+    for part, wait in enumerate(ready):
+        if wait is not None:
+            wait.wait()
+        pieces.append(dot(g, w2_ref[part * (feats // 2) : (part + 1) * (feats // 2), :], NT))
+    s = jnp.concatenate(pieces, axis=0)
     mixed_ref[...] = jnp.transpose(s).reshape(mixed_ref.shape).astype(bf16)
 
 
-def start_kernel(g_ref, packed_ref, stored_ref, mixed_ref, w2_ref):
-    feats = g_ref.shape[1]
-    blocks = feats // LANES
-    ids = packed_ref[0, 2 * feats :, :].astype(f32)
-    own = jnp.transpose(jnp.concatenate([ids[8 * b : 8 * b + 8] for b in range(blocks)], axis=1))[:, 1:2]
-    two = packed_ref[0, feats : 2 * feats, :].astype(f32)
-    for b in range(blocks):
-        w2_ref[:, b * LANES : (b + 1) * LANES] = jnp.where(own == b, two, 0.0).astype(bf16)
-    g = g_ref[...]
-    stored_ref[0] = g
-    mix(g, w2_ref, mixed_ref)
-
-
-def relay_kernel(step_ref, returned_ref, g_in_ref, slope_ref, w1_ref, w2_ref, old_ref, stored_ref, g_ref, mixed_ref):
-    del step_ref, old_ref
+def start_kernel(g_ref, packed_ref, mixed_ref, w2_ref):
+    spread(packed_ref, w2_ref)
+    mix(g_ref[...], w2_ref, mixed_ref)
+
+
+def relay_kernel(returned_ref, g_in_ref, slope_hbm, w1_hbm, w2_hbm, g_ref, mixed_ref, slope_ref, w1_ref, w2_ref, sems):
     groups, half, lanes = returned_ref.shape
     tokens = lanes // 2
-    dh = returned_ref[...].astype(f32).reshape(groups * half, lanes)
-    da = (jnp.transpose(dh) * slope_ref[...]).astype(bf16)
-    g = g_in_ref[...].astype(f32)
-    g = g + (dot(da[:tokens], w1_ref[: groups * half], NN) + dot(da[tokens:], w1_ref[groups * half :], NN))
-    g = g.astype(bf16)
-    stored_ref[0] = g
+    split = groups * half
+    upper, lower = pl.ds(0, split), pl.ds(split, split)
+    slope_copy = pltpu.make_async_copy(slope_hbm, slope_ref, sems.at[0])
+    copies = [
+        pltpu.make_async_copy(source.at[span], target.at[span], sems.at[1 + index])
+        for index, (source, target, span) in enumerate(
+            [(w1_hbm, w1_ref, upper), (w1_hbm, w1_ref, lower), (w2_hbm, w2_ref, upper), (w2_hbm, w2_ref, lower)]
+        )
+    ]
+    slope_copy.start()
+    for copy in copies:
+        copy.start()
+    dh = jnp.transpose(returned_ref[...].astype(f32).reshape(split, lanes))
+    slope_copy.wait()
+    da = (dh * slope_ref[...]).astype(bf16)
+    copies[0].wait()
+    term = dot(da[:tokens], w1_ref[:split], NN)
+    copies[1].wait()
+    term = term + dot(da[tokens:], w1_ref[split:], NN)
+    g = (g_in_ref[...].astype(f32) + term).astype(bf16)
     g_ref[...] = g
-    mix(g, w2_ref, mixed_ref)
+    mix(g, w2_ref, mixed_ref, copies[2:])
 
 
 def owner_send_kernel(g_ref, w2d_ref, mixed_ref):
@@ -199,26 +208,30 @@
     row = lax.axis_index("pipe").astype(i32)
     groups = lax.axis_size("tensor")
     group = lax.axis_index("tensor").astype(i32)
-    x = section_inputs[0]
-    micros, tokens, feats = x.shape
+    feats = section_inputs.shape[3]
+    tokens = 2 * section_inputs.shape[2]
+    micros = section_inputs.shape[1] // 2
+    x = section_inputs.reshape(micros, tokens, feats)
     share = micros * tokens // sections
     blocks, size = w_first.shape[2], w_first.shape[3]
     half = feats // groups // 2
     drop = drop_flags.reshape(1)
     params = pltpu.CompilerParams(vmem_limit_bytes=60 * 1024 * 1024)
     square = sds((feats, feats), bf16)
+    pack_rows = feats + IDS
 
     xs = lax.all_to_all(x.reshape(sections, share, feats), "pipe", 0, 0, tiled=True)
 
-    packed, w1d, w2d, pick1, pick2 = pl.pallas_call(
+    packed1, packed2, w1d, w2d, pick1, pick2 = pl.pallas_call(
         prep_kernel,
         in_specs=[whole(pltpu.SMEM), whole(pltpu.SMEM), whole(), whole(), whole()],
-        out_specs=[whole()] * 5,
-        out_shape=[sds((2 * feats + IDS, LANES), bf16)] + [square] * 4,
+        out_specs=[whole()] * 6,
+        out_shape=[sds((pack_rows, LANES), bf16)] * 2 + [square] * 4,
         compiler_params=params,
         name="prep",
-    )(group.reshape(1), drop, perm.reshape(groups, feats), w_first[0, 0], w_second[0, 0])
-    packed = lax.all_gather(packed, "pipe")
+    )(group.reshape(1), drop, perm[0], w_first[0, 0], w_second[0, 0])
+    packed2 = lax.all_gather(packed2, "pipe")
+    packed1 = lax.all_gather(packed1, "pipe")
 
     payload = sds((groups, micros, 2, half, tokens), bf16)
     payload_spec = pl.BlockSpec((groups, 1, 2, half, tokens), lambda m: (0, m, 0, 0, 0))
@@ -236,32 +249,27 @@
         compiler_params=params,
         name="forward",
     )(x, w1d)
-    hidden, xs = lax.optimization_barrier((hidden, xs))
-    z = lax.all_to_all(hidden, "tensor", 0, 0, tiled=True)
-
     mixed_shape = sds((groups, half, 2 * share), bf16)
     value_shape = sds((share, feats), bf16)
-    stored_shape = sds((sections, share, feats), bf16)
-    pack_rows = 2 * feats + IDS
-    own_grad = lax.dynamic_index_in_dim(out_grad.reshape(sections, share, feats), row, 0, keepdims=False)
-    own_grad, z = lax.optimization_barrier((own_grad, z))
-    g = own_grad
-    stored, mixed = pl.pallas_call(
+    g = lax.dynamic_index_in_dim(out_grad.reshape(sections, share, feats), row, 0, keepdims=False)
+    mixed = pl.pallas_call(
         start_kernel,
         grid=(1,),
         in_specs=[
             pl.BlockSpec((share, feats), lambda i: (0, 0)),
             pl.BlockSpec((1, pack_rows, LANES), lambda i: (sections - 1, 0, 0)),
         ],
-        out_specs=[
-            pl.BlockSpec((1, share, feats), lambda i: (sections - 1, 0, 0)),
-            pl.BlockSpec((groups, half, 2 * share), lambda i: (0, 0, 0)),
-        ],
-        out_shape=[stored_shape, mixed_shape],
+        out_specs=pl.BlockSpec((groups, half, 2 * share), lambda i: (0, 0, 0)),
+        out_shape=mixed_shape,
         scratch_shapes=[pltpu.VMEM((feats, feats), bf16)],
         compiler_params=params,
         name="start",
-    )(g, packed)
+    )(g, packed2)
+    mixed, xs = lax.optimization_barrier((mixed, xs))
+    returned = lax.all_to_all(mixed, "tensor", 0, 0, tiled=True)
+    returned, hidden = lax.optimization_barrier((returned, hidden))
+    z = lax.all_to_all(hidden, "tensor", 0, 0, tiled=True)
+    returned, z = lax.optimization_barrier((returned, z))
 
     expand = pl.pallas_call(
         expand_kernel,
@@ -285,31 +293,38 @@
     )
     relay = pl.pallas_call(
         relay_kernel,
-        grid_spec=pltpu.PrefetchScalarGridSpec(
-            num_scalar_prefetch=1,
-            grid=(1,),
-            in_specs=[whole()] * 5 + [whole(pl.ANY)],
-            out_specs=[
-                pl.BlockSpec((1, share, feats), lambda i, s: (s[0] - 1, 0, 0)),
-                whole(),
-                whole(),
-            ],
-        ),
-        out_shape=[stored_shape, value_shape, mixed_shape],
-        input_output_aliases={6: 0},
-        compiler_params=params,
+        in_specs=[whole()] * 2 + [whole(pltpu.HBM)] * 3,
+        out_specs=[whole()] * 2,
+        out_shape=[value_shape, mixed_shape],
+        scratch_shapes=[
+            pltpu.VMEM((2 * share, feats // 2), f32),
+            pltpu.VMEM((feats, feats), bf16),
+            pltpu.VMEM((feats, feats), bf16),
+            pltpu.SemaphoreType.DMA((5,)),
+        ],
+        compiler_params=pltpu.CompilerParams(vmem_limit_bytes=60 * 1024 * 1024),
         name="relay",
     )
+
+    def prepare(s):
+        return expand(jnp.full((1,), s, i32), packed1, packed2, xs)
+
+    w1, w2, scale = prepare(sections - 1)
+    stored = jnp.zeros((sections, share, feats), bf16)
+    stored = lax.dynamic_update_index_in_dim(stored, g, sections - 1, 0)
+    g, mixed = relay(returned, g, scale, w1, w2)
 
     def advance(k, carry):
         g, mixed, stored = carry
-        at = jnp.full((1,), sections - 1 - k, i32)
+        s = sections - 2 - k
         returned = lax.all_to_all(mixed, "tensor", 0, 0, tiled=True)
-        w1, w2, scale = expand(at, packed, packed, xs)
-        stored, g, mixed = relay(at, returned, g, scale, w1, w2, stored)
+        stored = lax.dynamic_update_index_in_dim(stored, g, s, 0)
+        w1, w2, scale = prepare(s)
+        g, mixed = relay(returned, g, scale, w1, w2)
         return (g, mixed, stored)
 
-    _, _, stored = lax.fori_loop(0, sections - 1, advance, (g, mixed, stored))
+    g, _, stored = lax.fori_loop(0, sections - 2, advance, (g, mixed, stored))
+    stored = lax.dynamic_update_index_in_dim(stored, g, 0, 0)
     stored, z = lax.optimization_barrier((stored, z))
     cotangent = lax.all_to_all(stored, "pipe", 0, 0, tiled=True)
     cotangent = cotangent.reshape(micros, tokens, feats)
@@ -351,7 +366,7 @@
         compiler_params=params,
         name="owner",
     )(drop, returned, slope, pick1, w_first[0, 0], x_turned, z, cotangent)
-    return (grads[None], first[None, None], second[None, None])
+    return (grads.reshape(section_inputs.shape), first[None, None], second[None, None])
 
 
 def solution(mesh):

time: 458 us -> 462 us (level)
  waiting for transfers between devices: 120 us -> 129 us
  Pallas kernels: 154 us -> 148 us
    all_gather x1 -> x2, waiting for transfers between devices: 0.01 us -> 74.9 us  [the longest x1 57.4 us: on_device(): packed2 = lax.all_gather(packed2, 'pipe')]
    all_to_all x1, waiting for transfers between devices: 44 us -> 0.01 us  [on_device(): lax.all_to_all(x.reshape(sections, share, feats), 'pipe', 0, 0, tiled=True)]
    all_to_all x1, waiting for transfers between devices: 26 us -> 0.12 us  [on_device(): z = lax.all_to_all(hidden, 'tensor', 0, 0, tiled=True)]
    dynamic_update_slice x0 -> x16, local copies, waits for them, and re-layouts: none -> 11.1 us  [the longest x14 9.16 us: advance(): stored = lax.dynamic_update_index_in_dim(stored, g, s, 0)]
    while x45 -> x70, local copies, waits for them, and re-layouts: 18.9 us -> 9.14 us
    all_to_all x1 -> x2, starting transfers between devices: 3.73 us -> 10.4 us  [on_device(): returned = lax.all_to_all(mixed, 'tensor', 0, 0, tiled=True)]
    all_to_all x15 -> x14, starting transfers between devices: 67.7 us -> 62.5 us  [advance(): returned = lax.all_to_all(mixed, 'tensor', 0, 0, tiled=True)]
    pallas_call x30, Pallas kernels: 110 us -> 115 us  [the longest x14 56.8 us: advance(): g, mixed = relay(returned, g, scale, w1, w2)]
  transfers between devices with their start and end apart: 19 -> 20, of which waited for: 18 -> 19; matrix products, arithmetic and copies ran while one was open for 2% -> 2% of each run, Pallas kernels for 17% -> 15%
where the time goes in v4:
time: 462 us; the launch traced here: 459 us
  Pallas kernels  148 us (32%)
  waiting for transfers between devices  129 us (28%)
  starting transfers between devices  89.5 us (19%)
  blocking collectives  53.3 us (12%)
  local copies, waits for them, and re-layouts  22.8 us (5%)
  between operations  14.9 us (3%)
    all_to_all x14, starting transfers between devices, advance(): returned = lax.all_to_all(mixed, 'tensor', 0, 0, tiled=True)  62.5 us
    all_gather x1, waiting for transfers between devices, on_device(): packed2 = lax.all_gather(packed2, 'pipe')  57.4 us
    pallas_call x14, Pallas kernels, advance(): g, mixed = relay(returned, g, scale, w1, w2)  56.8 us
    pallas_call x15, Pallas kernels, prepare(): return expand(jnp.full((1,), s, i32), packed1, packed2, xs)  54.2 us
    all_to_all x1, blocking collectives, on_device(): cotangent = lax.all_to_all(stored, 'pipe', 0, 0, tiled=True)  53.3 us
    all_to_all x14, waiting for transfers between devices, advance(): returned = lax.all_to_all(mixed, 'tensor', 0, 0, tiled=True)  32.9 us
    all_to_all x2, waiting for transfers between devices, on_device(): returned = lax.all_to_all(mixed, 'tensor', 0, 0, tiled=True)  20.7 us
    all_gather x1, waiting for transfers between devices, on_device(): packed1 = lax.all_gather(packed1, 'pipe')  17.5 us
  transfers between devices with their start and end apart: 20, of which 19 were waited for; matrix products, arithmetic and copies ran while one was open for 2% of the time, Pallas kernels for 15%

profile of v4, /device:TPU:1, one launch (start us, length us, event | category | flops | bytes accessed | tf_op | source)
XLA Modules:
  0.0 458.9 jit_solution(5779384467583037604)
XLA Ops:
  8.0 5.3 %prep.1 = (bf16[832,128]{1,0:T(8,128)(2,1)}, bf16[832,128]{1,0:T(8,128)(2,1)}, bf16[768,768]{1,0:T(8,128)(2,1)}, bf16[768,768]{1,0:T(8,128)(2,1)}, bf16[768,768]{1,0:T(8,128)(2,1)}, /*index=5*/bf16[768,768]{1,0:T(8,128)(2,1)}) custom-call(s32[1]{0:T(128)} %bitcast.5.group_ref, s32[1]{0:T(128)} %bitcast.25.drop_ref, s32[1,12288]{1,0:T(1,128)} %bitcast.42, ...), custom_call_target="tpu_custom_call" | custom-call | tf_op jit(solution)/shard_map/prep/pallas_call | solution.py:225
  14.1 10.0 %all-to-all-start.1 = ((bf16[16,64,768]{2,1,0:T(8,128)(2,1)}), bf16[16,64,768]{2,1,0:T(8,128)(2,1)S(1)}, u32[]{:S(2)}, u32[]{:S(2)}) async-start(bf16[16,64,768]{2,1,0:T(8,128)(2,1)} %bitcast.34), calls=%async_computation.1 | async-start | bytes 3145728 | tf_op jit(solution)/shard_map/all_to_all | solution.py:223
  24.7 57.4 %all-gather.5.cloned.1.call-done = bf16[13312,128]{1,0:T(8,128)(2,1)} async-done(((bf16[832,128]{1,0:T(8,128)(2,1)}), bf16[13312,128]{1,0:T(8,128)(2,1)}) %all-gather.5.cloned.1.call-update) | async-done | bytes 3407888 | tf_op jit(solution)/shard_map/all_gather | solution.py:233
  84.9 6.7 %all-to-all-start.2 = ((bf16[16,24,128]{2,1,0:T(8,128)(2,1)}), bf16[16,24,128]{2,1,0:T(8,128)(2,1)S(1)}, u32[]{:S(2)}, u32[]{:S(2)}) async-start(bf16[16,24,128]{2,1,0:T(8,128)(2,1)} %start.1), calls=%async_computation.2 | async-start | bytes 196608 | tf_op jit(solution)/shard_map/all_to_all | solution.py:269
  91.6 6.5 %forward.1 = (bf16[16,4,2,24,256]{4,3,2,1,0:T(8,128)(2,1)}, f32[4,768,256]{2,1,0:T(8,128)}) custom-call(bf16[4,256,768]{2,1,0:T(8,128)(2,1)} %bitcast.35, bf16[768,768]{1,0:T(8,128)(2,1)} %get-tuple-element.214.w1d_ref), custom_call_target="tpu_custom_call" | custom-call | tf_op jit(solution)/shard_map/forward/pallas_call | solution.py:243
  98.9 6.5 %all-to-all-start.3 = ((bf16[16,4,2,24,256]{4,3,2,1,0:T(8,128)(2,1)}), bf16[16,4,2,24,256]{4,3,2,1,0:T(8,128)(2,1)}, u32[]{:S(2)}, u32[]{:S(2)}) async-start(bf16[16,4,2,24,256]{4,3,2,1,0:T(8,128)(2,1)} %get-tuple-element.217), calls=%async_computation.3 | async-start | bytes 3145728 | tf_op jit(solution)/shard_map/all_to_all | solution.py:271
  106.7 17.5 %all-gather.7.cloned.1.call-done = bf16[13312,128]{1,0:T(8,128)(2,1)} async-done(((bf16[832,128]{1,0:T(8,128)(2,1)}), bf16[13312,128]{1,0:T(8,128)(2,1)}) %all-gather.7.cloned.1.call-update) | async-done | bytes 3407888 | tf_op jit(solution)/shard_map/all_gather | solution.py:234
  128.0 4.1 relay.9
  132.0 222.0 %while.19 = (s32[]{:T(128)}, bf16[64,768]{1,0:T(8,128)(2,1)S(1)}, bf16[16,24,128]{2,1,0:T(8,128)(2,1)}, bf16[16,64,768]{2,1,0:T(8,128)(2,1)}, bf16[16,832,128]{2...) while((s32[]{:T(128)}, bf16[64,768]{1,0:T(8,128)(2,1)S(1)}, ...), condition=%wide.region_1.2_spmd, body=%wide.region_0.1_spmd.sunk | while | flops 6 | bytes 1474807 | solution.py:326
  132.1 6.5 %all-to-all-start = ((bf16[16,24,128]{2,1,0:T(8,128)(2,1)}), bf16[16,24,128]{2,1,0:T(8,128)(2,1)S(1)}, u32[]{:S(2)}, u32[]{:S(2)}) async-start(bf16[16,24,128]{2,1,0:T(8,128)(2,1)} %get-tuple-element.320), calls=%async_computation | async-start | bytes 196608 | tf_op jit(solution)/shard_map/while/body/eval_jaxpr/all_to_all | solution.py:320
  145.8 4.1 relay.10
  149.9 4.3 all-to-all-start
  161.5 4.1 relay.10
  165.6 4.3 all-to-all-start
  177.2 4.1 relay.10
  181.3 4.3 all-to-all-start
  192.9 4.1 relay.10
  197.0 4.3 all-to-all-start
  212.7 4.3 all-to-all-start
  228.4 4.3 all-to-all-start
  244.1 4.3 all-to-all-start
  259.8 4.3 all-to-all-start
  275.5 4.3 all-to-all-start
  291.2 4.3 all-to-all-start
  307.0 4.3 all-to-all-start
  322.7 4.3 all-to-all-start
  338.4 4.3 all-to-all-start
  354.7 53.3 %all_to_all.31 = bf16[16,64,768]{2,1,0:T(8,128)(2,1)} all-to-all(bf16[16,64,768]{2,1,0:T(8,128)(2,1)} %bitcast_dynamic-update-slice_fusion.1), channel_id=1, replica_groups=mesh['pipe'=16,'tensor'=16] {'pipe'}, dimensions={0} | all-to-all | bytes 3145728 | tf_op jit(solution)/shard_map/all_to_all | solution.py:329
  408.1 4.9 %owner_send.1 = bf16[16,4,2,24,256]{4,3,2,1,0:T(8,128)(2,1)} custom-call(bf16[4,256,768]{2,1,0:T(8,128)(2,1)} %bitcast.37, bf16[768,768]{1,0:T(8,128)(2,1)} %get-tuple-element.230.w2d_ref), custom_call_target="tpu_custom_call" | custom-call | tf_op jit(solution)/shard_map/owner_send/pallas_call | solution.py:341
  416.7 5.3 %settle.1 = (bf16[4,768,256]{2,1,0:T(8,128)(2,1)}, bf16[4,768,256]{2,1,0:T(8,128)(2,1)}) custom-call(bf16[16,4,2,24,256]{4,3,2,1,0:T(8,128)(2,1)} %all-to-all-done.3.z_ref, bf16[4,256,768]{2,1,0:T(8,128)(2,1)} %bitcast.36, bf16[768,768]{1,0:T(8,128)(2,1)} %get-tuple-element.234.pick2_ref), custom_call_target="tpu_custom_call" | custom-call | tf_op jit(solution)/shard_map/settle/pallas_call | solution.py:331
  422.0 20.5 %all-to-all-done.5.returned_ref = bf16[16,4,2,24,256]{4,3,2,1,0:T(8,128)(2,1)S(1)} async-done(((bf16[16,4,2,24,256]{4,3,2,1,0:T(8,128)(2,1)}), bf16[16,4,2,24,256]{4,3,2,1,0:T(8,128)(2,1)S(1)}, u32[]{:S(2)}, u32[]{:S(2)}) %all-to-all-start.5) | async-done | bytes 1572896 | tf_op jit(solution)/shard_map/all_to_all | solution.py:350
  443.6 8.4 %owner.1 = (bf16[4,256,768]{2,1,0:T(8,128)(2,1)}, f32[6,128,128]{2,1,0:T(8,128)}, f32[6,128,128]{2,1,0:T(8,128)}) custom-call(s32[1]{0:T(128)} %bitcast.26.drop_ref, bf16[16,4,2,24,256]{4,3,2,1,0:T(8,128)(2,1)} %copy-done.3, f32[4,768,256]{2,1,0:T(8,128)} %get-tuple-element.231.slope_ref, bf16[768,768]{1,0:T(8,128)(2,1)} %get-tuple-element.232.pick1_ref, ...), custom_call_target="tpu_custom_call" | custom-call | tf_op jit(solution)/shard_map/owner/pallas_call | solution.py:351
  (142 shorter events, 158.0 us)
Async XLA Ops:
  7.2 16.9 %copy-start = (bf16[8,128,768]{2,1,0:T(8,128)(2,1)S(1)}, bf16[8,128,768]{2,1,0:T(8,128)(2,1)}, u32[]{:S(2)}) copy-start(bf16[8,128,768]{2,1,0:T(8,128)(2,1)} %param.9) | copy-start | bytes 4718596
  7.2 74.9 %all-gather.5.cloned.1.call-start = ((), (), s32[]{:S(2)}) async-start(), calls=%async_computation.6 | async-start | bytes 3620864 | tf_op jit(solution)/shard_map/all_gather | solution.py:233
  13.3 110.9 %all-gather.7.cloned.1.call-start = ((), (), s32[]{:S(2)}) async-start(), calls=%async_computation.7 | async-start | bytes 3620864 | tf_op jit(solution)/shard_map/all_gather | solution.py:234
  14.1 70.8 %all-to-all-start.1 = ((bf16[16,64,768]{2,1,0:T(8,128)(2,1)}), bf16[16,64,768]{2,1,0:T(8,128)(2,1)S(1)}, u32[]{:S(2)}, u32[]{:S(2)}) async-start(bf16[16,64,768]{2,1,0:T(8,128)(2,1)} %bitcast.34), calls=%async_computation.1 | async-start | bytes 3145728 | tf_op jit(solution)/shard_map/all_to_all | solution.py:223
  84.9 13.4 %all-to-all-start.2 = ((bf16[16,24,128]{2,1,0:T(8,128)(2,1)}), bf16[16,24,128]{2,1,0:T(8,128)(2,1)S(1)}, u32[]{:S(2)}, u32[]{:S(2)}) async-start(bf16[16,24,128]{2,1,0:T(8,128)(2,1)} %start.1), calls=%async_computation.2 | async-start | bytes 196608 | tf_op jit(solution)/shard_map/all_to_all | solution.py:269
  98.9 29.1 %all-to-all-start.3 = ((bf16[16,4,2,24,256]{4,3,2,1,0:T(8,128)(2,1)}), bf16[16,4,2,24,256]{4,3,2,1,0:T(8,128)(2,1)}, u32[]{:S(2)}, u32[]{:S(2)}) async-start(bf16[16,4,2,24,256]{4,3,2,1,0:T(8,128)(2,1)} %get-tuple-element.217), calls=%async_computation.3 | async-start | bytes 3145728 | tf_op jit(solution)/shard_map/all_to_all | solution.py:271
  132.1 13.1 %all-to-all-start = ((bf16[16,24,128]{2,1,0:T(8,128)(2,1)}), bf16[16,24,128]{2,1,0:T(8,128)(2,1)S(1)}, u32[]{:S(2)}, u32[]{:S(2)}) async-start(bf16[16,24,128]{2,1,0:T(8,128)(2,1)} %get-tuple-element.320), calls=%async_computation | async-start | bytes 196608 | tf_op jit(solution)/shard_map/while/body/eval_jaxpr/all_to_all | solution.py:320
  149.9 11.0 %all-to-all-start = ((bf16[16,24,128]{2,1,0:T(8,128)(2,1)}), bf16[16,24,128]{2,1,0:T(8,128)(2,1)S(1)}, u32[]{:S(2)}, u32[]{:S(2)}) async-start(bf16[16,24,128]{2,1,0:T(8,128)(2,1)} %get-tuple-element.320), calls=%async_computation | async-start | bytes 196608 | tf_op jit(solution)/shard_map/while/body/eval_jaxpr/all_to_all | solution.py:320
  154.2 4.3 copy-start.1
  165.6 11.0 %all-to-all-start = ((bf16[16,24,128]{2,1,0:T(8,128)(2,1)}), bf16[16,24,128]{2,1,0:T(8,128)(2,1)S(1)}, u32[]{:S(2)}, u32[]{:S(2)}) async-start(bf16[16,24,128]{2,1,0:T(8,128)(2,1)} %get-tuple-element.320), calls=%async_computation | async-start | bytes 196608 | tf_op jit(solution)/shard_map/while/body/eval_jaxpr/all_to_all | solution.py:320
  169.9 4.3 copy-start.1
  181.3 11.0 %all-to-all-start = ((bf16[16,24,128]{2,1,0:T(8,128)(2,1)}), bf16[16,24,128]{2,1,0:T(8,128)(2,1)S(1)}, u32[]{:S(2)}, u32[]{:S(2)}) async-start(bf16[16,24,128]{2,1,0:T(8,128)(2,1)} %get-tuple-element.320), calls=%async_computation | async-start | bytes 196608 | tf_op jit(solution)/shard_map/while/body/eval_jaxpr/all_to_all | solution.py:320
  185.7 4.3 copy-start.1
  197.0 11.0 %all-to-all-start = ((bf16[16,24,128]{2,1,0:T(8,128)(2,1)}), bf16[16,24,128]{2,1,0:T(8,128)(2,1)S(1)}, u32[]{:S(2)}, u32[]{:S(2)}) async-start(bf16[16,24,128]{2,1,0:T(8,128)(2,1)} %get-tuple-element.320), calls=%async_computation | async-start | bytes 196608 | tf_op jit(solution)/shard_map/while/body/eval_jaxpr/all_to_all | solution.py:320
  201.4 4.3 copy-start.1
  212.7 11.0 %all-to-all-start = ((bf16[16,24,128]{2,1,0:T(8,128)(2,1)}), bf16[16,24,128]{2,1,0:T(8,128)(2,1)S(1)}, u32[]{:S(2)}, u32[]{:S(2)}) async-start(bf16[16,24,128]{2,1,0:T(8,128)(2,1)} %get-tuple-element.320), calls=%async_computation | async-start | bytes 196608 | tf_op jit(solution)/shard_map/while/body/eval_jaxpr/all_to_all | solution.py:320
  217.1 4.3 copy-start.1
  228.4 11.0 %all-to-all-start = ((bf16[16,24,128]{2,1,0:T(8,128)(2,1)}), bf16[16,24,128]{2,1,0:T(8,128)(2,1)S(1)}, u32[]{:S(2)}, u32[]{:S(2)}) async-start(bf16[16,24,128]{2,1,0:T(8,128)(2,1)} %get-tuple-element.320), calls=%async_computation | async-start | bytes 196608 | tf_op jit(solution)/shard_map/while/body/eval_jaxpr/all_to_all | solution.py:320
  232.8 4.3 copy-start.1
  244.1 11.0 %all-to-all-start = ((bf16[16,24,128]{2,1,0:T(8,128)(2,1)}), bf16[16,24,128]{2,1,0:T(8,128)(2,1)S(1)}, u32[]{:S(2)}, u32[]{:S(2)}) async-start(bf16[16,24,128]{2,1,0:T(8,128)(2,1)} %get-tuple-element.320), calls=%async_computation | async-start | bytes 196608 | tf_op jit(solution)/shard_map/while/body/eval_jaxpr/all_to_all | solution.py:320
  248.5 4.3 copy-start.1
  259.8 11.0 %all-to-all-start = ((bf16[16,24,128]{2,1,0:T(8,128)(2,1)}), bf16[16,24,128]{2,1,0:T(8,128)(2,1)S(1)}, u32[]{:S(2)}, u32[]{:S(2)}) async-start(bf16[16,24,128]{2,1,0:T(8,128)(2,1)} %get-tuple-element.320), calls=%async_computation | async-start | bytes 196608 | tf_op jit(solution)/shard_map/while/body/eval_jaxpr/all_to_all | solution.py:320
  264.2 4.3 copy-start.1
  275.5 11.0 %all-to-all-start = ((bf16[16,24,128]{2,1,0:T(8,128)(2,1)}), bf16[16,24,128]{2,1,0:T(8,128)(2,1)S(1)}, u32[]{:S(2)}, u32[]{:S(2)}) async-start(bf16[16,24,128]{2,1,0:T(8,128)(2,1)} %get-tuple-element.320), calls=%async_computation | async-start | bytes 196608 | tf_op jit(solution)/shard_map/while/body/eval_jaxpr/all_to_all | solution.py:320
  279.9 4.3 copy-start.1
  291.2 11.0 %all-to-all-start = ((bf16[16,24,128]{2,1,0:T(8,128)(2,1)}), bf16[16,24,128]{2,1,0:T(8,128)(2,1)S(1)}, u32[]{:S(2)}, u32[]{:S(2)}) async-start(bf16[16,24,128]{2,1,0:T(8,128)(2,1)} %get-tuple-element.320), calls=%async_computation | async-start | bytes 196608 | tf_op jit(solution)/shard_map/while/body/eval_jaxpr/all_to_all | solution.py:320
  295.6 4.3 copy-start.1
  307.0 11.0 %all-to-all-start = ((bf16[16,24,128]{2,1,0:T(8,128)(2,1)}), bf16[16,24,128]{2,1,0:T(8,128)(2,1)S(1)}, u32[]{:S(2)}, u32[]{:S(2)}) async-start(bf16[16,24,128]{2,1,0:T(8,128)(2,1)} %get-tuple-element.320), calls=%async_computation | async-start | bytes 196608 | tf_op jit(solution)/shard_map/while/body/eval_jaxpr/all_to_all | solution.py:320
  311.3 4.3 copy-start.1
  322.7 11.0 %all-to-all-start = ((bf16[16,24,128]{2,1,0:T(8,128)(2,1)}), bf16[16,24,128]{2,1,0:T(8,128)(2,1)S(1)}, u32[]{:S(2)}, u32[]{:S(2)}) async-start(bf16[16,24,128]{2,1,0:T(8,128)(2,1)} %get-tuple-element.320), calls=%async_computation | async-start | bytes 196608 | tf_op jit(solution)/shard_map/while/body/eval_jaxpr/all_to_all | solution.py:320
  338.4 11.0 %all-to-all-start = ((bf16[16,24,128]{2,1,0:T(8,128)(2,1)}), bf16[16,24,128]{2,1,0:T(8,128)(2,1)S(1)}, u32[]{:S(2)}, u32[]{:S(2)}) async-start(bf16[16,24,128]{2,1,0:T(8,128)(2,1)} %get-tuple-element.320), calls=%async_computation | async-start | bytes 196608 | tf_op jit(solution)/shard_map/while/body/eval_jaxpr/all_to_all | solution.py:320
  413.0 29.4 %all-to-all-start.5 = ((bf16[16,4,2,24,256]{4,3,2,1,0:T(8,128)(2,1)}), bf16[16,4,2,24,256]{4,3,2,1,0:T(8,128)(2,1)S(1)}, u32[]{:S(2)}, u32[]{:S(2)}) async-start(bf16[16,4,2,24,256]{4,3,2,1,0:T(8,128)(2,1)} %owner_send.1), calls=%async_computation.5 | async-start | bytes 3145728 | tf_op jit(solution)/shard_map/all_to_all | solution.py:350
  (19 other events, 23.7 us)
Sparse Core Ops, SparseCore 0:
  13.4 68.6 all-gather.4
  84.5 39.6 all-gather.6

commit v5 on v4

--- a/solution.py
+++ b/solution.py
@@ -15,7 +15,9 @@
 NN = ((1,), (0,))
 NT = ((1,), (1,))
 LANES = 128
-IDS = 64
+IDS = 16
+RELAY_MIB = 16
+EXPAND_MIB = 16
 
 
 def dot(left, right, dims):
@@ -33,7 +35,7 @@
     return value, slope
 
 
-def prep_kernel(group_ref, drop_ref, perm_ref, w1_ref, w2_ref, packed1_ref, packed2_ref, w1d_ref, w2d_ref, pick1_ref, pick2_ref):
+def prep_kernel(group_ref, drop_ref, perm_ref, w1_ref, w2_ref, packed_ref, w1d_ref, w2d_ref, pick1_ref, pick2_ref):
     feats = pick1_ref.shape[0]
     groups = perm_ref.shape[1] // feats
     blocks, size, _ = w1_ref.shape
@@ -68,28 +70,24 @@
     slot = jnp.sum(marks * place, axis=0, keepdims=True).astype(i32)
     arrive = jnp.where(rows == slot, 1.0, 0.0)
     pick1_ref[...] = leave
-    pick2_ref[...] = jnp.transpose(arrive).astype(bf16)
+    arrive_t = jnp.transpose(arrive).astype(bf16)
+    pick2_ref[...] = arrive_t
     arrive = arrive.astype(bf16)
-    part1 = jnp.zeros((feats, size), f32)
-    part2 = jnp.zeros((feats, size), f32)
+    part1 = jnp.zeros((size, feats), f32)
+    part2 = jnp.zeros((size, feats), f32)
     for block in range(blocks):
         span = slice(block * size, (block + 1) * size)
-        one = dot(leave[:, span], w1_ref[block], NT)
-        two = keep * dot(arrive[:, span], w2_ref[block], NN)
-        w1d_ref[:, span] = one.astype(bf16)
-        w2d_ref[:, span] = two.astype(bf16)
-        part1 += one
-        part2 += two
-    packed1_ref[0:feats, :] = part1.astype(bf16)
-    packed2_ref[0:feats, :] = part2.astype(bf16)
-    line = lax.broadcasted_iota(i32, (8, feats), 0)
-    owner = (lax.broadcasted_iota(i32, (8, feats), 1) // size).astype(f32)
-    owner = jnp.where(line == 0, owner, 0.0).astype(bf16)
-    for ref, chosen in ((packed1_ref, leave), (packed2_ref, arrive)):
-        ids = dot(owner, chosen, NT)
-        pieces = [ids[:, b * LANES : (b + 1) * LANES] for b in range(feats // LANES)]
-        pieces.append(jnp.zeros((IDS - 8 * len(pieces), LANES), f32))
-        ref[feats:, :] = jnp.concatenate(pieces, axis=0).astype(bf16)
+        w1d_ref[:, span] = dot(leave[:, span], w1_ref[block], NT).astype(bf16)
+        w2d_ref[:, span] = (keep * dot(arrive[:, span], w2_ref[block], NN)).astype(bf16)
+        part1 += dot(w1_ref[block], leave[:, span], NT)
+        part2 += keep * dot(jnp.transpose(w2_ref[block].astype(f32)).astype(bf16), arrive_t[span, :], NN)
+    packed_ref[0:size, :] = part1.astype(bf16)
+    packed_ref[size : 2 * size, :] = part2.astype(bf16)
+    line = lax.broadcasted_iota(i32, (IDS, feats), 0)
+    owner = (lax.broadcasted_iota(i32, (IDS, feats), 1) // size).astype(f32)
+    ids = dot(jnp.where(line == 0, owner, 0.0).astype(bf16), leave, NT)
+    ids += dot(jnp.where(line == 1, owner, 0.0).astype(bf16), arrive, NT)
+    packed_ref[2 * size :, :] = ids.astype(bf16)
 
 
 def to_payload(values, ref):
@@ -117,67 +115,47 @@
     x_out[0] = jnp.transpose(x_ref[0].astype(f32)).astype(bf16)
 
 
-def spread(packed_ref, dense_ref):
-    feats = dense_ref.shape[0]
-    blocks = feats // LANES
-    ids = packed_ref[0, feats:, :].astype(f32)
-    own = jnp.transpose(jnp.concatenate([ids[8 * b : 8 * b + 8] for b in range(blocks)], axis=1))[:, 0:1]
-    values = packed_ref[0, 0:feats, :].astype(f32)
-    for b in range(blocks):
-        dense_ref[:, b * LANES : (b + 1) * LANES] = jnp.where(own == b, values, 0.0).astype(bf16)
+def spread(values, ids, dense_ref):
+    size = values.shape[0]
+    for b in range(dense_ref.shape[0] // size):
+        dense_ref[b * size : (b + 1) * size, :] = jnp.where(ids == b, values, 0.0).astype(bf16)
 
 
 def expand_kernel(step_ref, first_ref, second_ref, x_ref, w1_ref, w2_ref, slope_ref):
     del step_ref
     feats = x_ref.shape[2]
-    spread(first_ref, w1_ref)
-    spread(second_ref, w2_ref)
-    v = dot(x_ref[0], w1_ref[...], NT)
+    first = first_ref[0].astype(f32)
+    spread(first[:LANES], first[2 * LANES : 2 * LANES + 1], w1_ref)
+    w2_ref[...] = second_ref[0, LANES:, :]
+    v = dot(x_ref[0], w1_ref[...], NN)
     _, slope = gelu_pair(jnp.concatenate([v[:, : feats // 2], v[:, feats // 2 :]], axis=0))
     slope_ref[...] = slope
 
 
-def mix(g, w2_ref, mixed_ref, ready=(None, None)):
+def mix(g, w2_ref, mixed_ref):
     feats = g.shape[1]
-    pieces = []
-    for part, wait in enumerate(ready):
-        if wait is not None:
-            wait.wait()
-        pieces.append(dot(g, w2_ref[part * (feats // 2) : (part + 1) * (feats // 2), :], NT))
-    s = jnp.concatenate(pieces, axis=0)
+    s = dot(g, w2_ref[...], NN)
+    s = jnp.concatenate([s[:, : feats // 2], s[:, feats // 2 :]], axis=0)
     mixed_ref[...] = jnp.transpose(s).reshape(mixed_ref.shape).astype(bf16)
 
 
 def start_kernel(g_ref, packed_ref, mixed_ref, w2_ref):
-    spread(packed_ref, w2_ref)
+    packed = packed_ref[0].astype(f32)
+    spread(packed[LANES : 2 * LANES], packed[2 * LANES + 1 : 2 * LANES + 2], w2_ref)
     mix(g_ref[...], w2_ref, mixed_ref)
 
 
-def relay_kernel(returned_ref, g_in_ref, slope_hbm, w1_hbm, w2_hbm, g_ref, mixed_ref, slope_ref, w1_ref, w2_ref, sems):
+def relay_kernel(returned_ref, g_in_ref, slope_ref, w1_ref, packed_ref, g_ref, mixed_ref, w2_ref):
+    packed = packed_ref[...].astype(f32)
+    spread(packed[:LANES], packed[LANES + 1 : LANES + 2], w2_ref)
     groups, half, lanes = returned_ref.shape
     tokens = lanes // 2
-    split = groups * half
-    upper, lower = pl.ds(0, split), pl.ds(split, split)
-    slope_copy = pltpu.make_async_copy(slope_hbm, slope_ref, sems.at[0])
-    copies = [
-        pltpu.make_async_copy(source.at[span], target.at[span], sems.at[1 + index])
-        for index, (source, target, span) in enumerate(
-            [(w1_hbm, w1_ref, upper), (w1_hbm, w1_ref, lower), (w2_hbm, w2_ref, upper), (w2_hbm, w2_ref, lower)]
-        )
-    ]
-    slope_copy.start()
-    for copy in copies:
-        copy.start()
-    dh = jnp.transpose(returned_ref[...].astype(f32).reshape(split, lanes))
-    slope_copy.wait()
-    da = (dh * slope_ref[...]).astype(bf16)
-    copies[0].wait()
-    term = dot(da[:tokens], w1_ref[:split], NN)
-    copies[1].wait()
-    term = term + dot(da[tokens:], w1_ref[split:], NN)
-    g = (g_in_ref[...].astype(f32) + term).astype(bf16)
+    dh = returned_ref[...].astype(f32).reshape(groups * half, lanes)
+    da = (jnp.transpose(dh) * slope_ref[...]).astype(bf16)
+    da = jnp.concatenate([da[:tokens], da[tokens:]], axis=1)
+    g = (g_in_ref[...].astype(f32) + dot(da, w1_ref[...], NT)).astype(bf16)
     g_ref[...] = g
-    mix(g, w2_ref, mixed_ref, copies[2:])
+    mix(g, w2_ref, mixed_ref)
 
 
 def owner_send_kernel(g_ref, w2d_ref, mixed_ref):
@@ -218,20 +196,20 @@
     drop = drop_flags.reshape(1)
     params = pltpu.CompilerParams(vmem_limit_bytes=60 * 1024 * 1024)
     square = sds((feats, feats), bf16)
-    pack_rows = feats + IDS
+    pack_rows = 2 * LANES + IDS
 
     xs = lax.all_to_all(x.reshape(sections, share, feats), "pipe", 0, 0, tiled=True)
 
-    packed1, packed2, w1d, w2d, pick1, pick2 = pl.pallas_call(
+    packed, w1d, w2d, pick1, pick2 = pl.pallas_call(
         prep_kernel,
         in_specs=[whole(pltpu.SMEM), whole(pltpu.SMEM), whole(), whole(), whole()],
-        out_specs=[whole()] * 6,
-        out_shape=[sds((pack_rows, LANES), bf16)] * 2 + [square] * 4,
+        out_specs=[whole()] * 5,
+        out_shape=[sds((pack_rows, feats), bf16)] + [square] * 4,
         compiler_params=params,
         name="prep",
     )(group.reshape(1), drop, perm[0], w_first[0, 0], w_second[0, 0])
-    packed2 = lax.all_gather(packed2, "pipe")
-    packed1 = lax.all_gather(packed1, "pipe")
+    packed, xs = lax.optimization_barrier((packed, xs))
+    packed = lax.all_gather(packed, "pipe")
 
     payload = sds((groups, micros, 2, half, tokens), bf16)
     payload_spec = pl.BlockSpec((groups, 1, 2, half, tokens), lambda m: (0, m, 0, 0, 0))
@@ -257,19 +235,18 @@
         grid=(1,),
         in_specs=[
             pl.BlockSpec((share, feats), lambda i: (0, 0)),
-            pl.BlockSpec((1, pack_rows, LANES), lambda i: (sections - 1, 0, 0)),
+            pl.BlockSpec((1, pack_rows, feats), lambda i: (sections - 1, 0, 0)),
         ],
         out_specs=pl.BlockSpec((groups, half, 2 * share), lambda i: (0, 0, 0)),
         out_shape=mixed_shape,
         scratch_shapes=[pltpu.VMEM((feats, feats), bf16)],
         compiler_params=params,
         name="start",
-    )(g, packed2)
-    mixed, xs = lax.optimization_barrier((mixed, xs))
+    )(g, packed)
+    hidden, xs = lax.optimization_barrier((hidden, xs))
+    z = lax.all_to_all(hidden, "tensor", 0, 0, tiled=True)
+    mixed, z = lax.optimization_barrier((mixed, z))
     returned = lax.all_to_all(mixed, "tensor", 0, 0, tiled=True)
-    returned, hidden = lax.optimization_barrier((returned, hidden))
-    z = lax.all_to_all(hidden, "tensor", 0, 0, tiled=True)
-    returned, z = lax.optimization_barrier((returned, z))
 
     expand = pl.pallas_call(
         expand_kernel,
@@ -277,37 +254,28 @@
             num_scalar_prefetch=1,
             grid=(1,),
             in_specs=[
-                pl.BlockSpec((1, pack_rows, LANES), lambda i, s: (s[0], 0, 0)),
-                pl.BlockSpec((1, pack_rows, LANES), lambda i, s: (s[0] - 1, 0, 0)),
+                pl.BlockSpec((1, pack_rows, feats), lambda i, s: (s[0], 0, 0)),
+                pl.BlockSpec((1, pack_rows, feats), lambda i, s: (s[0] - 1, 0, 0)),
                 pl.BlockSpec((1, share, feats), lambda i, s: (s[0], 0, 0)),
             ],
-            out_specs=[
-                pl.BlockSpec((feats, feats), lambda i, s: (0, 0)),
-                pl.BlockSpec((feats, feats), lambda i, s: (0, 0)),
-                pl.BlockSpec((2 * share, feats // 2), lambda i, s: (0, 0)),
-            ],
+            out_specs=[whole()] * 3,
         ),
-        out_shape=[square, square, sds((2 * share, feats // 2), f32)],
-        compiler_params=params,
+        out_shape=[square, sds((pack_rows - LANES, feats), bf16), sds((2 * share, feats // 2), f32)],
+        compiler_params=pltpu.CompilerParams(vmem_limit_bytes=EXPAND_MIB * 1024 * 1024),
         name="expand",
     )
     relay = pl.pallas_call(
         relay_kernel,
-        in_specs=[whole()] * 2 + [whole(pltpu.HBM)] * 3,
+        in_specs=[whole()] * 5,
         out_specs=[whole()] * 2,
         out_shape=[value_shape, mixed_shape],
-        scratch_shapes=[
-            pltpu.VMEM((2 * share, feats // 2), f32),
-            pltpu.VMEM((feats, feats), bf16),
-            pltpu.VMEM((feats, feats), bf16),
-            pltpu.SemaphoreType.DMA((5,)),
-        ],
-        compiler_params=pltpu.CompilerParams(vmem_limit_bytes=60 * 1024 * 1024),
+        scratch_shapes=[pltpu.VMEM((feats, feats), bf16)],
+        compiler_params=pltpu.CompilerParams(vmem_limit_bytes=RELAY_MIB * 1024 * 1024),
         name="relay",
     )
 
     def prepare(s):
-        return expand(jnp.full((1,), s, i32), packed1, packed2, xs)
+        return expand(jnp.full((1,), s, i32), packed, packed, xs)
 
     w1, w2, scale = prepare(sections - 1)
     stored = jnp.zeros((sections, share, feats), bf16)

time: 462 us -> 398 us (0.86)
  Pallas kernels: 148 us -> 78.5 us
  waiting for transfers between devices: 129 us -> 150 us
  starting transfers between devices: 89.5 us -> 76.2 us
  blocking collectives: 53.3 us -> 61.9 us
  local copies, waits for them, and re-layouts: 22.8 us -> 14.3 us
    all_gather x2 -> x1, waiting for transfers between devices: 74.9 us -> 31.9 us  [on_device(): packed = lax.all_gather(packed, 'pipe')]
    pallas_call x14, Pallas kernels: 56.8 us -> 20.6 us  [advance(): g, mixed = relay(returned, g, scale, w1, w2)]
    all_to_all x1, waiting for transfers between devices: 0.01 us -> 32.7 us  [on_device(): lax.all_to_all(x.reshape(sections, share, feats), 'pipe', 0, 0, tiled=True)]
    pallas_call x15, Pallas kernels: 54.2 us -> 23.6 us  [prepare(): return expand(jnp.full((1,), s, i32), packed, packed, xs)]
    all_to_all x14, waiting for transfers between devices: 32.9 us -> 61.6 us  [advance(): returned = lax.all_to_all(mixed, 'tensor', 0, 0, tiled=True)]
    all_to_all x14, starting transfers between devices: 62.5 us -> 49.1 us  [advance(): returned = lax.all_to_all(mixed, 'tensor', 0, 0, tiled=True)]
    while x70 -> x14, local copies, waits for them, and re-layouts: 9.14 us -> 0.12 us
    all_to_all x1, blocking collectives: 53.3 us -> 61.9 us  [on_device(): cotangent = lax.all_to_all(stored, 'pipe', 0, 0, tiled=True)]
  transfers between devices with their start and end apart: 20 -> 19, of which waited for: 19 -> 18; matrix products, arithmetic and copies ran while one was open for 2% -> 3% of each run, Pallas kernels for 15% -> 11%
where the time goes in v5:
time: 398 us; the launch traced here: 396 us
  waiting for transfers between devices  150 us (38%)
  Pallas kernels  78.5 us (20%)
  starting transfers between devices  76.2 us (19%)
  blocking collectives  61.9 us (16%)
  between operations  14.7 us (4%)
  local copies, waits for them, and re-layouts  14.3 us (4%)
    all_to_all x1, blocking collectives, on_device(): cotangent = lax.all_to_all(stored, 'pipe', 0, 0, tiled=True)  61.9 us
    all_to_all x14, waiting for transfers between devices, advance(): returned = lax.all_to_all(mixed, 'tensor', 0, 0, tiled=True)  61.6 us
    all_to_all x14, starting transfers between devices, advance(): returned = lax.all_to_all(mixed, 'tensor', 0, 0, tiled=True)  49.1 us
    all_to_all x1, waiting for transfers between devices, on_device(): lax.all_to_all(x.reshape(sections, share, feats), 'pipe', 0, 0, tiled=True)  32.7 us
    all_gather x1, waiting for transfers between devices, on_device(): packed = lax.all_gather(packed, 'pipe')  31.9 us
    all_to_all x2, waiting for transfers between devices, on_device(): returned = lax.all_to_all(mixed, 'tensor', 0, 0, tiled=True)  23.8 us
    pallas_call x15, Pallas kernels, prepare(): return expand(jnp.full((1,), s, i32), packed, packed, xs)  23.6 us
    pallas_call x14, Pallas kernels, advance(): g, mixed = relay(returned, g, scale, w1, w2)  20.6 us
  transfers between devices with their start and end apart: 19, of which 18 were waited for; matrix products, arithmetic and copies ran while one was open for 3% of the time, Pallas kernels for 11%

profile of v5, /device:TPU:1, one launch (start us, length us, event | category | flops | bytes accessed | tf_op | source)
XLA Modules:
  0.0 396.2 jit_solution(2536151160726650900)
XLA Ops:
  7.2 10.1 %all-to-all-start.1 = ((bf16[16,64,768]{2,1,0:T(8,128)(2,1)}), bf16[16,64,768]{2,1,0:T(8,128)(2,1)S(1)}, u32[]{:S(2)}, u32[]{:S(2)}) async-start(bf16[16,64,768]{2,1,0:T(8,128)(2,1)} %bitcast.32), calls=%async_computation.1 | async-start | bytes 3145728 | tf_op jit(solution)/shard_map/all_to_all | solution.py:201
  18.0 5.2 %prep.1 = (bf16[272,768]{1,0:T(8,128)(2,1)}, bf16[768,768]{1,0:T(8,128)(2,1)}, bf16[768,768]{1,0:T(8,128)(2,1)}, bf16[768,768]{1,0:T(8,128)(2,1)}, bf16[768,768]{1,0:T(8,128)(2,1)}) custom-call(s32[1]{0:T(128)} %bitcast.5.group_ref, s32[1]{0:T(128)} %bitcast.24.drop_ref, s32[1,12288]{1,0:T(1,128)} %bitcast.40, bf16[6,128,128]{2,1,0:T(8,128)(2,1)} %bitcast.37, ...), custom_call_target="tpu_custom_call" | custom-call | tf_op jit(solution)/shard_map/prep/pallas_call | solution.py:203
  23.1 32.7 %all-to-all-done.1.x_ref = bf16[16,64,768]{2,1,0:T(8,128)(2,1)S(1)} async-done(((bf16[16,64,768]{2,1,0:T(8,128)(2,1)}), bf16[16,64,768]{2,1,0:T(8,128)(2,1)S(1)}, u32[]{:S(2)}, u32[]{:S(2)}) %all-to-all-start.1) | async-done | bytes 1572896 | tf_op jit(solution)/shard_map/all_to_all | solution.py:201
  55.8 7.0 %forward.1 = (bf16[16,4,2,24,256]{4,3,2,1,0:T(8,128)(2,1)}, f32[4,768,256]{2,1,0:T(8,128)}) custom-call(bf16[4,256,768]{2,1,0:T(8,128)(2,1)} %bitcast.33, bf16[768,768]{1,0:T(8,128)(2,1)} %get-tuple-element.193.w1d_ref), custom_call_target="tpu_custom_call" | custom-call | tf_op jit(solution)/shard_map/forward/pallas_call | solution.py:221
  62.8 6.8 %all-to-all-start.2 = ((bf16[16,4,2,24,256]{4,3,2,1,0:T(8,128)(2,1)}), bf16[16,4,2,24,256]{4,3,2,1,0:T(8,128)(2,1)S(1)}, u32[]{:S(2)}, u32[]{:S(2)}) async-start(bf16[16,4,2,24,256]{4,3,2,1,0:T(8,128)(2,1)} %get-tuple-element.196), calls=%async_computation.2 | async-start | bytes 3145728 | tf_op jit(solution)/shard_map/all_to_all | solution.py:247
  70.2 31.9 %all-gather.3.cloned.1.call-done = bf16[4352,768]{1,0:T(8,128)(2,1)} async-done(((bf16[272,768]{1,0:T(8,128)(2,1)}), bf16[4352,768]{1,0:T(8,128)(2,1)}) %all-gather.3.cloned.1.call-update) | async-done | bytes 6684688 | tf_op jit(solution)/shard_map/all_gather | solution.py:212
  105.5 6.5 %all-to-all-start.3 = ((bf16[16,24,128]{2,1,0:T(8,128)(2,1)}), bf16[16,24,128]{2,1,0:T(8,128)(2,1)S(1)}, u32[]{:S(2)}, u32[]{:S(2)}) async-start(bf16[16,24,128]{2,1,0:T(8,128)(2,1)} %start.1), calls=%async_computation.3 | async-start | bytes 196608 | tf_op jit(solution)/shard_map/all_to_all | solution.py:249
  115.0 3.6 all-to-all-done.3.returned_ref
  120.1 163.0 %while.19 = (s32[]{:T(128)}, bf16[64,768]{1,0:T(8,128)(2,1)S(1)}, bf16[16,24,128]{2,1,0:T(8,128)(2,1)}, bf16[16,64,768]{2,1,0:T(8,128)(2,1)}, bf16[16,272,768]{2...) while((s32[]{:T(128)}, bf16[64,768]{1,0:T(8,128)(2,1)S(1)}, ...), condition=%wide.region_1.2_spmd, body=%wide.region_0.1_spmd.sunk | while | flops 6 | bytes 688311 | solution.py:294
  125.9 4.4 %all-to-all-done.returned_ref = bf16[16,24,128]{2,1,0:T(8,128)(2,1)S(1)} async-done(((bf16[16,24,128]{2,1,0:T(8,128)(2,1)}), bf16[16,24,128]{2,1,0:T(8,128)(2,1)S(1)}, u32[]{:S(2)}, u32[]{:S(2)}) %all-to-all-start) | async-done | bytes 98336 | tf_op jit(solution)/shard_map/while/body/eval_jaxpr/all_to_all | solution.py:288
  131.8 3.5 all-to-all-start
  137.5 4.4 %all-to-all-done.returned_ref = bf16[16,24,128]{2,1,0:T(8,128)(2,1)S(1)} async-done(((bf16[16,24,128]{2,1,0:T(8,128)(2,1)}), bf16[16,24,128]{2,1,0:T(8,128)(2,1)S(1)}, u32[]{:S(2)}, u32[]{:S(2)}) %all-to-all-start) | async-done | bytes 98336 | tf_op jit(solution)/shard_map/while/body/eval_jaxpr/all_to_all | solution.py:288
  143.4 3.5 all-to-all-start
  149.2 4.4 %all-to-all-done.returned_ref = bf16[16,24,128]{2,1,0:T(8,128)(2,1)S(1)} async-done(((bf16[16,24,128]{2,1,0:T(8,128)(2,1)}), bf16[16,24,128]{2,1,0:T(8,128)(2,1)S(1)}, u32[]{:S(2)}, u32[]{:S(2)}) %all-to-all-start) | async-done | bytes 98336 | tf_op jit(solution)/shard_map/while/body/eval_jaxpr/all_to_all | solution.py:288
  155.0 3.5 all-to-all-start
  160.8 4.4 %all-to-all-done.returned_ref = bf16[16,24,128]{2,1,0:T(8,128)(2,1)S(1)} async-done(((bf16[16,24,128]{2,1,0:T(8,128)(2,1)}), bf16[16,24,128]{2,1,0:T(8,128)(2,1)S(1)}, u32[]{:S(2)}, u32[]{:S(2)}) %all-to-all-start) | async-done | bytes 98336 | tf_op jit(solution)/shard_map/while/body/eval_jaxpr/all_to_all | solution.py:288
  172.4 4.4 %all-to-all-done.returned_ref = bf16[16,24,128]{2,1,0:T(8,128)(2,1)S(1)} async-done(((bf16[16,24,128]{2,1,0:T(8,128)(2,1)}), bf16[16,24,128]{2,1,0:T(8,128)(2,1)S(1)}, u32[]{:S(2)}, u32[]{:S(2)}) %all-to-all-start) | async-done | bytes 98336 | tf_op jit(solution)/shard_map/while/body/eval_jaxpr/all_to_all | solution.py:288
  184.0 4.4 %all-to-all-done.returned_ref = bf16[16,24,128]{2,1,0:T(8,128)(2,1)S(1)} async-done(((bf16[16,24,128]{2,1,0:T(8,128)(2,1)}), bf16[16,24,128]{2,1,0:T(8,128)(2,1)S(1)}, u32[]{:S(2)}, u32[]{:S(2)}) %all-to-all-start) | async-done | bytes 98336 | tf_op jit(solution)/shard_map/while/body/eval_jaxpr/all_to_all | solution.py:288
  195.6 4.4 %all-to-all-done.returned_ref = bf16[16,24,128]{2,1,0:T(8,128)(2,1)S(1)} async-done(((bf16[16,24,128]{2,1,0:T(8,128)(2,1)}), bf16[16,24,128]{2,1,0:T(8,128)(2,1)S(1)}, u32[]{:S(2)}, u32[]{:S(2)}) %all-to-all-start) | async-done | bytes 98336 | tf_op jit(solution)/shard_map/while/body/eval_jaxpr/all_to_all | solution.py:288
  207.2 4.4 %all-to-all-done.returned_ref = bf16[16,24,128]{2,1,0:T(8,128)(2,1)S(1)} async-done(((bf16[16,24,128]{2,1,0:T(8,128)(2,1)}), bf16[16,24,128]{2,1,0:T(8,128)(2,1)S(1)}, u32[]{:S(2)}, u32[]{:S(2)}) %all-to-all-start) | async-done | bytes 98336 | tf_op jit(solution)/shard_map/while/body/eval_jaxpr/all_to_all | solution.py:288
  218.9 4.4 %all-to-all-done.returned_ref = bf16[16,24,128]{2,1,0:T(8,128)(2,1)S(1)} async-done(((bf16[16,24,128]{2,1,0:T(8,128)(2,1)}), bf16[16,24,128]{2,1,0:T(8,128)(2,1)S(1)}, u32[]{:S(2)}, u32[]{:S(2)}) %all-to-all-start) | async-done | bytes 98336 | tf_op jit(solution)/shard_map/while/body/eval_jaxpr/all_to_all | solution.py:288
  230.5 4.8 %all-to-all-done.returned_ref = bf16[16,24,128]{2,1,0:T(8,128)(2,1)S(1)} async-done(((bf16[16,24,128]{2,1,0:T(8,128)(2,1)}), bf16[16,24,128]{2,1,0:T(8,128)(2,1)S(1)}, u32[]{:S(2)}, u32[]{:S(2)}) %all-to-all-start) | async-done | bytes 98336 | tf_op jit(solution)/shard_map/while/body/eval_jaxpr/all_to_all | solution.py:288
  242.5 4.4 %all-to-all-done.returned_ref = bf16[16,24,128]{2,1,0:T(8,128)(2,1)S(1)} async-done(((bf16[16,24,128]{2,1,0:T(8,128)(2,1)}), bf16[16,24,128]{2,1,0:T(8,128)(2,1)S(1)}, u32[]{:S(2)}, u32[]{:S(2)}) %all-to-all-start) | async-done | bytes 98336 | tf_op jit(solution)/shard_map/while/body/eval_jaxpr/all_to_all | solution.py:288
  254.1 4.4 %all-to-all-done.returned_ref = bf16[16,24,128]{2,1,0:T(8,128)(2,1)S(1)} async-done(((bf16[16,24,128]{2,1,0:T(8,128)(2,1)}), bf16[16,24,128]{2,1,0:T(8,128)(2,1)S(1)}, u32[]{:S(2)}, u32[]{:S(2)}) %all-to-all-start) | async-done | bytes 98336 | tf_op jit(solution)/shard_map/while/body/eval_jaxpr/all_to_all | solution.py:288
  265.7 4.4 %all-to-all-done.returned_ref = bf16[16,24,128]{2,1,0:T(8,128)(2,1)S(1)} async-done(((bf16[16,24,128]{2,1,0:T(8,128)(2,1)}), bf16[16,24,128]{2,1,0:T(8,128)(2,1)S(1)}, u32[]{:S(2)}, u32[]{:S(2)}) %all-to-all-start) | async-done | bytes 98336 | tf_op jit(solution)/shard_map/while/body/eval_jaxpr/all_to_all | solution.py:288
  277.3 4.4 %all-to-all-done.returned_ref = bf16[16,24,128]{2,1,0:T(8,128)(2,1)S(1)} async-done(((bf16[16,24,128]{2,1,0:T(8,128)(2,1)}), bf16[16,24,128]{2,1,0:T(8,128)(2,1)S(1)}, u32[]{:S(2)}, u32[]{:S(2)}) %all-to-all-start) | async-done | bytes 98336 | tf_op jit(solution)/shard_map/while/body/eval_jaxpr/all_to_all | solution.py:288
  283.8 61.9 %all_to_all.31 = bf16[16,64,768]{2,1,0:T(8,128)(2,1)} all-to-all(bf16[16,64,768]{2,1,0:T(8,128)(2,1)} %bitcast_dynamic-update-slice_fusion.1), channel_id=1, replica_groups=mesh['pipe'=16,'tensor'=16] {'pipe'}, dimensions={0} | all-to-all | bytes 3145728 | tf_op jit(solution)/shard_map/all_to_all | solution.py:297
  345.7 4.9 %owner_send.1 = bf16[16,4,2,24,256]{4,3,2,1,0:T(8,128)(2,1)} custom-call(bf16[4,256,768]{2,1,0:T(8,128)(2,1)} %bitcast.35, bf16[768,768]{1,0:T(8,128)(2,1)} %get-tuple-element.208.w2d_ref), custom_call_target="tpu_custom_call" | custom-call | tf_op jit(solution)/shard_map/owner_send/pallas_call | solution.py:309
  350.6 3.7 all-to-all-start.5
  354.3 5.3 %settle.1 = (bf16[4,768,256]{2,1,0:T(8,128)(2,1)}, bf16[4,768,256]{2,1,0:T(8,128)(2,1)}) custom-call(bf16[16,4,2,24,256]{4,3,2,1,0:T(8,128)(2,1)} %copy-done.3, bf16[4,256,768]{2,1,0:T(8,128)(2,1)} %bitcast.34, bf16[768,768]{1,0:T(8,128)(2,1)} %get-tuple-element.212.pick2_ref), custom_call_target="tpu_custom_call" | custom-call | tf_op jit(solution)/shard_map/settle/pallas_call | solution.py:299
  359.6 20.1 %all-to-all-done.5.returned_ref = bf16[16,4,2,24,256]{4,3,2,1,0:T(8,128)(2,1)S(1)} async-done(((bf16[16,4,2,24,256]{4,3,2,1,0:T(8,128)(2,1)}), bf16[16,4,2,24,256]{4,3,2,1,0:T(8,128)(2,1)S(1)}, u32[]{:S(2)}, u32[]{:S(2)}) %all-to-all-start.5) | async-done | bytes 1572896 | tf_op jit(solution)/shard_map/all_to_all | solution.py:318
  380.9 8.4 %owner.1 = (bf16[4,256,768]{2,1,0:T(8,128)(2,1)}, f32[6,128,128]{2,1,0:T(8,128)}, f32[6,128,128]{2,1,0:T(8,128)}) custom-call(s32[1]{0:T(128)} %bitcast.25.drop_ref, bf16[16,4,2,24,256]{4,3,2,1,0:T(8,128)(2,1)} %copy-done.4, f32[4,768,256]{2,1,0:T(8,128)} %get-tuple-element.209.slope_ref, bf16[768,768]{1,0:T(8,128)(2,1)} %get-tuple-element.210.pick1_ref, ...), custom_call_target="tpu_custom_call" | custom-call | tf_op jit(solution)/shard_map/owner/pallas_call | solution.py:319
  (87 shorter events, 100.8 us)
Async XLA Ops:
  7.2 62.4 %copy-start = (bf16[8,128,768]{2,1,0:T(8,128)(2,1)S(1)}, bf16[8,128,768]{2,1,0:T(8,128)(2,1)}, u32[]{:S(2)}) copy-start(bf16[8,128,768]{2,1,0:T(8,128)(2,1)} %param.9) | copy-start | bytes 4718596
  7.2 48.6 %all-to-all-start.1 = ((bf16[16,64,768]{2,1,0:T(8,128)(2,1)}), bf16[16,64,768]{2,1,0:T(8,128)(2,1)S(1)}, u32[]{:S(2)}, u32[]{:S(2)}) async-start(bf16[16,64,768]{2,1,0:T(8,128)(2,1)} %bitcast.32), calls=%async_computation.1 | async-start | bytes 3145728 | tf_op jit(solution)/shard_map/all_to_all | solution.py:201
  17.3 84.9 %all-gather.3.cloned.1.call-start = ((), (), s32[]{:S(2)}) async-start(), calls=%async_computation.6 | async-start | bytes 7102464 | tf_op jit(solution)/shard_map/all_gather | solution.py:212
  55.8 7.0 %copy-start.2 = (bf16[16,64,768]{2,1,0:T(8,128)(2,1)}, bf16[16,64,768]{2,1,0:T(8,128)(2,1)S(1)}, u32[]{:S(2)}) copy-start(bf16[16,64,768]{2,1,0:T(8,128)(2,1)S(1)} %all-to-all-done.1.x_ref) | copy-start | bytes 4718596
  62.8 41.5 %all-to-all-start.2 = ((bf16[16,4,2,24,256]{4,3,2,1,0:T(8,128)(2,1)}), bf16[16,4,2,24,256]{4,3,2,1,0:T(8,128)(2,1)S(1)}, u32[]{:S(2)}, u32[]{:S(2)}) async-start(bf16[16,4,2,24,256]{4,3,2,1,0:T(8,128)(2,1)} %get-tuple-element.196), calls=%async_computation.2 | async-start | bytes 3145728 | tf_op jit(solution)/shard_map/all_to_all | solution.py:247
  104.3 1.2 copy-start.3
  105.5 13.2 %all-to-all-start.3 = ((bf16[16,24,128]{2,1,0:T(8,128)(2,1)}), bf16[16,24,128]{2,1,0:T(8,128)(2,1)S(1)}, u32[]{:S(2)}, u32[]{:S(2)}) async-start(bf16[16,24,128]{2,1,0:T(8,128)(2,1)} %start.1), calls=%async_computation.3 | async-start | bytes 196608 | tf_op jit(solution)/shard_map/all_to_all | solution.py:249
  113.4 5.2 %copy-start.1 = (bf16[64,768]{1,0:T(8,128)(2,1)S(1)}, bf16[64,768]{1,0:T(8,128)(2,1)}, u32[]{:S(2)}) copy-start(bf16[64,768]{1,0:T(8,128)(2,1)} %fusion.g_ref.g_in_ref) | copy-start | bytes 294916
  120.1 10.1 %all-to-all-start = ((bf16[16,24,128]{2,1,0:T(8,128)(2,1)}), bf16[16,24,128]{2,1,0:T(8,128)(2,1)S(1)}, u32[]{:S(2)}, u32[]{:S(2)}) async-start(bf16[16,24,128]{2,1,0:T(8,128)(2,1)} %get-tuple-element.289), calls=%async_computation | async-start | bytes 196608 | tf_op jit(solution)/shard_map/while/body/eval_jaxpr/all_to_all | solution.py:288
  131.8 10.1 %all-to-all-start = ((bf16[16,24,128]{2,1,0:T(8,128)(2,1)}), bf16[16,24,128]{2,1,0:T(8,128)(2,1)S(1)}, u32[]{:S(2)}, u32[]{:S(2)}) async-start(bf16[16,24,128]{2,1,0:T(8,128)(2,1)} %get-tuple-element.289), calls=%async_computation | async-start | bytes 196608 | tf_op jit(solution)/shard_map/while/body/eval_jaxpr/all_to_all | solution.py:288
  143.4 10.1 %all-to-all-start = ((bf16[16,24,128]{2,1,0:T(8,128)(2,1)}), bf16[16,24,128]{2,1,0:T(8,128)(2,1)S(1)}, u32[]{:S(2)}, u32[]{:S(2)}) async-start(bf16[16,24,128]{2,1,0:T(8,128)(2,1)} %get-tuple-element.289), calls=%async_computation | async-start | bytes 196608 | tf_op jit(solution)/shard_map/while/body/eval_jaxpr/all_to_all | solution.py:288
  155.0 10.1 %all-to-all-start = ((bf16[16,24,128]{2,1,0:T(8,128)(2,1)}), bf16[16,24,128]{2,1,0:T(8,128)(2,1)S(1)}, u32[]{:S(2)}, u32[]{:S(2)}) async-start(bf16[16,24,128]{2,1,0:T(8,128)(2,1)} %get-tuple-element.289), calls=%async_computation | async-start | bytes 196608 | tf_op jit(solution)/shard_map/while/body/eval_jaxpr/all_to_all | solution.py:288
  166.6 10.1 %all-to-all-start = ((bf16[16,24,128]{2,1,0:T(8,128)(2,1)}), bf16[16,24,128]{2,1,0:T(8,128)(2,1)S(1)}, u32[]{:S(2)}, u32[]{:S(2)}) async-start(bf16[16,24,128]{2,1,0:T(8,128)(2,1)} %get-tuple-element.289), calls=%async_computation | async-start | bytes 196608 | tf_op jit(solution)/shard_map/while/body/eval_jaxpr/all_to_all | solution.py:288
  178.2 10.1 %all-to-all-start = ((bf16[16,24,128]{2,1,0:T(8,128)(2,1)}), bf16[16,24,128]{2,1,0:T(8,128)(2,1)S(1)}, u32[]{:S(2)}, u32[]{:S(2)}) async-start(bf16[16,24,128]{2,1,0:T(8,128)(2,1)} %get-tuple-element.289), calls=%async_computation | async-start | bytes 196608 | tf_op jit(solution)/shard_map/while/body/eval_jaxpr/all_to_all | solution.py:288
  189.8 10.1 %all-to-all-start = ((bf16[16,24,128]{2,1,0:T(8,128)(2,1)}), bf16[16,24,128]{2,1,0:T(8,128)(2,1)S(1)}, u32[]{:S(2)}, u32[]{:S(2)}) async-start(bf16[16,24,128]{2,1,0:T(8,128)(2,1)} %get-tuple-element.289), calls=%async_computation | async-start | bytes 196608 | tf_op jit(solution)/shard_map/while/body/eval_jaxpr/all_to_all | solution.py:288
  201.5 10.1 %all-to-all-start = ((bf16[16,24,128]{2,1,0:T(8,128)(2,1)}), bf16[16,24,128]{2,1,0:T(8,128)(2,1)S(1)}, u32[]{:S(2)}, u32[]{:S(2)}) async-start(bf16[16,24,128]{2,1,0:T(8,128)(2,1)} %get-tuple-element.289), calls=%async_computation | async-start | bytes 196608 | tf_op jit(solution)/shard_map/while/body/eval_jaxpr/all_to_all | solution.py:288
  213.1 10.1 %all-to-all-start = ((bf16[16,24,128]{2,1,0:T(8,128)(2,1)}), bf16[16,24,128]{2,1,0:T(8,128)(2,1)S(1)}, u32[]{:S(2)}, u32[]{:S(2)}) async-start(bf16[16,24,128]{2,1,0:T(8,128)(2,1)} %get-tuple-element.289), calls=%async_computation | async-start | bytes 196608 | tf_op jit(solution)/shard_map/while/body/eval_jaxpr/all_to_all | solution.py:288
  224.7 10.5 %all-to-all-start = ((bf16[16,24,128]{2,1,0:T(8,128)(2,1)}), bf16[16,24,128]{2,1,0:T(8,128)(2,1)S(1)}, u32[]{:S(2)}, u32[]{:S(2)}) async-start(bf16[16,24,128]{2,1,0:T(8,128)(2,1)} %get-tuple-element.289), calls=%async_computation | async-start | bytes 196608 | tf_op jit(solution)/shard_map/while/body/eval_jaxpr/all_to_all | solution.py:288
  236.7 10.1 %all-to-all-start = ((bf16[16,24,128]{2,1,0:T(8,128)(2,1)}), bf16[16,24,128]{2,1,0:T(8,128)(2,1)S(1)}, u32[]{:S(2)}, u32[]{:S(2)}) async-start(bf16[16,24,128]{2,1,0:T(8,128)(2,1)} %get-tuple-element.289), calls=%async_computation | async-start | bytes 196608 | tf_op jit(solution)/shard_map/while/body/eval_jaxpr/all_to_all | solution.py:288
  248.3 10.1 %all-to-all-start = ((bf16[16,24,128]{2,1,0:T(8,128)(2,1)}), bf16[16,24,128]{2,1,0:T(8,128)(2,1)S(1)}, u32[]{:S(2)}, u32[]{:S(2)}) async-start(bf16[16,24,128]{2,1,0:T(8,128)(2,1)} %get-tuple-element.289), calls=%async_computation | async-start | bytes 196608 | tf_op jit(solution)/shard_map/while/body/eval_jaxpr/all_to_all | solution.py:288
  259.9 10.1 %all-to-all-start = ((bf16[16,24,128]{2,1,0:T(8,128)(2,1)}), bf16[16,24,128]{2,1,0:T(8,128)(2,1)S(1)}, u32[]{:S(2)}, u32[]{:S(2)}) async-start(bf16[16,24,128]{2,1,0:T(8,128)(2,1)} %get-tuple-element.289), calls=%async_computation | async-start | bytes 196608 | tf_op jit(solution)/shard_map/while/body/eval_jaxpr/all_to_all | solution.py:288
  271.6 10.1 %all-to-all-start = ((bf16[16,24,128]{2,1,0:T(8,128)(2,1)}), bf16[16,24,128]{2,1,0:T(8,128)(2,1)S(1)}, u32[]{:S(2)}, u32[]{:S(2)}) async-start(bf16[16,24,128]{2,1,0:T(8,128)(2,1)} %get-tuple-element.289), calls=%async_computation | async-start | bytes 196608 | tf_op jit(solution)/shard_map/while/body/eval_jaxpr/all_to_all | solution.py:288
  350.6 29.1 %all-to-all-start.5 = ((bf16[16,4,2,24,256]{4,3,2,1,0:T(8,128)(2,1)}), bf16[16,4,2,24,256]{4,3,2,1,0:T(8,128)(2,1)S(1)}, u32[]{:S(2)}, u32[]{:S(2)}) async-start(bf16[16,4,2,24,256]{4,3,2,1,0:T(8,128)(2,1)} %owner_send.1), calls=%async_computation.5 | async-start | bytes 3145728 | tf_op jit(solution)/shard_map/all_to_all | solution.py:318
  379.7 1.2 copy-start.4
Sparse Core Ops, SparseCore 0:
  56.0 46.1 all-gather.2

commit v6 on v5

--- a/solution.py
+++ b/solution.py
@@ -16,6 +16,7 @@
 NT = ((1,), (1,))
 LANES = 128
 IDS = 16
+OWNER_MIB = 52
 RELAY_MIB = 16
 EXPAND_MIB = 16
 
@@ -198,8 +199,6 @@
     square = sds((feats, feats), bf16)
     pack_rows = 2 * LANES + IDS
 
-    xs = lax.all_to_all(x.reshape(sections, share, feats), "pipe", 0, 0, tiled=True)
-
     packed, w1d, w2d, pick1, pick2 = pl.pallas_call(
         prep_kernel,
         in_specs=[whole(pltpu.SMEM), whole(pltpu.SMEM), whole(), whole(), whole()],
@@ -208,7 +207,6 @@
         compiler_params=params,
         name="prep",
     )(group.reshape(1), drop, perm[0], w_first[0, 0], w_second[0, 0])
-    packed, xs = lax.optimization_barrier((packed, xs))
     packed = lax.all_gather(packed, "pipe")
 
     payload = sds((groups, micros, 2, half, tokens), bf16)
@@ -243,9 +241,10 @@
         compiler_params=params,
         name="start",
     )(g, packed)
-    hidden, xs = lax.optimization_barrier((hidden, xs))
     z = lax.all_to_all(hidden, "tensor", 0, 0, tiled=True)
-    mixed, z = lax.optimization_barrier((mixed, z))
+    to_share, z = lax.optimization_barrier((x, z))
+    xs = lax.all_to_all(to_share.reshape(sections, share, feats), "pipe", 0, 0, tiled=True)
+    mixed, xs = lax.optimization_barrier((mixed, xs))
     returned = lax.all_to_all(mixed, "tensor", 0, 0, tiled=True)
 
     expand = pl.pallas_call(
@@ -331,7 +330,7 @@
         ],
         out_specs=[token_spec, weight_spec, weight_spec],
         out_shape=[sds(x.shape, bf16), sds((blocks, size, size), f32), sds((blocks, size, size), f32)],
-        compiler_params=params,
+        compiler_params=pltpu.CompilerParams(vmem_limit_bytes=OWNER_MIB * 1024 * 1024),
         name="owner",
     )(drop, returned, slope, pick1, w_first[0, 0], x_turned, z, cotangent)
     return (grads.reshape(section_inputs.shape), first[None, None], second[None, None])

time: 398 us -> 391 us (0.982)
  blocking collectives: 61.9 us -> 91.1 us
  waiting for transfers between devices: 150 us -> 121 us
  starting transfers between devices: 76.2 us -> 70.4 us
    all_to_all x0 -> x1, blocking collectives: none -> 29.3 us  [on_device(): z = lax.all_to_all(hidden, 'tensor', 0, 0, tiled=True)]
    all_gather x1, waiting for transfers between devices: 31.9 us -> 5.23 us  [on_device(): packed = lax.all_gather(packed, 'pipe')]
    all_to_all x2 -> x1, starting transfers between devices: 16.9 us -> 10.5 us  [on_device(): lax.all_to_all(to_share.reshape(sections, share, feats), 'pipe', 0, 0, ti...]
    all_to_all x2 -> x1, waiting for transfers between devices: 32.7 us -> 30.3 us  [on_device(): lax.all_to_all(to_share.reshape(sections, share, feats), 'pipe', 0, 0, ti...]
  transfers between devices with their start and end apart: 19 -> 18, of which waited for: 18 -> 18; matrix products, arithmetic and copies ran while one was open for 3% -> 3% of each run, Pallas kernels for 11% -> 10%
where the time goes in v6:
time: 391 us; the launch traced here: 389 us
  waiting for transfers between devices  121 us (31%)
  blocking collectives  91.1 us (23%)
  Pallas kernels  77.6 us (20%)
  starting transfers between devices  70.4 us (18%)
  between operations  14.9 us (4%)
  local copies, waits for them, and re-layouts  13.6 us (3%)
    all_to_all x14, waiting for transfers between devices, advance(): returned = lax.all_to_all(mixed, 'tensor', 0, 0, tiled=True)  61.9 us
    all_to_all x1, blocking collectives, on_device(): cotangent = lax.all_to_all(stored, 'pipe', 0, 0, tiled=True)  61.8 us
    all_to_all x14, starting transfers between devices, advance(): returned = lax.all_to_all(mixed, 'tensor', 0, 0, tiled=True)  49.2 us
    all_to_all x1, waiting for transfers between devices, on_device(): lax.all_to_all(to_share.reshape(sections, share, feats), 'pipe', 0, 0, ti...  30.3 us
    all_to_all x1, blocking collectives, on_device(): z = lax.all_to_all(hidden, 'tensor', 0, 0, tiled=True)  29.3 us
    pallas_call x15, Pallas kernels, prepare(): return expand(jnp.full((1,), s, i32), packed, packed, xs)  23.5 us
    all_to_all x2, waiting for transfers between devices, on_device(): returned = lax.all_to_all(mixed, 'tensor', 0, 0, tiled=True)  23 us
    pallas_call x14, Pallas kernels, advance(): g, mixed = relay(returned, g, scale, w1, w2)  20.6 us
  transfers between devices with their start and end apart: 18, of which 18 were waited for; matrix products, arithmetic and copies ran while one was open for 3% of the time, Pallas kernels for 10%

profile of v6, /device:TPU:1, one launch (start us, length us, event | category | flops | bytes accessed | tf_op | source)
XLA Modules:
  0.0 388.6 jit_solution(16349809113232213253)
XLA Ops:
  8.0 5.1 %prep.1 = (bf16[272,768]{1,0:T(8,128)(2,1)}, bf16[768,768]{1,0:T(8,128)(2,1)}, bf16[768,768]{1,0:T(8,128)(2,1)}, bf16[768,768]{1,0:T(8,128)(2,1)}, bf16[768,768]{1,0:T(8,128)(2,1)}) custom-call(s32[1]{0:T(128)} %bitcast.5.group_ref, s32[1]{0:T(128)} %bitcast.24.drop_ref, s32[1,12288]{1,0:T(1,128)} %bitcast.40, bf16[6,128,128]{2,1,0:T(8,128)(2,1)} %bitcast.28, ...), custom_call_target="tpu_custom_call" | custom-call | tf_op jit(solution)/shard_map/prep/pallas_call | solution.py:202
  13.1 6.4 %forward.1 = (bf16[16,4,2,24,256]{4,3,2,1,0:T(8,128)(2,1)}, f32[4,768,256]{2,1,0:T(8,128)}) custom-call(bf16[4,256,768]{2,1,0:T(8,128)(2,1)} %bitcast.34, bf16[768,768]{1,0:T(8,128)(2,1)} %get-tuple-element.190.w1d_ref), custom_call_target="tpu_custom_call" | custom-call | tf_op jit(solution)/shard_map/forward/pallas_call | solution.py:219
  19.5 29.3 %all_to_all.31.z_ref = bf16[16,4,2,24,256]{4,3,2,1,0:T(8,128)(2,1)} all-to-all(bf16[16,4,2,24,256]{4,3,2,1,0:T(8,128)(2,1)} %get-tuple-element.191), channel_id=1, replica_groups=mesh['pipe'=16,'tensor'=16] {'tensor'}, dimensions={0} | all-to-all | bytes 3145728 | tf_op jit(solution)/shard_map/all_to_all | solution.py:244
  48.9 10.5 %all-to-all-start.2 = ((bf16[16,64,768]{2,1,0:T(8,128)(2,1)}), bf16[16,64,768]{2,1,0:T(8,128)(2,1)S(1)}, u32[]{:S(2)}, u32[]{:S(2)}) async-start(bf16[16,64,768]{2,1,0:T(8,128)(2,1)} %bitcast.35), calls=%async_computation.2 | async-start | bytes 3145728 | tf_op jit(solution)/shard_map/all_to_all | solution.py:246
  60.1 5.2 %all-gather.3.cloned.1.call-done = bf16[4352,768]{1,0:T(8,128)(2,1)} async-done(((bf16[272,768]{1,0:T(8,128)(2,1)}), bf16[4352,768]{1,0:T(8,128)(2,1)}) %all-gather.3.cloned.1.call-update) | async-done | bytes 6684688 | tf_op jit(solution)/shard_map/all_gather | solution.py:210
  67.4 30.3 %all-to-all-done.2.x_ref = bf16[16,64,768]{2,1,0:T(8,128)(2,1)S(1)} async-done(((bf16[16,64,768]{2,1,0:T(8,128)(2,1)}), bf16[16,64,768]{2,1,0:T(8,128)(2,1)S(1)}, u32[]{:S(2)}, u32[]{:S(2)}) %all-to-all-start.2) | async-done | bytes 1572896 | tf_op jit(solution)/shard_map/all_to_all | solution.py:246
  98.9 6.3 %all-to-all-start.3 = ((bf16[16,24,128]{2,1,0:T(8,128)(2,1)}), bf16[16,24,128]{2,1,0:T(8,128)(2,1)S(1)}, u32[]{:S(2)}, u32[]{:S(2)}) async-start(bf16[16,24,128]{2,1,0:T(8,128)(2,1)} %start.1), calls=%async_computation.3 | async-start | bytes 196608 | tf_op jit(solution)/shard_map/all_to_all | solution.py:248
  113.4 163.4 %while.19 = (s32[]{:T(128)}, bf16[64,768]{1,0:T(8,128)(2,1)S(1)}, bf16[16,24,128]{2,1,0:T(8,128)(2,1)}, bf16[16,64,768]{2,1,0:T(8,128)(2,1)}, bf16[16,272,768]{2...) while((s32[]{:T(128)}, bf16[64,768]{1,0:T(8,128)(2,1)S(1)}, ...), condition=%wide.region_1.2_spmd, body=%wide.region_0.1_spmd.sunk | while | flops 6 | bytes 688311 | solution.py:293
  113.4 3.6 all-to-all-start
  119.2 4.4 %all-to-all-done.returned_ref = bf16[16,24,128]{2,1,0:T(8,128)(2,1)S(1)} async-done(((bf16[16,24,128]{2,1,0:T(8,128)(2,1)}), bf16[16,24,128]{2,1,0:T(8,128)(2,1)S(1)}, u32[]{:S(2)}, u32[]{:S(2)}) %all-to-all-start) | async-done | bytes 98336 | tf_op jit(solution)/shard_map/while/body/eval_jaxpr/all_to_all | solution.py:287
  125.1 3.5 all-to-all-start
  130.8 4.4 %all-to-all-done.returned_ref = bf16[16,24,128]{2,1,0:T(8,128)(2,1)S(1)} async-done(((bf16[16,24,128]{2,1,0:T(8,128)(2,1)}), bf16[16,24,128]{2,1,0:T(8,128)(2,1)S(1)}, u32[]{:S(2)}, u32[]{:S(2)}) %all-to-all-start) | async-done | bytes 98336 | tf_op jit(solution)/shard_map/while/body/eval_jaxpr/all_to_all | solution.py:287
  142.5 4.4 %all-to-all-done.returned_ref = bf16[16,24,128]{2,1,0:T(8,128)(2,1)S(1)} async-done(((bf16[16,24,128]{2,1,0:T(8,128)(2,1)}), bf16[16,24,128]{2,1,0:T(8,128)(2,1)S(1)}, u32[]{:S(2)}, u32[]{:S(2)}) %all-to-all-start) | async-done | bytes 98336 | tf_op jit(solution)/shard_map/while/body/eval_jaxpr/all_to_all | solution.py:287
  154.1 4.4 %all-to-all-done.returned_ref = bf16[16,24,128]{2,1,0:T(8,128)(2,1)S(1)} async-done(((bf16[16,24,128]{2,1,0:T(8,128)(2,1)}), bf16[16,24,128]{2,1,0:T(8,128)(2,1)S(1)}, u32[]{:S(2)}, u32[]{:S(2)}) %all-to-all-start) | async-done | bytes 98336 | tf_op jit(solution)/shard_map/while/body/eval_jaxpr/all_to_all | solution.py:287
  159.9 3.5 all-to-all-start
  165.7 4.4 %all-to-all-done.returned_ref = bf16[16,24,128]{2,1,0:T(8,128)(2,1)S(1)} async-done(((bf16[16,24,128]{2,1,0:T(8,128)(2,1)}), bf16[16,24,128]{2,1,0:T(8,128)(2,1)S(1)}, u32[]{:S(2)}, u32[]{:S(2)}) %all-to-all-start) | async-done | bytes 98336 | tf_op jit(solution)/shard_map/while/body/eval_jaxpr/all_to_all | solution.py:287
  171.6 3.5 all-to-all-start
  177.3 4.4 %all-to-all-done.returned_ref = bf16[16,24,128]{2,1,0:T(8,128)(2,1)S(1)} async-done(((bf16[16,24,128]{2,1,0:T(8,128)(2,1)}), bf16[16,24,128]{2,1,0:T(8,128)(2,1)S(1)}, u32[]{:S(2)}, u32[]{:S(2)}) %all-to-all-start) | async-done | bytes 98336 | tf_op jit(solution)/shard_map/while/body/eval_jaxpr/all_to_all | solution.py:287
  188.9 4.4 %all-to-all-done.returned_ref = bf16[16,24,128]{2,1,0:T(8,128)(2,1)S(1)} async-done(((bf16[16,24,128]{2,1,0:T(8,128)(2,1)}), bf16[16,24,128]{2,1,0:T(8,128)(2,1)S(1)}, u32[]{:S(2)}, u32[]{:S(2)}) %all-to-all-start) | async-done | bytes 98336 | tf_op jit(solution)/shard_map/while/body/eval_jaxpr/all_to_all | solution.py:287
  200.5 4.4 %all-to-all-done.returned_ref = bf16[16,24,128]{2,1,0:T(8,128)(2,1)S(1)} async-done(((bf16[16,24,128]{2,1,0:T(8,128)(2,1)}), bf16[16,24,128]{2,1,0:T(8,128)(2,1)S(1)}, u32[]{:S(2)}, u32[]{:S(2)}) %all-to-all-start) | async-done | bytes 98336 | tf_op jit(solution)/shard_map/while/body/eval_jaxpr/all_to_all | solution.py:287
  212.2 4.4 %all-to-all-done.returned_ref = bf16[16,24,128]{2,1,0:T(8,128)(2,1)S(1)} async-done(((bf16[16,24,128]{2,1,0:T(8,128)(2,1)}), bf16[16,24,128]{2,1,0:T(8,128)(2,1)S(1)}, u32[]{:S(2)}, u32[]{:S(2)}) %all-to-all-start) | async-done | bytes 98336 | tf_op jit(solution)/shard_map/while/body/eval_jaxpr/all_to_all | solution.py:287
  223.8 5.0 %all-to-all-done.returned_ref = bf16[16,24,128]{2,1,0:T(8,128)(2,1)S(1)} async-done(((bf16[16,24,128]{2,1,0:T(8,128)(2,1)}), bf16[16,24,128]{2,1,0:T(8,128)(2,1)S(1)}, u32[]{:S(2)}, u32[]{:S(2)}) %all-to-all-start) | async-done | bytes 98336 | tf_op jit(solution)/shard_map/while/body/eval_jaxpr/all_to_all | solution.py:287
  236.0 4.4 %all-to-all-done.returned_ref = bf16[16,24,128]{2,1,0:T(8,128)(2,1)S(1)} async-done(((bf16[16,24,128]{2,1,0:T(8,128)(2,1)}), bf16[16,24,128]{2,1,0:T(8,128)(2,1)S(1)}, u32[]{:S(2)}, u32[]{:S(2)}) %all-to-all-start) | async-done | bytes 98336 | tf_op jit(solution)/shard_map/while/body/eval_jaxpr/all_to_all | solution.py:287
  247.6 4.4 %all-to-all-done.returned_ref = bf16[16,24,128]{2,1,0:T(8,128)(2,1)S(1)} async-done(((bf16[16,24,128]{2,1,0:T(8,128)(2,1)}), bf16[16,24,128]{2,1,0:T(8,128)(2,1)S(1)}, u32[]{:S(2)}, u32[]{:S(2)}) %all-to-all-start) | async-done | bytes 98336 | tf_op jit(solution)/shard_map/while/body/eval_jaxpr/all_to_all | solution.py:287
  259.3 4.4 %all-to-all-done.returned_ref = bf16[16,24,128]{2,1,0:T(8,128)(2,1)S(1)} async-done(((bf16[16,24,128]{2,1,0:T(8,128)(2,1)}), bf16[16,24,128]{2,1,0:T(8,128)(2,1)S(1)}, u32[]{:S(2)}, u32[]{:S(2)}) %all-to-all-start) | async-done | bytes 98336 | tf_op jit(solution)/shard_map/while/body/eval_jaxpr/all_to_all | solution.py:287
  270.9 4.4 %all-to-all-done.returned_ref = bf16[16,24,128]{2,1,0:T(8,128)(2,1)S(1)} async-done(((bf16[16,24,128]{2,1,0:T(8,128)(2,1)}), bf16[16,24,128]{2,1,0:T(8,128)(2,1)S(1)}, u32[]{:S(2)}, u32[]{:S(2)}) %all-to-all-start) | async-done | bytes 98336 | tf_op jit(solution)/shard_map/while/body/eval_jaxpr/all_to_all | solution.py:287
  277.4 61.8 %all_to_all.32 = bf16[16,64,768]{2,1,0:T(8,128)(2,1)} all-to-all(bf16[16,64,768]{2,1,0:T(8,128)(2,1)} %bitcast_dynamic-update-slice_fusion.1), channel_id=1, replica_groups=mesh['pipe'=16,'tensor'=16] {'pipe'}, dimensions={0} | all-to-all | bytes 3145728 | tf_op jit(solution)/shard_map/all_to_all | solution.py:296
  339.1 4.9 %owner_send.1 = bf16[16,4,2,24,256]{4,3,2,1,0:T(8,128)(2,1)} custom-call(bf16[4,256,768]{2,1,0:T(8,128)(2,1)} %bitcast.37, bf16[768,768]{1,0:T(8,128)(2,1)} %get-tuple-element.204.w2d_ref), custom_call_target="tpu_custom_call" | custom-call | tf_op jit(solution)/shard_map/owner_send/pallas_call | solution.py:308
  344.1 4.4 %all-to-all-start.5 = ((bf16[16,4,2,24,256]{4,3,2,1,0:T(8,128)(2,1)}), bf16[16,4,2,24,256]{4,3,2,1,0:T(8,128)(2,1)}, u32[]{:S(2)}, u32[]{:S(2)}) async-start(bf16[16,4,2,24,256]{4,3,2,1,0:T(8,128)(2,1)} %owner_send.1), calls=%async_computation.5 | async-start | bytes 3145728 | tf_op jit(solution)/shard_map/all_to_all | solution.py:317
  348.5 5.4 %settle.1 = (bf16[4,768,256]{2,1,0:T(8,128)(2,1)}, bf16[4,768,256]{2,1,0:T(8,128)(2,1)}) custom-call(bf16[16,4,2,24,256]{4,3,2,1,0:T(8,128)(2,1)} %all_to_all.31.z_ref, bf16[4,256,768]{2,1,0:T(8,128)(2,1)} %bitcast.36, bf16[768,768]{1,0:T(8,128)(2,1)} %get-tuple-element.208.pick2_ref), custom_call_target="tpu_custom_call" | custom-call | tf_op jit(solution)/shard_map/settle/pallas_call | solution.py:298
  353.9 19.9 %all-to-all-done.5.returned_ref = bf16[16,4,2,24,256]{4,3,2,1,0:T(8,128)(2,1)} async-done(((bf16[16,4,2,24,256]{4,3,2,1,0:T(8,128)(2,1)}), bf16[16,4,2,24,256]{4,3,2,1,0:T(8,128)(2,1)}, u32[]{:S(2)}, u32[]{:S(2)}) %all-to-all-start.5) | async-done | bytes 1572896 | tf_op jit(solution)/shard_map/all_to_all | solution.py:317
  373.8 8.0 %owner.1 = (bf16[4,256,768]{2,1,0:T(8,128)(2,1)}, f32[6,128,128]{2,1,0:T(8,128)}, f32[6,128,128]{2,1,0:T(8,128)}) custom-call(s32[1]{0:T(128)} %bitcast.25.drop_ref, bf16[16,4,2,24,256]{4,3,2,1,0:T(8,128)(2,1)} %all-to-all-done.5.returned_ref, f32[4,768,256]{2,1,0:T(8,128)} %get-tuple-element.205.slope_ref, bf16[768,768]{1,0:T(8,128)(2,1)S(1)} %copy-done.1, ...), custom_call_target="tpu_custom_call" | custom-call | tf_op jit(solution)/shard_map/owner/pallas_call | solution.py:318
  (88 shorter events, 99.6 us)
Async XLA Ops:
  7.2 52.3 %copy-start = (bf16[8,128,768]{2,1,0:T(8,128)(2,1)S(1)}, bf16[8,128,768]{2,1,0:T(8,128)(2,1)}, u32[]{:S(2)}) copy-start(bf16[8,128,768]{2,1,0:T(8,128)(2,1)} %param.9) | copy-start | bytes 4718596
  7.2 58.1 %all-gather.3.cloned.1.call-start = ((), (), s32[]{:S(2)}) async-start(), calls=%async_computation.6 | async-start | bytes 7102464 | tf_op jit(solution)/shard_map/all_gather | solution.py:210
  48.9 48.9 %all-to-all-start.2 = ((bf16[16,64,768]{2,1,0:T(8,128)(2,1)}), bf16[16,64,768]{2,1,0:T(8,128)(2,1)S(1)}, u32[]{:S(2)}, u32[]{:S(2)}) async-start(bf16[16,64,768]{2,1,0:T(8,128)(2,1)} %bitcast.35), calls=%async_computation.2 | async-start | bytes 3145728 | tf_op jit(solution)/shard_map/all_to_all | solution.py:246
  97.8 1.1 copy-start.4
  98.9 13.0 %all-to-all-start.3 = ((bf16[16,24,128]{2,1,0:T(8,128)(2,1)}), bf16[16,24,128]{2,1,0:T(8,128)(2,1)S(1)}, u32[]{:S(2)}, u32[]{:S(2)}) async-start(bf16[16,24,128]{2,1,0:T(8,128)(2,1)} %start.1), calls=%async_computation.3 | async-start | bytes 196608 | tf_op jit(solution)/shard_map/all_to_all | solution.py:248
  105.2 2.0 copy-start.5
  107.2 4.7 %copy-start.2 = (bf16[64,768]{1,0:T(8,128)(2,1)S(1)}, bf16[64,768]{1,0:T(8,128)(2,1)}, u32[]{:S(2)}) copy-start(bf16[64,768]{1,0:T(8,128)(2,1)} %fusion.g_ref.g_in_ref) | copy-start | bytes 294916
  113.4 10.2 %all-to-all-start = ((bf16[16,24,128]{2,1,0:T(8,128)(2,1)}), bf16[16,24,128]{2,1,0:T(8,128)(2,1)S(1)}, u32[]{:S(2)}, u32[]{:S(2)}) async-start(bf16[16,24,128]{2,1,0:T(8,128)(2,1)} %get-tuple-element.285), calls=%async_computation | async-start | bytes 196608 | tf_op jit(solution)/shard_map/while/body/eval_jaxpr/all_to_all | solution.py:287
  125.1 10.1 %all-to-all-start = ((bf16[16,24,128]{2,1,0:T(8,128)(2,1)}), bf16[16,24,128]{2,1,0:T(8,128)(2,1)S(1)}, u32[]{:S(2)}, u32[]{:S(2)}) async-start(bf16[16,24,128]{2,1,0:T(8,128)(2,1)} %get-tuple-element.285), calls=%async_computation | async-start | bytes 196608 | tf_op jit(solution)/shard_map/while/body/eval_jaxpr/all_to_all | solution.py:287
  136.7 10.1 %all-to-all-start = ((bf16[16,24,128]{2,1,0:T(8,128)(2,1)}), bf16[16,24,128]{2,1,0:T(8,128)(2,1)S(1)}, u32[]{:S(2)}, u32[]{:S(2)}) async-start(bf16[16,24,128]{2,1,0:T(8,128)(2,1)} %get-tuple-element.285), calls=%async_computation | async-start | bytes 196608 | tf_op jit(solution)/shard_map/while/body/eval_jaxpr/all_to_all | solution.py:287
  148.3 10.1 %all-to-all-start = ((bf16[16,24,128]{2,1,0:T(8,128)(2,1)}), bf16[16,24,128]{2,1,0:T(8,128)(2,1)S(1)}, u32[]{:S(2)}, u32[]{:S(2)}) async-start(bf16[16,24,128]{2,1,0:T(8,128)(2,1)} %get-tuple-element.285), calls=%async_computation | async-start | bytes 196608 | tf_op jit(solution)/shard_map/while/body/eval_jaxpr/all_to_all | solution.py:287
  159.9 10.1 %all-to-all-start = ((bf16[16,24,128]{2,1,0:T(8,128)(2,1)}), bf16[16,24,128]{2,1,0:T(8,128)(2,1)S(1)}, u32[]{:S(2)}, u32[]{:S(2)}) async-start(bf16[16,24,128]{2,1,0:T(8,128)(2,1)} %get-tuple-element.285), calls=%async_computation | async-start | bytes 196608 | tf_op jit(solution)/shard_map/while/body/eval_jaxpr/all_to_all | solution.py:287
  171.6 10.1 %all-to-all-start = ((bf16[16,24,128]{2,1,0:T(8,128)(2,1)}), bf16[16,24,128]{2,1,0:T(8,128)(2,1)S(1)}, u32[]{:S(2)}, u32[]{:S(2)}) async-start(bf16[16,24,128]{2,1,0:T(8,128)(2,1)} %get-tuple-element.285), calls=%async_computation | async-start | bytes 196608 | tf_op jit(solution)/shard_map/while/body/eval_jaxpr/all_to_all | solution.py:287
  183.2 10.1 %all-to-all-start = ((bf16[16,24,128]{2,1,0:T(8,128)(2,1)}), bf16[16,24,128]{2,1,0:T(8,128)(2,1)S(1)}, u32[]{:S(2)}, u32[]{:S(2)}) async-start(bf16[16,24,128]{2,1,0:T(8,128)(2,1)} %get-tuple-element.285), calls=%async_computation | async-start | bytes 196608 | tf_op jit(solution)/shard_map/while/body/eval_jaxpr/all_to_all | solution.py:287
  194.8 10.1 %all-to-all-start = ((bf16[16,24,128]{2,1,0:T(8,128)(2,1)}), bf16[16,24,128]{2,1,0:T(8,128)(2,1)S(1)}, u32[]{:S(2)}, u32[]{:S(2)}) async-start(bf16[16,24,128]{2,1,0:T(8,128)(2,1)} %get-tuple-element.285), calls=%async_computation | async-start | bytes 196608 | tf_op jit(solution)/shard_map/while/body/eval_jaxpr/all_to_all | solution.py:287
  206.4 10.1 %all-to-all-start = ((bf16[16,24,128]{2,1,0:T(8,128)(2,1)}), bf16[16,24,128]{2,1,0:T(8,128)(2,1)S(1)}, u32[]{:S(2)}, u32[]{:S(2)}) async-start(bf16[16,24,128]{2,1,0:T(8,128)(2,1)} %get-tuple-element.285), calls=%async_computation | async-start | bytes 196608 | tf_op jit(solution)/shard_map/while/body/eval_jaxpr/all_to_all | solution.py:287
  218.0 10.8 %all-to-all-start = ((bf16[16,24,128]{2,1,0:T(8,128)(2,1)}), bf16[16,24,128]{2,1,0:T(8,128)(2,1)S(1)}, u32[]{:S(2)}, u32[]{:S(2)}) async-start(bf16[16,24,128]{2,1,0:T(8,128)(2,1)} %get-tuple-element.285), calls=%async_computation | async-start | bytes 196608 | tf_op jit(solution)/shard_map/while/body/eval_jaxpr/all_to_all | solution.py:287
  230.2 10.1 %all-to-all-start = ((bf16[16,24,128]{2,1,0:T(8,128)(2,1)}), bf16[16,24,128]{2,1,0:T(8,128)(2,1)S(1)}, u32[]{:S(2)}, u32[]{:S(2)}) async-start(bf16[16,24,128]{2,1,0:T(8,128)(2,1)} %get-tuple-element.285), calls=%async_computation | async-start | bytes 196608 | tf_op jit(solution)/shard_map/while/body/eval_jaxpr/all_to_all | solution.py:287
  241.9 10.1 %all-to-all-start = ((bf16[16,24,128]{2,1,0:T(8,128)(2,1)}), bf16[16,24,128]{2,1,0:T(8,128)(2,1)S(1)}, u32[]{:S(2)}, u32[]{:S(2)}) async-start(bf16[16,24,128]{2,1,0:T(8,128)(2,1)} %get-tuple-element.285), calls=%async_computation | async-start | bytes 196608 | tf_op jit(solution)/shard_map/while/body/eval_jaxpr/all_to_all | solution.py:287
  253.5 10.1 %all-to-all-start = ((bf16[16,24,128]{2,1,0:T(8,128)(2,1)}), bf16[16,24,128]{2,1,0:T(8,128)(2,1)S(1)}, u32[]{:S(2)}, u32[]{:S(2)}) async-start(bf16[16,24,128]{2,1,0:T(8,128)(2,1)} %get-tuple-element.285), calls=%async_computation | async-start | bytes 196608 | tf_op jit(solution)/shard_map/while/body/eval_jaxpr/all_to_all | solution.py:287
  265.1 10.1 %all-to-all-start = ((bf16[16,24,128]{2,1,0:T(8,128)(2,1)}), bf16[16,24,128]{2,1,0:T(8,128)(2,1)S(1)}, u32[]{:S(2)}, u32[]{:S(2)}) async-start(bf16[16,24,128]{2,1,0:T(8,128)(2,1)} %get-tuple-element.285), calls=%async_computation | async-start | bytes 196608 | tf_op jit(solution)/shard_map/while/body/eval_jaxpr/all_to_all | solution.py:287
  344.1 29.7 %all-to-all-start.5 = ((bf16[16,4,2,24,256]{4,3,2,1,0:T(8,128)(2,1)}), bf16[16,4,2,24,256]{4,3,2,1,0:T(8,128)(2,1)}, u32[]{:S(2)}, u32[]{:S(2)}) async-start(bf16[16,4,2,24,256]{4,3,2,1,0:T(8,128)(2,1)} %owner_send.1), calls=%async_computation.5 | async-start | bytes 3145728 | tf_op jit(solution)/shard_map/all_to_all | solution.py:317
  348.5 25.3 %copy-start.1 = (bf16[768,768]{1,0:T(8,128)(2,1)S(1)}, bf16[768,768]{1,0:T(8,128)(2,1)}, u32[]{:S(2)}) copy-start(bf16[768,768]{1,0:T(8,128)(2,1)} %get-tuple-element.206.pick1_ref) | copy-start | bytes 3538948
  348.5 25.3 %copy-start.3 = (bf16[1,1,6,128,128]{4,3,2,1,0:T(8,128)(2,1)S(1)}, bf16[1,1,6,128,128]{4,3,2,1,0:T(8,128)(2,1)}, u32[]{:S(2)}) copy-start(bf16[1,1,6,128,128]{4,3,2,1,0:T(8,128)(2,1)} %param.10) | copy-start | bytes 589828
Sparse Core Ops, SparseCore 0:
  13.2 52.0 all-gather.2

commit v7 on v6

--- a/solution.py
+++ b/solution.py
@@ -122,7 +122,7 @@
         dense_ref[b * size : (b + 1) * size, :] = jnp.where(ids == b, values, 0.0).astype(bf16)
 
 
-def expand_kernel(step_ref, first_ref, second_ref, x_ref, w1_ref, w2_ref, slope_ref):
+def expand_kernel(step_ref, table_ref, first_ref, second_ref, x_ref, w1_ref, w2_ref, slope_ref):
     del step_ref
     feats = x_ref.shape[2]
     first = first_ref[0].astype(f32)
@@ -140,7 +140,7 @@
     mixed_ref[...] = jnp.transpose(s).reshape(mixed_ref.shape).astype(bf16)
 
 
-def start_kernel(g_ref, packed_ref, mixed_ref, w2_ref):
+def start_kernel(table_ref, g_ref, packed_ref, mixed_ref, w2_ref):
     packed = packed_ref[0].astype(f32)
     spread(packed[LANES : 2 * LANES], packed[2 * LANES + 1 : 2 * LANES + 2], w2_ref)
     mix(g_ref[...], w2_ref, mixed_ref)
@@ -207,7 +207,22 @@
         compiler_params=params,
         name="prep",
     )(group.reshape(1), drop, perm[0], w_first[0, 0], w_second[0, 0])
-    packed = lax.all_gather(packed, "pipe")
+    chips = sections // 2
+    core, chip = row % 2, row // 2
+    swap = [(i, i ^ 1) for i in range(sections)]
+    onward = [(2 * z, 2 * ((z + 1) % chips)) for z in range(chips)]
+    onward += [(2 * z + 1, 2 * ((z - 1) % chips) + 1) for z in range(chips)]
+    other = lax.ppermute(packed, "pipe", swap)
+    current = jnp.stack([jnp.where(core == 0, packed, other), jnp.where(core == 0, other, packed)])
+    places = [current] + [None] * (chips - 1)
+    for distance in range(1, chips // 2 + 1):
+        current = lax.ppermute(current, "pipe", onward)
+        places[chips - distance] = current
+        if 2 * distance < chips:
+            places[distance] = lax.ppermute(current, "pipe", swap)
+    packed = jnp.stack(places).reshape(sections, pack_rows, feats)
+    index = jnp.arange(sections, dtype=i32)
+    table = ((1 - 2 * core) * (index // 2 - chip)) % chips * 2 + index % 2
 
     payload = sds((groups, micros, 2, half, tokens), bf16)
     payload_spec = pl.BlockSpec((groups, 1, 2, half, tokens), lambda m: (0, m, 0, 0, 0))
@@ -230,17 +245,20 @@
     g = lax.dynamic_index_in_dim(out_grad.reshape(sections, share, feats), row, 0, keepdims=False)
     mixed = pl.pallas_call(
         start_kernel,
-        grid=(1,),
-        in_specs=[
-            pl.BlockSpec((share, feats), lambda i: (0, 0)),
-            pl.BlockSpec((1, pack_rows, feats), lambda i: (sections - 1, 0, 0)),
-        ],
-        out_specs=pl.BlockSpec((groups, half, 2 * share), lambda i: (0, 0, 0)),
+        grid_spec=pltpu.PrefetchScalarGridSpec(
+            num_scalar_prefetch=1,
+            grid=(1,),
+            in_specs=[
+                pl.BlockSpec((share, feats), lambda i, t: (0, 0)),
+                pl.BlockSpec((1, pack_rows, feats), lambda i, t: (t[sections - 1], 0, 0)),
+            ],
+            out_specs=pl.BlockSpec((groups, half, 2 * share), lambda i, t: (0, 0, 0)),
+            scratch_shapes=[pltpu.VMEM((feats, feats), bf16)],
+        ),
         out_shape=mixed_shape,
-        scratch_shapes=[pltpu.VMEM((feats, feats), bf16)],
         compiler_params=params,
         name="start",
-    )(g, packed)
+    )(table, g, packed)
     z = lax.all_to_all(hidden, "tensor", 0, 0, tiled=True)
     to_share, z = lax.optimization_barrier((x, z))
     xs = lax.all_to_all(to_share.reshape(sections, share, feats), "pipe", 0, 0, tiled=True)
@@ -250,12 +268,12 @@
     expand = pl.pallas_call(
         expand_kernel,
         grid_spec=pltpu.PrefetchScalarGridSpec(
-            num_scalar_prefetch=1,
+            num_scalar_prefetch=2,
             grid=(1,),
             in_specs=[
-                pl.BlockSpec((1, pack_rows, feats), lambda i, s: (s[0], 0, 0)),
-                pl.BlockSpec((1, pack_rows, feats), lambda i, s: (s[0] - 1, 0, 0)),
-                pl.BlockSpec((1, share, feats), lambda i, s: (s[0], 0, 0)),
+                pl.BlockSpec((1, pack_rows, feats), lambda i, s, t: (t[s[0]], 0, 0)),
+                pl.BlockSpec((1, pack_rows, feats), lambda i, s, t: (t[s[0] - 1], 0, 0)),
+                pl.BlockSpec((1, share, feats), lambda i, s, t: (s[0], 0, 0)),
             ],
             out_specs=[whole()] * 3,
         ),
@@ -274,7 +292,7 @@
     )
 
     def prepare(s):
-        return expand(jnp.full((1,), s, i32), packed, packed, xs)
+        return expand(jnp.full((1,), s, i32), table, packed, packed, xs)
 
     w1, w2, scale = prepare(sections - 1)
     stored = jnp.zeros((sections, share, feats), bf16)

time: 391 us -> 401 us (1.026)
  blocking collectives: 91.1 us -> 63 us
  starting transfers between devices: 70.4 us -> 85.8 us
  local copies, waits for them, and re-layouts: 13.6 us -> 27.5 us
  between operations: 14.9 us -> 1.53 us
  Pallas kernels: 77.6 us -> 86.5 us
  waiting for transfers between devices: 121 us -> 129 us
  other arithmetic: 0 us -> 4.94 us
    ppermute x0 -> x8, waiting for transfers between devices: none -> 45.1 us  [the longest x4 43.5 us: on_device(): current = lax.ppermute(current, 'pipe', onward)]
    all_to_all x1, waiting for transfers between devices: 30.3 us -> 0.01 us  [on_device(): lax.all_to_all(to_share.reshape(sections, share, feats), 'pipe', 0, 0, ti...]
    all_to_all x1 -> x0, blocking collectives: 29.3 us -> none  [on_device(): z = lax.all_to_all(hidden, 'tensor', 0, 0, tiled=True)]
    ppermute x0 -> x8, starting transfers between devices: none -> 13.3 us  [the longest x4 9.38 us: on_device(): current = lax.ppermute(current, 'pipe', onward)]
    unnamed x12 -> x24, local copies, waits for them, and re-layouts: 1.71 us -> 13.6 us
    pallas_call x16, Pallas kernels: 25.7 us -> 34.5 us  [the longest x15 31.7 us: prepare(): return expand(jnp.full((1,), s, i32), table, packed, packed, xs)]
    all_to_all x14, waiting for transfers between devices: 61.9 us -> 53.7 us  [advance(): returned = lax.all_to_all(mixed, 'tensor', 0, 0, tiled=True)]
    all_to_all x0 -> x1, waiting for transfers between devices: none -> 7.35 us  [on_device(): z = lax.all_to_all(hidden, 'tensor', 0, 0, tiled=True)]
  transfers between devices with their start and end apart: 18 -> 26, of which waited for: 18 -> 20; matrix products, arithmetic and copies ran while one was open for 3% -> 7% of each run, Pallas kernels for 10% -> 12%
where the time goes in v7:
time: 401 us; the launch traced here: 399 us
  waiting for transfers between devices  129 us (32%)
  Pallas kernels  86.5 us (22%)
  starting transfers between devices  85.8 us (21%)
  blocking collectives  63 us (16%)
  local copies, waits for them, and re-layouts  27.5 us (7%)
  other arithmetic  4.94 us (1%)
    all_to_all x1, blocking collectives, on_device(): cotangent = lax.all_to_all(stored, 'pipe', 0, 0, tiled=True)  63 us
    all_to_all x14, waiting for transfers between devices, advance(): returned = lax.all_to_all(mixed, 'tensor', 0, 0, tiled=True)  53.7 us
    all_to_all x14, starting transfers between devices, advance(): returned = lax.all_to_all(mixed, 'tensor', 0, 0, tiled=True)  49.1 us
    ppermute x4, waiting for transfers between devices, on_device(): current = lax.ppermute(current, 'pipe', onward)  43.5 us
    pallas_call x15, Pallas kernels, prepare(): return expand(jnp.full((1,), s, i32), table, packed, packed, xs)  31.7 us
    all_to_all x2, waiting for transfers between devices, on_device(): returned = lax.all_to_all(mixed, 'tensor', 0, 0, tiled=True)  23.1 us
    pallas_call x14, Pallas kernels, advance(): g, mixed = relay(returned, g, scale, w1, w2)  20.6 us
    unnamed x24, local copies, waits for them, and re-layouts  13.6 us
  transfers between devices with their start and end apart: 26, of which 20 were waited for; matrix products, arithmetic and copies ran while one was open for 7% of the time, Pallas kernels for 12%

profile of v7, /device:TPU:1, one launch (start us, length us, event | category | flops | bytes accessed | tf_op | source)
XLA Modules:
  0.0 398.9 jit_solution(6369634703275758190)
XLA Ops:
  1.4 5.2 %prep.1 = (bf16[272,768]{1,0:T(8,128)(2,1)}, bf16[768,768]{1,0:T(8,128)(2,1)}, bf16[768,768]{1,0:T(8,128)(2,1)}, bf16[768,768]{1,0:T(8,128)(2,1)}, bf16[768,768]{1,0:T(8,128)(2,1)}) custom-call(s32[1]{0:T(128)} %bitcast.3.group_ref, s32[1]{0:T(128)} %bitcast.44.drop_ref, s32[1,12288]{1,0:T(1,128)} %bitcast.56, bf16[6,128,128]{2,1,0:T(8,128)(2,1)} %bitcast.48, ...), custom_call_target="tpu_custom_call" | custom-call | tf_op jit(solution)/shard_map/prep/pallas_call | solution.py:202
  14.2 3.9 collective-permute-start.1
  18.0 6.4 %forward.1 = (bf16[16,4,2,24,256]{4,3,2,1,0:T(8,128)(2,1)}, f32[4,768,256]{2,1,0:T(8,128)}) custom-call(bf16[4,256,768]{2,1,0:T(8,128)(2,1)} %bitcast.50, bf16[768,768]{1,0:T(8,128)(2,1)} %get-tuple-element.210.w1d_ref), custom_call_target="tpu_custom_call" | custom-call | tf_op jit(solution)/shard_map/forward/pallas_call | solution.py:234
  24.5 6.8 %all-to-all-start.1 = ((bf16[16,4,2,24,256]{4,3,2,1,0:T(8,128)(2,1)}), bf16[16,4,2,24,256]{4,3,2,1,0:T(8,128)(2,1)S(1)}, u32[]{:S(2)}, u32[]{:S(2)}) async-start(bf16[16,4,2,24,256]{4,3,2,1,0:T(8,128)(2,1)} %get-tuple-element.211), calls=%async_computation.1 | async-start | bytes 3145728 | tf_op jit(solution)/shard_map/all_to_all | solution.py:262
  32.0 11.1 %collective-permute-done.3 = bf16[2,272,768]{2,1,0:T(8,128)(2,1)} collective-permute-done((bf16[2,272,768]{2,1,0:T(8,128)(2,1)}, bf16[2,272,768]{2,1,0:T(8,128)(2,1)}, u32[]{:S(2)}, u32[]{:S(2)}) %collective-permute-start.3) | collective-permute-done | bytes 835616 | tf_op jit(solution)/shard_map/ppermute | solution.py:219
  45.1 7.3 %all-to-all-done.1.z_ref = bf16[16,4,2,24,256]{4,3,2,1,0:T(8,128)(2,1)S(1)} async-done(((bf16[16,4,2,24,256]{4,3,2,1,0:T(8,128)(2,1)}), bf16[16,4,2,24,256]{4,3,2,1,0:T(8,128)(2,1)S(1)}, u32[]{:S(2)}, u32[]{:S(2)}) %all-to-all-start.1) | async-done | bytes 1572896 | tf_op jit(solution)/shard_map/all_to_all | solution.py:262
  53.7 8.6 %all-to-all-start.2 = ((bf16[16,64,768]{2,1,0:T(8,128)(2,1)}), bf16[16,64,768]{2,1,0:T(8,128)(2,1)S(1)}, u32[]{:S(2)}, u32[]{:S(2)}) async-start(bf16[16,64,768]{2,1,0:T(8,128)(2,1)} %bitcast.51), calls=%async_computation.2 | async-start | bytes 3145728 | tf_op jit(solution)/shard_map/all_to_all | solution.py:264
  75.5 32.3 %collective-permute-done.7 = bf16[2,272,768]{2,1,0:T(8,128)(2,1)S(1)} collective-permute-done((bf16[2,272,768]{2,1,0:T(8,128)(2,1)}, bf16[2,272,768]{2,1,0:T(8,128)(2,1)S(1)}, u32[]{:S(2)}, u32[]{:S(2)}) %collective-permute-start.7) | collective-permute-done | bytes 835616 | tf_op jit(solution)/shard_map/ppermute | solution.py:219
  118.0 3.7 all-to-all-start.3
  129.6 162.9 %while.20 = (s32[]{:T(128)}, bf16[64,768]{1,0:T(8,128)(2,1)S(1)}, bf16[16,24,128]{2,1,0:T(8,128)(2,1)}, bf16[16,64,768]{2,1,0:T(8,128)(2,1)}, bf16[16,272,768]{2...) while((s32[]{:T(128)}, bf16[64,768]{1,0:T(8,128)(2,1)S(1)}, ...), condition=%wide.region_1.2_spmd.clone, body=%wide.region_0.1_spmd.clone.sunk | while | flops 438 | bytes 688399 | solution.py:311
  135.9 3.8 all-to-all-done.returned_ref
  147.5 3.8 all-to-all-done.returned_ref
  159.1 3.8 all-to-all-done.returned_ref
  170.8 3.8 all-to-all-done.returned_ref
  176.1 3.5 all-to-all-start
  182.4 3.8 all-to-all-done.returned_ref
  187.7 3.5 all-to-all-start
  194.0 3.8 all-to-all-done.returned_ref
  205.6 3.8 all-to-all-done.returned_ref
  217.2 3.8 all-to-all-done.returned_ref
  228.8 4.1 %all-to-all-done.returned_ref = bf16[16,24,128]{2,1,0:T(8,128)(2,1)S(1)} async-done(((bf16[16,24,128]{2,1,0:T(8,128)(2,1)}), bf16[16,24,128]{2,1,0:T(8,128)(2,1)S(1)}, u32[]{:S(2)}, u32[]{:S(2)}) %all-to-all-start) | async-done | bytes 98336 | tf_op jit(solution)/shard_map/while/body/eval_jaxpr/all_to_all | solution.py:305
  240.7 3.8 all-to-all-done.returned_ref
  252.4 3.8 all-to-all-done.returned_ref
  264.0 3.8 all-to-all-done.returned_ref
  275.6 3.8 all-to-all-done.returned_ref
  287.2 3.8 all-to-all-done.returned_ref
  293.2 63.0 %all_to_all.32 = bf16[16,64,768]{2,1,0:T(8,128)(2,1)} all-to-all(bf16[16,64,768]{2,1,0:T(8,128)(2,1)} %bitcast_dynamic-update-slice_fusion.9), channel_id=1, replica_groups=mesh['pipe'=16,'tensor'=16] {'pipe'}, dimensions={0} | all-to-all | bytes 3145728 | tf_op jit(solution)/shard_map/all_to_all | solution.py:314
  356.1 4.9 %owner_send.1 = bf16[16,4,2,24,256]{4,3,2,1,0:T(8,128)(2,1)} custom-call(bf16[4,256,768]{2,1,0:T(8,128)(2,1)} %bitcast.53, bf16[768,768]{1,0:T(8,128)(2,1)} %get-tuple-element.224.w2d_ref), custom_call_target="tpu_custom_call" | custom-call | tf_op jit(solution)/shard_map/owner_send/pallas_call | solution.py:326
  361.0 4.4 %all-to-all-start.5 = ((bf16[16,4,2,24,256]{4,3,2,1,0:T(8,128)(2,1)}), bf16[16,4,2,24,256]{4,3,2,1,0:T(8,128)(2,1)}, u32[]{:S(2)}, u32[]{:S(2)}) async-start(bf16[16,4,2,24,256]{4,3,2,1,0:T(8,128)(2,1)} %owner_send.1), calls=%async_computation.5 | async-start | bytes 3145728 | tf_op jit(solution)/shard_map/all_to_all | solution.py:335
  365.5 5.3 %settle.1 = (bf16[4,768,256]{2,1,0:T(8,128)(2,1)}, bf16[4,768,256]{2,1,0:T(8,128)(2,1)}) custom-call(bf16[16,4,2,24,256]{4,3,2,1,0:T(8,128)(2,1)} %copy-done.6, bf16[4,256,768]{2,1,0:T(8,128)(2,1)} %bitcast.52, bf16[768,768]{1,0:T(8,128)(2,1)} %get-tuple-element.228.pick2_ref), custom_call_target="tpu_custom_call" | custom-call | tf_op jit(solution)/shard_map/settle/pallas_call | solution.py:316
  370.8 20.1 %all-to-all-done.5.returned_ref = bf16[16,4,2,24,256]{4,3,2,1,0:T(8,128)(2,1)} async-done(((bf16[16,4,2,24,256]{4,3,2,1,0:T(8,128)(2,1)}), bf16[16,4,2,24,256]{4,3,2,1,0:T(8,128)(2,1)}, u32[]{:S(2)}, u32[]{:S(2)}) %all-to-all-start.5) | async-done | bytes 1572896 | tf_op jit(solution)/shard_map/all_to_all | solution.py:335
  390.9 8.0 %owner.1 = (bf16[4,256,768]{2,1,0:T(8,128)(2,1)}, f32[6,128,128]{2,1,0:T(8,128)}, f32[6,128,128]{2,1,0:T(8,128)}) custom-call(s32[1]{0:T(128)} %bitcast.45.drop_ref, bf16[16,4,2,24,256]{4,3,2,1,0:T(8,128)(2,1)} %all-to-all-done.5.returned_ref, f32[4,768,256]{2,1,0:T(8,128)} %get-tuple-element.225.slope_ref, bf16[768,768]{1,0:T(8,128)(2,1)S(1)} %copy-done.1, ...), custom_call_target="tpu_custom_call" | custom-call | tf_op jit(solution)/shard_map/owner/pallas_call | solution.py:336
  (133 shorter events, 145.1 us)
Async XLA Ops:
  0.6 62.9 %copy-start = (bf16[8,128,768]{2,1,0:T(8,128)(2,1)S(1)}, bf16[8,128,768]{2,1,0:T(8,128)(2,1)}, u32[]{:S(2)}) copy-start(bf16[8,128,768]{2,1,0:T(8,128)(2,1)} %param.9) | copy-start | bytes 4718596
  6.6 4.8 %collective-permute-start = (bf16[272,768]{1,0:T(8,128)(2,1)}, bf16[272,768]{1,0:T(8,128)(2,1)S(1)}, u32[]{:S(2)}, u32[]{:S(2)}) collective-permute-start(bf16[272,768]{1,0:T(8,128)(2,1)} %get-tuple-element.209), channel_id=1, source_target_pairs={{0,16},{16,0},{32,48},{48,32},{64,80},{80,64},{96,112},{112,96},{1... | collective-permute-start | bytes 1253384 | tf_op jit(solution)/shard_map/ppermute | solution.py:215
  14.2 17.1 %collective-permute-start.1 = (bf16[2,272,768]{2,1,0:T(8,128)(2,1)}, bf16[2,272,768]{2,1,0:T(8,128)(2,1)}, u32[]{:S(2)}, u32[]{:S(2)}) collective-permute-start(bf16[2,272,768]{2,1,0:T(8,128)(2,1)} %pad_maximum_fusion), channel_id=1, source_target_pairs={{0,32},{32,64},{64,96},{96,128},{128,160},{160,192},{192,224},{224... | collective-permute-start | bytes 2506760 | tf_op jit(solution)/shard_map/ppermute | solution.py:219
  24.5 28.0 %all-to-all-start.1 = ((bf16[16,4,2,24,256]{4,3,2,1,0:T(8,128)(2,1)}), bf16[16,4,2,24,256]{4,3,2,1,0:T(8,128)(2,1)S(1)}, u32[]{:S(2)}, u32[]{:S(2)}) async-start(bf16[16,4,2,24,256]{4,3,2,1,0:T(8,128)(2,1)} %get-tuple-element.211), calls=%async_computation.1 | async-start | bytes 3145728 | tf_op jit(solution)/shard_map/all_to_all | solution.py:262
  31.2 12.0 %collective-permute-start.3 = (bf16[2,272,768]{2,1,0:T(8,128)(2,1)}, bf16[2,272,768]{2,1,0:T(8,128)(2,1)}, u32[]{:S(2)}, u32[]{:S(2)}) collective-permute-start(bf16[2,272,768]{2,1,0:T(8,128)(2,1)} %collective-permute-done.1), channel_id=1, source_target_pairs={{0,32},{32,64},{64,96},{96,128},{128,160},{160,192},{192,224},{224... | collective-permute-start | bytes 2506760 | tf_op jit(solution)/shard_map/ppermute | solution.py:219
  43.2 19.6 %collective-permute-start.5 = (bf16[2,272,768]{2,1,0:T(8,128)(2,1)}, bf16[2,272,768]{2,1,0:T(8,128)(2,1)}, u32[]{:S(2)}, u32[]{:S(2)}) collective-permute-start(bf16[2,272,768]{2,1,0:T(8,128)(2,1)} %collective-permute-done.3), channel_id=1, source_target_pairs={{0,32},{32,64},{64,96},{96,128},{128,160},{160,192},{192,224},{224... | collective-permute-start | bytes 2506760 | tf_op jit(solution)/shard_map/ppermute | solution.py:219
  53.7 64.2 %all-to-all-start.2 = ((bf16[16,64,768]{2,1,0:T(8,128)(2,1)}), bf16[16,64,768]{2,1,0:T(8,128)(2,1)S(1)}, u32[]{:S(2)}, u32[]{:S(2)}) async-start(bf16[16,64,768]{2,1,0:T(8,128)(2,1)} %bitcast.51), calls=%async_computation.2 | async-start | bytes 3145728 | tf_op jit(solution)/shard_map/all_to_all | solution.py:264
  62.3 6.8 %collective-permute-start.2 = (bf16[2,272,768]{2,1,0:T(8,128)(2,1)}, bf16[2,272,768]{2,1,0:T(8,128)(2,1)}, u32[]{:S(2)}, u32[]{:S(2)}) collective-permute-start(bf16[2,272,768]{2,1,0:T(8,128)(2,1)} %collective-permute-done.1), channel_id=1, source_target_pairs={{0,16},{16,0},{32,48},{48,32},{64,80},{80,64},{96,112},{112,96},{1... | collective-permute-start | bytes 2506760 | tf_op jit(solution)/shard_map/ppermute | solution.py:222
  62.5 8.8 %collective-permute-start.4 = (bf16[2,272,768]{2,1,0:T(8,128)(2,1)}, bf16[2,272,768]{2,1,0:T(8,128)(2,1)}, u32[]{:S(2)}, u32[]{:S(2)}) collective-permute-start(bf16[2,272,768]{2,1,0:T(8,128)(2,1)} %collective-permute-done.3), channel_id=1, source_target_pairs={{0,16},{16,0},{32,48},{48,32},{64,80},{80,64},{96,112},{112,96},{1... | collective-permute-start | bytes 2506760 | tf_op jit(solution)/shard_map/ppermute | solution.py:222
  62.8 10.5 %collective-permute-start.6 = (bf16[2,272,768]{2,1,0:T(8,128)(2,1)}, bf16[2,272,768]{2,1,0:T(8,128)(2,1)}, u32[]{:S(2)}, u32[]{:S(2)}) collective-permute-start(bf16[2,272,768]{2,1,0:T(8,128)(2,1)} %collective-permute-done.5), channel_id=1, source_target_pairs={{0,16},{16,0},{32,48},{48,32},{64,80},{80,64},{96,112},{112,96},{1... | collective-permute-start | bytes 2506760 | tf_op jit(solution)/shard_map/ppermute | solution.py:222
  64.2 43.6 %collective-permute-start.7 = (bf16[2,272,768]{2,1,0:T(8,128)(2,1)}, bf16[2,272,768]{2,1,0:T(8,128)(2,1)S(1)}, u32[]{:S(2)}, u32[]{:S(2)}) collective-permute-start(bf16[2,272,768]{2,1,0:T(8,128)(2,1)} %collective-permute-done.5), channel_id=1, source_target_pairs={{0,32},{32,64},{64,96},{96,128},{128,160},{160,192},{192,224},{224... | collective-permute-start | bytes 2506760 | tf_op jit(solution)/shard_map/ppermute | solution.py:219
  117.9 5.1 %copy-start.4 = (s32[16]{0:T(128)S(1)}, s32[16]{0:T(128)}, u32[]{:S(2)}) copy-start(s32[16]{0:T(128)} %fusion.7.table_ref) | copy-start | bytes 196
  117.9 3.7 copy-start.5
  118.0 10.2 %all-to-all-start.3 = ((bf16[16,24,128]{2,1,0:T(8,128)(2,1)}), bf16[16,24,128]{2,1,0:T(8,128)(2,1)S(1)}, u32[]{:S(2)}, u32[]{:S(2)}) async-start(bf16[16,24,128]{2,1,0:T(8,128)(2,1)} %start.1), calls=%async_computation.3 | async-start | bytes 196608 | tf_op jit(solution)/shard_map/all_to_all | solution.py:266
  123.0 5.1 %copy-start.2 = (bf16[64,768]{1,0:T(8,128)(2,1)S(1)}, bf16[64,768]{1,0:T(8,128)(2,1)}, u32[]{:S(2)}) copy-start(bf16[64,768]{1,0:T(8,128)(2,1)} %fusion.12.g_ref.g_in_ref) | copy-start | bytes 294916
  129.6 10.1 %all-to-all-start = ((bf16[16,24,128]{2,1,0:T(8,128)(2,1)}), bf16[16,24,128]{2,1,0:T(8,128)(2,1)S(1)}, u32[]{:S(2)}, u32[]{:S(2)}) async-start(bf16[16,24,128]{2,1,0:T(8,128)(2,1)} %get-tuple-element.350), calls=%async_computation | async-start | bytes 196608 | tf_op jit(solution)/shard_map/while/body/eval_jaxpr/all_to_all | solution.py:305
  141.2 10.1 %all-to-all-start = ((bf16[16,24,128]{2,1,0:T(8,128)(2,1)}), bf16[16,24,128]{2,1,0:T(8,128)(2,1)S(1)}, u32[]{:S(2)}, u32[]{:S(2)}) async-start(bf16[16,24,128]{2,1,0:T(8,128)(2,1)} %get-tuple-element.350), calls=%async_computation | async-start | bytes 196608 | tf_op jit(solution)/shard_map/while/body/eval_jaxpr/all_to_all | solution.py:305
  152.8 10.1 %all-to-all-start = ((bf16[16,24,128]{2,1,0:T(8,128)(2,1)}), bf16[16,24,128]{2,1,0:T(8,128)(2,1)S(1)}, u32[]{:S(2)}, u32[]{:S(2)}) async-start(bf16[16,24,128]{2,1,0:T(8,128)(2,1)} %get-tuple-element.350), calls=%async_computation | async-start | bytes 196608 | tf_op jit(solution)/shard_map/while/body/eval_jaxpr/all_to_all | solution.py:305
  164.4 10.1 %all-to-all-start = ((bf16[16,24,128]{2,1,0:T(8,128)(2,1)}), bf16[16,24,128]{2,1,0:T(8,128)(2,1)S(1)}, u32[]{:S(2)}, u32[]{:S(2)}) async-start(bf16[16,24,128]{2,1,0:T(8,128)(2,1)} %get-tuple-element.350), calls=%async_computation | async-start | bytes 196608 | tf_op jit(solution)/shard_map/while/body/eval_jaxpr/all_to_all | solution.py:305
  176.1 10.1 %all-to-all-start = ((bf16[16,24,128]{2,1,0:T(8,128)(2,1)}), bf16[16,24,128]{2,1,0:T(8,128)(2,1)S(1)}, u32[]{:S(2)}, u32[]{:S(2)}) async-start(bf16[16,24,128]{2,1,0:T(8,128)(2,1)} %get-tuple-element.350), calls=%async_computation | async-start | bytes 196608 | tf_op jit(solution)/shard_map/while/body/eval_jaxpr/all_to_all | solution.py:305
  187.7 10.1 %all-to-all-start = ((bf16[16,24,128]{2,1,0:T(8,128)(2,1)}), bf16[16,24,128]{2,1,0:T(8,128)(2,1)S(1)}, u32[]{:S(2)}, u32[]{:S(2)}) async-start(bf16[16,24,128]{2,1,0:T(8,128)(2,1)} %get-tuple-element.350), calls=%async_computation | async-start | bytes 196608 | tf_op jit(solution)/shard_map/while/body/eval_jaxpr/all_to_all | solution.py:305
  199.3 10.1 %all-to-all-start = ((bf16[16,24,128]{2,1,0:T(8,128)(2,1)}), bf16[16,24,128]{2,1,0:T(8,128)(2,1)S(1)}, u32[]{:S(2)}, u32[]{:S(2)}) async-start(bf16[16,24,128]{2,1,0:T(8,128)(2,1)} %get-tuple-element.350), calls=%async_computation | async-start | bytes 196608 | tf_op jit(solution)/shard_map/while/body/eval_jaxpr/all_to_all | solution.py:305
  210.9 10.1 %all-to-all-start = ((bf16[16,24,128]{2,1,0:T(8,128)(2,1)}), bf16[16,24,128]{2,1,0:T(8,128)(2,1)S(1)}, u32[]{:S(2)}, u32[]{:S(2)}) async-start(bf16[16,24,128]{2,1,0:T(8,128)(2,1)} %get-tuple-element.350), calls=%async_computation | async-start | bytes 196608 | tf_op jit(solution)/shard_map/while/body/eval_jaxpr/all_to_all | solution.py:305
  222.5 10.4 %all-to-all-start = ((bf16[16,24,128]{2,1,0:T(8,128)(2,1)}), bf16[16,24,128]{2,1,0:T(8,128)(2,1)S(1)}, u32[]{:S(2)}, u32[]{:S(2)}) async-start(bf16[16,24,128]{2,1,0:T(8,128)(2,1)} %get-tuple-element.350), calls=%async_computation | async-start | bytes 196608 | tf_op jit(solution)/shard_map/while/body/eval_jaxpr/all_to_all | solution.py:305
  234.4 10.1 %all-to-all-start = ((bf16[16,24,128]{2,1,0:T(8,128)(2,1)}), bf16[16,24,128]{2,1,0:T(8,128)(2,1)S(1)}, u32[]{:S(2)}, u32[]{:S(2)}) async-start(bf16[16,24,128]{2,1,0:T(8,128)(2,1)} %get-tuple-element.350), calls=%async_computation | async-start | bytes 196608 | tf_op jit(solution)/shard_map/while/body/eval_jaxpr/all_to_all | solution.py:305
  246.0 10.1 %all-to-all-start = ((bf16[16,24,128]{2,1,0:T(8,128)(2,1)}), bf16[16,24,128]{2,1,0:T(8,128)(2,1)S(1)}, u32[]{:S(2)}, u32[]{:S(2)}) async-start(bf16[16,24,128]{2,1,0:T(8,128)(2,1)} %get-tuple-element.350), calls=%async_computation | async-start | bytes 196608 | tf_op jit(solution)/shard_map/while/body/eval_jaxpr/all_to_all | solution.py:305
  257.7 10.1 %all-to-all-start = ((bf16[16,24,128]{2,1,0:T(8,128)(2,1)}), bf16[16,24,128]{2,1,0:T(8,128)(2,1)S(1)}, u32[]{:S(2)}, u32[]{:S(2)}) async-start(bf16[16,24,128]{2,1,0:T(8,128)(2,1)} %get-tuple-element.350), calls=%async_computation | async-start | bytes 196608 | tf_op jit(solution)/shard_map/while/body/eval_jaxpr/all_to_all | solution.py:305
  269.3 10.1 %all-to-all-start = ((bf16[16,24,128]{2,1,0:T(8,128)(2,1)}), bf16[16,24,128]{2,1,0:T(8,128)(2,1)S(1)}, u32[]{:S(2)}, u32[]{:S(2)}) async-start(bf16[16,24,128]{2,1,0:T(8,128)(2,1)} %get-tuple-element.350), calls=%async_computation | async-start | bytes 196608 | tf_op jit(solution)/shard_map/while/body/eval_jaxpr/all_to_all | solution.py:305
  280.9 10.1 %all-to-all-start = ((bf16[16,24,128]{2,1,0:T(8,128)(2,1)}), bf16[16,24,128]{2,1,0:T(8,128)(2,1)S(1)}, u32[]{:S(2)}, u32[]{:S(2)}) async-start(bf16[16,24,128]{2,1,0:T(8,128)(2,1)} %get-tuple-element.350), calls=%async_computation | async-start | bytes 196608 | tf_op jit(solution)/shard_map/while/body/eval_jaxpr/all_to_all | solution.py:305
  361.0 29.9 %all-to-all-start.5 = ((bf16[16,4,2,24,256]{4,3,2,1,0:T(8,128)(2,1)}), bf16[16,4,2,24,256]{4,3,2,1,0:T(8,128)(2,1)}, u32[]{:S(2)}, u32[]{:S(2)}) async-start(bf16[16,4,2,24,256]{4,3,2,1,0:T(8,128)(2,1)} %owner_send.1), calls=%async_computation.5 | async-start | bytes 3145728 | tf_op jit(solution)/shard_map/all_to_all | solution.py:335
  365.4 25.5 %copy-start.1 = (bf16[768,768]{1,0:T(8,128)(2,1)S(1)}, bf16[768,768]{1,0:T(8,128)(2,1)}, u32[]{:S(2)}) copy-start(bf16[768,768]{1,0:T(8,128)(2,1)} %get-tuple-element.226.pick1_ref) | copy-start | bytes 3538948
  365.5 25.4 %copy-start.3 = (bf16[1,1,6,128,128]{4,3,2,1,0:T(8,128)(2,1)S(1)}, bf16[1,1,6,128,128]{4,3,2,1,0:T(8,128)(2,1)}, u32[]{:S(2)}) copy-start(bf16[1,1,6,128,128]{4,3,2,1,0:T(8,128)(2,1)} %param.10) | copy-start | bytes 589828
  (3 other events, 3.7 us)

commit v8 on v7

--- a/solution.py
+++ b/solution.py
@@ -140,8 +140,18 @@
     mixed_ref[...] = jnp.transpose(s).reshape(mixed_ref.shape).astype(bf16)
 
 
-def start_kernel(table_ref, g_ref, packed_ref, mixed_ref, w2_ref):
-    packed = packed_ref[0].astype(f32)
+def start_kernel(table_ref, g_ref, *refs):
+    *place_refs, mixed_ref, packed_ref, w2_ref, sem = refs
+    last = table_ref[table_ref.shape[0] - 1]
+    for place, place_ref in enumerate(place_refs):
+
+        @pl.when(last // 2 == place)
+        def _():
+            copy = pltpu.make_async_copy(place_ref.at[last % 2], packed_ref, sem)
+            copy.start()
+            copy.wait()
+
+    packed = packed_ref[...].astype(f32)
     spread(packed[LANES : 2 * LANES], packed[2 * LANES + 1 : 2 * LANES + 2], w2_ref)
     mix(g_ref[...], w2_ref, mixed_ref)
 
@@ -198,6 +208,8 @@
     params = pltpu.CompilerParams(vmem_limit_bytes=60 * 1024 * 1024)
     square = sds((feats, feats), bf16)
     pack_rows = 2 * LANES + IDS
+
+    xs = lax.all_to_all(x.reshape(sections, share, feats), "pipe", 0, 0, tiled=True)
 
     packed, w1d, w2d, pick1, pick2 = pl.pallas_call(
         prep_kernel,
@@ -245,24 +257,20 @@
     g = lax.dynamic_index_in_dim(out_grad.reshape(sections, share, feats), row, 0, keepdims=False)
     mixed = pl.pallas_call(
         start_kernel,
-        grid_spec=pltpu.PrefetchScalarGridSpec(
-            num_scalar_prefetch=1,
-            grid=(1,),
-            in_specs=[
-                pl.BlockSpec((share, feats), lambda i, t: (0, 0)),
-                pl.BlockSpec((1, pack_rows, feats), lambda i, t: (t[sections - 1], 0, 0)),
-            ],
-            out_specs=pl.BlockSpec((groups, half, 2 * share), lambda i, t: (0, 0, 0)),
-            scratch_shapes=[pltpu.VMEM((feats, feats), bf16)],
-        ),
+        in_specs=[whole(pltpu.SMEM), whole()] + [whole(pl.ANY)] * chips,
+        out_specs=whole(),
         out_shape=mixed_shape,
+        scratch_shapes=[
+            pltpu.VMEM((pack_rows, feats), bf16),
+            pltpu.VMEM((feats, feats), bf16),
+            pltpu.SemaphoreType.DMA,
+        ],
         compiler_params=params,
         name="start",
-    )(table, g, packed)
+    )(table, g, *places)
+    hidden, xs = lax.optimization_barrier((hidden, xs))
     z = lax.all_to_all(hidden, "tensor", 0, 0, tiled=True)
-    to_share, z = lax.optimization_barrier((x, z))
-    xs = lax.all_to_all(to_share.reshape(sections, share, feats), "pipe", 0, 0, tiled=True)
-    mixed, xs = lax.optimization_barrier((mixed, xs))
+    mixed, z = lax.optimization_barrier((mixed, z))
     returned = lax.all_to_all(mixed, "tensor", 0, 0, tiled=True)
 
     expand = pl.pallas_call(

time: 401 us -> 423 us (1.055)
  waiting for transfers between devices: 129 us -> 148 us
    ppermute x4, waiting for transfers between devices: 43.5 us -> 60.2 us  [on_device(): current = lax.ppermute(current, 'pipe', onward)]
    ppermute x3, starting transfers between devices: 0.7 us -> 7.61 us  [on_device(): places[distance] = lax.ppermute(current, 'pipe', swap)]
  transfers between devices with their start and end apart: 26 -> 26, of which waited for: 20 -> 21; matrix products, arithmetic and copies ran while one was open for 7% -> 7% of each run, Pallas kernels for 12% -> 11%
where the time goes in v8:
time: 423 us; the launch traced here: 420 us
  waiting for transfers between devices  148 us (35%)
  starting transfers between devices  88.1 us (21%)
  Pallas kernels  86.7 us (20%)
  blocking collectives  62 us (15%)
  local copies, waits for them, and re-layouts  28.8 us (7%)
  other arithmetic  4.87 us (1%)
    all_to_all x1, blocking collectives, on_device(): cotangent = lax.all_to_all(stored, 'pipe', 0, 0, tiled=True)  62 us
    ppermute x4, waiting for transfers between devices, on_device(): current = lax.ppermute(current, 'pipe', onward)  60.2 us
    all_to_all x14, waiting for transfers between devices, advance(): returned = lax.all_to_all(mixed, 'tensor', 0, 0, tiled=True)  53.8 us
    all_to_all x14, starting transfers between devices, advance(): returned = lax.all_to_all(mixed, 'tensor', 0, 0, tiled=True)  49.8 us
    pallas_call x15, Pallas kernels, prepare(): return expand(jnp.full((1,), s, i32), table, packed, packed, xs)  31.7 us
    all_to_all x2, waiting for transfers between devices, on_device(): returned = lax.all_to_all(mixed, 'tensor', 0, 0, tiled=True)  22.3 us
    pallas_call x14, Pallas kernels, advance(): g, mixed = relay(returned, g, scale, w1, w2)  20.6 us
    unnamed x24, local copies, waits for them, and re-layouts  14.8 us
  transfers between devices with their start and end apart: 26, of which 21 were waited for; matrix products, arithmetic and copies ran while one was open for 7% of the time, Pallas kernels for 11%

profile of v8, /device:TPU:1, one launch (start us, length us, event | category | flops | bytes accessed | tf_op | source)
XLA Modules:
  0.0 420.3 jit_solution(14190949947384565291)
XLA Ops:
  1.4 5.2 %prep.1 = (bf16[272,768]{1,0:T(8,128)(2,1)}, bf16[768,768]{1,0:T(8,128)(2,1)}, bf16[768,768]{1,0:T(8,128)(2,1)}, bf16[768,768]{1,0:T(8,128)(2,1)}, bf16[768,768]{1,0:T(8,128)(2,1)}) custom-call(s32[1]{0:T(128)} %bitcast.3.group_ref, s32[1]{0:T(128)} %bitcast.44.drop_ref, s32[1,12288]{1,0:T(1,128)} %bitcast.59, bf16[6,128,128]{2,1,0:T(8,128)(2,1)} %bitcast.48, ...), custom_call_target="tpu_custom_call" | custom-call | tf_op jit(solution)/shard_map/prep/pallas_call | solution.py:214
  13.3 7.1 %all-to-all-start.1 = ((bf16[16,64,768]{2,1,0:T(8,128)(2,1)}), bf16[16,64,768]{2,1,0:T(8,128)(2,1)S(1)}, u32[]{:S(2)}, u32[]{:S(2)}) async-start(bf16[16,64,768]{2,1,0:T(8,128)(2,1)} %bitcast.53), calls=%async_computation.1 | async-start | bytes 3145728 | tf_op jit(solution)/shard_map/all_to_all | solution.py:212
  25.2 40.9 %collective-permute-done.1.refs_7_ = bf16[2,272,768]{2,1,0:T(8,128)(2,1)} collective-permute-done((bf16[2,272,768]{2,1,0:T(8,128)(2,1)S(1)}, bf16[2,272,768]{2,1,0:T(8,128)(2,1)}, u32[]{:S(2)}, u32[]{:S(2)}) %collective-permute-start.1) | collective-permute-done | bytes 835616 | tf_op jit(solution)/shard_map/ppermute | solution.py:231
  67.1 11.0 %collective-permute-done.3.refs_6_ = bf16[2,272,768]{2,1,0:T(8,128)(2,1)} collective-permute-done((bf16[2,272,768]{2,1,0:T(8,128)(2,1)}, bf16[2,272,768]{2,1,0:T(8,128)(2,1)}, u32[]{:S(2)}, u32[]{:S(2)}) %collective-permute-start.3) | collective-permute-done | bytes 835616 | tf_op jit(solution)/shard_map/ppermute | solution.py:231
  81.8 8.2 %collective-permute-done.5.refs_5_ = bf16[2,272,768]{2,1,0:T(8,128)(2,1)} collective-permute-done((bf16[2,272,768]{2,1,0:T(8,128)(2,1)}, bf16[2,272,768]{2,1,0:T(8,128)(2,1)}, u32[]{:S(2)}, u32[]{:S(2)}) %collective-permute-start.5) | collective-permute-done | bytes 835616 | tf_op jit(solution)/shard_map/ppermute | solution.py:231
  90.0 5.8 %collective-permute-start.6 = (bf16[2,272,768]{2,1,0:T(8,128)(2,1)}, bf16[2,272,768]{2,1,0:T(8,128)(2,1)}, u32[]{:S(2)}, u32[]{:S(2)}) collective-permute-start(bf16[2,272,768]{2,1,0:T(8,128)(2,1)} %collective-permute-done.5.refs_5_), channel_id=1, source_target_pairs={{0,16},{16,0},{32,48},{48,32},{64,80},{80,64},{96,112},{112,96},{1... | collective-permute-start | bytes 2506760 | tf_op jit(solution)/shard_map/ppermute | solution.py:234
  96.4 6.4 %forward.1 = (bf16[16,4,2,24,256]{4,3,2,1,0:T(8,128)(2,1)}, f32[4,768,256]{2,1,0:T(8,128)}) custom-call(bf16[4,256,768]{2,1,0:T(8,128)(2,1)} %bitcast.54, bf16[768,768]{1,0:T(8,128)(2,1)} %get-tuple-element.210.w1d_ref), custom_call_target="tpu_custom_call" | custom-call | tf_op jit(solution)/shard_map/forward/pallas_call | solution.py:246
  107.0 6.8 %all-to-all-start.2 = ((bf16[16,4,2,24,256]{4,3,2,1,0:T(8,128)(2,1)}), bf16[16,4,2,24,256]{4,3,2,1,0:T(8,128)(2,1)}, u32[]{:S(2)}, u32[]{:S(2)}) async-start(bf16[16,4,2,24,256]{4,3,2,1,0:T(8,128)(2,1)} %get-tuple-element.212), calls=%async_computation.2 | async-start | bytes 3145728 | tf_op jit(solution)/shard_map/all_to_all | solution.py:272
  129.5 10.0 %all-to-all-done.2.z_ref = bf16[16,4,2,24,256]{4,3,2,1,0:T(8,128)(2,1)} async-done(((bf16[16,4,2,24,256]{4,3,2,1,0:T(8,128)(2,1)}), bf16[16,4,2,24,256]{4,3,2,1,0:T(8,128)(2,1)}, u32[]{:S(2)}, u32[]{:S(2)}) %all-to-all-start.2) | async-done | bytes 1572896 | tf_op jit(solution)/shard_map/all_to_all | solution.py:272
  139.4 3.7 all-to-all-start.3
  151.0 163.8 %while.20 = (s32[]{:T(128)}, bf16[64,768]{1,0:T(8,128)(2,1)S(1)}, bf16[16,24,128]{2,1,0:T(8,128)(2,1)}, bf16[16,64,768]{2,1,0:T(8,128)(2,1)}, bf16[16,272,768]{2...) while((s32[]{:T(128)}, bf16[64,768]{1,0:T(8,128)(2,1)S(1)}, ...), condition=%wide.region_1.2_spmd.clone, body=%wide.region_0.1_spmd.clone.sunk | while | flops 438 | bytes 688399 | solution.py:319
  151.0 4.2 %all-to-all-start = ((bf16[16,24,128]{2,1,0:T(8,128)(2,1)}), bf16[16,24,128]{2,1,0:T(8,128)(2,1)S(1)}, u32[]{:S(2)}, u32[]{:S(2)}) async-start(bf16[16,24,128]{2,1,0:T(8,128)(2,1)} %get-tuple-element.350), calls=%async_computation | async-start | bytes 196608 | tf_op jit(solution)/shard_map/while/body/eval_jaxpr/all_to_all | solution.py:313
  158.1 3.8 all-to-all-done.returned_ref
  169.8 3.8 all-to-all-done.returned_ref
  181.4 3.8 all-to-all-done.returned_ref
  193.0 3.8 all-to-all-done.returned_ref
  204.6 3.8 all-to-all-done.returned_ref
  216.2 3.8 all-to-all-done.returned_ref
  227.9 3.8 all-to-all-done.returned_ref
  239.5 3.8 all-to-all-done.returned_ref
  251.1 3.8 all-to-all-done.returned_ref
  262.7 4.2 all-to-all-done.returned_ref
  274.7 3.8 all-to-all-done.returned_ref
  286.3 3.8 all-to-all-done.returned_ref
  297.9 3.8 all-to-all-done.returned_ref
  309.5 3.8 all-to-all-done.returned_ref
  315.5 62.0 %all_to_all.32 = bf16[16,64,768]{2,1,0:T(8,128)(2,1)} all-to-all(bf16[16,64,768]{2,1,0:T(8,128)(2,1)} %bitcast_dynamic-update-slice_fusion.9), channel_id=1, replica_groups=mesh['pipe'=16,'tensor'=16] {'pipe'}, dimensions={0} | all-to-all | bytes 3145728 | tf_op jit(solution)/shard_map/all_to_all | solution.py:322
  377.5 4.9 %owner_send.1 = bf16[16,4,2,24,256]{4,3,2,1,0:T(8,128)(2,1)} custom-call(bf16[4,256,768]{2,1,0:T(8,128)(2,1)} %bitcast.56, bf16[768,768]{1,0:T(8,128)(2,1)} %get-tuple-element.224.w2d_ref), custom_call_target="tpu_custom_call" | custom-call | tf_op jit(solution)/shard_map/owner_send/pallas_call | solution.py:334
  382.4 4.4 %all-to-all-start.5 = ((bf16[16,4,2,24,256]{4,3,2,1,0:T(8,128)(2,1)}), bf16[16,4,2,24,256]{4,3,2,1,0:T(8,128)(2,1)}, u32[]{:S(2)}, u32[]{:S(2)}) async-start(bf16[16,4,2,24,256]{4,3,2,1,0:T(8,128)(2,1)} %owner_send.1), calls=%async_computation.5 | async-start | bytes 3145728 | tf_op jit(solution)/shard_map/all_to_all | solution.py:343
  386.8 5.4 %settle.1 = (bf16[4,768,256]{2,1,0:T(8,128)(2,1)}, bf16[4,768,256]{2,1,0:T(8,128)(2,1)}) custom-call(bf16[16,4,2,24,256]{4,3,2,1,0:T(8,128)(2,1)} %all-to-all-done.2.z_ref, bf16[4,256,768]{2,1,0:T(8,128)(2,1)} %bitcast.55, bf16[768,768]{1,0:T(8,128)(2,1)} %get-tuple-element.228.pick2_ref), custom_call_target="tpu_custom_call" | custom-call | tf_op jit(solution)/shard_map/settle/pallas_call | solution.py:324
  392.2 20.1 %all-to-all-done.5.returned_ref = bf16[16,4,2,24,256]{4,3,2,1,0:T(8,128)(2,1)} async-done(((bf16[16,4,2,24,256]{4,3,2,1,0:T(8,128)(2,1)}), bf16[16,4,2,24,256]{4,3,2,1,0:T(8,128)(2,1)}, u32[]{:S(2)}, u32[]{:S(2)}) %all-to-all-start.5) | async-done | bytes 1572896 | tf_op jit(solution)/shard_map/all_to_all | solution.py:343
  412.2 8.0 %owner.1 = (bf16[4,256,768]{2,1,0:T(8,128)(2,1)}, f32[6,128,128]{2,1,0:T(8,128)}, f32[6,128,128]{2,1,0:T(8,128)}) custom-call(s32[1]{0:T(128)} %bitcast.45.drop_ref, bf16[16,4,2,24,256]{4,3,2,1,0:T(8,128)(2,1)} %all-to-all-done.5.returned_ref, f32[4,768,256]{2,1,0:T(8,128)} %get-tuple-element.225.slope_ref, bf16[768,768]{1,0:T(8,128)(2,1)S(1)} %copy-done.1, ...), custom_call_target="tpu_custom_call" | custom-call | tf_op jit(solution)/shard_map/owner/pallas_call | solution.py:344
  (133 shorter events, 150.4 us)
Async XLA Ops:
  0.6 81.2 %copy-start = (bf16[8,128,768]{2,1,0:T(8,128)(2,1)S(1)}, bf16[8,128,768]{2,1,0:T(8,128)(2,1)}, u32[]{:S(2)}) copy-start(bf16[8,128,768]{2,1,0:T(8,128)(2,1)} %param.9) | copy-start | bytes 4718596
  6.6 4.8 %collective-permute-start = (bf16[272,768]{1,0:T(8,128)(2,1)}, bf16[272,768]{1,0:T(8,128)(2,1)S(1)}, u32[]{:S(2)}, u32[]{:S(2)}) collective-permute-start(bf16[272,768]{1,0:T(8,128)(2,1)} %get-tuple-element.209), channel_id=1, source_target_pairs={{0,16},{16,0},{32,48},{48,32},{64,80},{80,64},{96,112},{112,96},{1... | collective-permute-start | bytes 1253384 | tf_op jit(solution)/shard_map/ppermute | solution.py:227
  13.3 92.5 %all-to-all-start.1 = ((bf16[16,64,768]{2,1,0:T(8,128)(2,1)}), bf16[16,64,768]{2,1,0:T(8,128)(2,1)S(1)}, u32[]{:S(2)}, u32[]{:S(2)}) async-start(bf16[16,64,768]{2,1,0:T(8,128)(2,1)} %bitcast.53), calls=%async_computation.1 | async-start | bytes 3145728 | tf_op jit(solution)/shard_map/all_to_all | solution.py:212
  22.6 43.5 %collective-permute-start.1 = (bf16[2,272,768]{2,1,0:T(8,128)(2,1)S(1)}, bf16[2,272,768]{2,1,0:T(8,128)(2,1)}, u32[]{:S(2)}, u32[]{:S(2)}) collective-permute-start(bf16[2,272,768]{2,1,0:T(8,128)(2,1)S(1)} %pad_maximum_fusion.refs_0_), channel_id=1, source_target_pairs={{0,32},{32,64},{64,96},{96,128},{128,160},{160,192},{192,224},{224... | collective-permute-start | bytes 2506760 | tf_op jit(solution)/shard_map/ppermute | solution.py:231
  66.1 12.0 %collective-permute-start.3 = (bf16[2,272,768]{2,1,0:T(8,128)(2,1)}, bf16[2,272,768]{2,1,0:T(8,128)(2,1)}, u32[]{:S(2)}, u32[]{:S(2)}) collective-permute-start(bf16[2,272,768]{2,1,0:T(8,128)(2,1)} %collective-permute-done.1.refs_7_), channel_id=1, source_target_pairs={{0,32},{32,64},{64,96},{96,128},{128,160},{160,192},{192,224},{224... | collective-permute-start | bytes 2506760 | tf_op jit(solution)/shard_map/ppermute | solution.py:231
  78.1 12.0 %collective-permute-start.5 = (bf16[2,272,768]{2,1,0:T(8,128)(2,1)}, bf16[2,272,768]{2,1,0:T(8,128)(2,1)}, u32[]{:S(2)}, u32[]{:S(2)}) collective-permute-start(bf16[2,272,768]{2,1,0:T(8,128)(2,1)} %collective-permute-done.3.refs_6_), channel_id=1, source_target_pairs={{0,32},{32,64},{64,96},{96,128},{128,160},{160,192},{192,224},{224... | collective-permute-start | bytes 2506760 | tf_op jit(solution)/shard_map/ppermute | solution.py:231
  80.0 33.8 %collective-permute-start.2 = (bf16[2,272,768]{2,1,0:T(8,128)(2,1)}, bf16[2,272,768]{2,1,0:T(8,128)(2,1)}, u32[]{:S(2)}, u32[]{:S(2)}) collective-permute-start(bf16[2,272,768]{2,1,0:T(8,128)(2,1)} %collective-permute-done.1.refs_7_), channel_id=1, source_target_pairs={{0,16},{16,0},{32,48},{48,32},{64,80},{80,64},{96,112},{112,96},{1... | collective-permute-start | bytes 2506760 | tf_op jit(solution)/shard_map/ppermute | solution.py:234
  81.8 34.1 %collective-permute-start.4 = (bf16[2,272,768]{2,1,0:T(8,128)(2,1)}, bf16[2,272,768]{2,1,0:T(8,128)(2,1)}, u32[]{:S(2)}, u32[]{:S(2)}) collective-permute-start(bf16[2,272,768]{2,1,0:T(8,128)(2,1)} %collective-permute-done.3.refs_6_), channel_id=1, source_target_pairs={{0,16},{16,0},{32,48},{48,32},{64,80},{80,64},{96,112},{112,96},{1... | collective-permute-start | bytes 2506760 | tf_op jit(solution)/shard_map/ppermute | solution.py:234
  90.0 28.0 %collective-permute-start.6 = (bf16[2,272,768]{2,1,0:T(8,128)(2,1)}, bf16[2,272,768]{2,1,0:T(8,128)(2,1)}, u32[]{:S(2)}, u32[]{:S(2)}) collective-permute-start(bf16[2,272,768]{2,1,0:T(8,128)(2,1)} %collective-permute-done.5.refs_5_), channel_id=1, source_target_pairs={{0,16},{16,0},{32,48},{48,32},{64,80},{80,64},{96,112},{112,96},{1... | collective-permute-start | bytes 2506760 | tf_op jit(solution)/shard_map/ppermute | solution.py:234
  95.8 22.2 %collective-permute-start.7 = (bf16[2,272,768]{2,1,0:T(8,128)(2,1)}, bf16[2,272,768]{2,1,0:T(8,128)(2,1)}, u32[]{:S(2)}, u32[]{:S(2)}) collective-permute-start(bf16[2,272,768]{2,1,0:T(8,128)(2,1)} %collective-permute-done.5.refs_5_), channel_id=1, source_target_pairs={{0,32},{32,64},{64,96},{96,128},{128,160},{160,192},{192,224},{224... | collective-permute-start | bytes 2506760 | tf_op jit(solution)/shard_map/ppermute | solution.py:231
  102.8 2.1 copy-start.7
  107.0 32.5 %all-to-all-start.2 = ((bf16[16,4,2,24,256]{4,3,2,1,0:T(8,128)(2,1)}), bf16[16,4,2,24,256]{4,3,2,1,0:T(8,128)(2,1)}, u32[]{:S(2)}, u32[]{:S(2)}) async-start(bf16[16,4,2,24,256]{4,3,2,1,0:T(8,128)(2,1)} %get-tuple-element.212), calls=%async_computation.2 | async-start | bytes 3145728 | tf_op jit(solution)/shard_map/all_to_all | solution.py:272
  127.4 17.9 %copy-start.4 = (s32[16]{0:T(128)S(1)}, s32[16]{0:T(128)}, u32[]{:S(2)}) copy-start(s32[16]{0:T(128)} %fusion.7.table_ref) | copy-start | bytes 196
  139.4 10.1 %all-to-all-start.3 = ((bf16[16,24,128]{2,1,0:T(8,128)(2,1)}), bf16[16,24,128]{2,1,0:T(8,128)(2,1)S(1)}, u32[]{:S(2)}, u32[]{:S(2)}) async-start(bf16[16,24,128]{2,1,0:T(8,128)(2,1)} %start.1), calls=%async_computation.3 | async-start | bytes 196608 | tf_op jit(solution)/shard_map/all_to_all | solution.py:274
  145.3 4.3 %copy-start.2 = (bf16[64,768]{1,0:T(8,128)(2,1)S(1)}, bf16[64,768]{1,0:T(8,128)(2,1)}, u32[]{:S(2)}) copy-start(bf16[64,768]{1,0:T(8,128)(2,1)} %fusion.12.g_ref.g_in_ref) | copy-start | bytes 294916
  151.0 10.9 %all-to-all-start = ((bf16[16,24,128]{2,1,0:T(8,128)(2,1)}), bf16[16,24,128]{2,1,0:T(8,128)(2,1)S(1)}, u32[]{:S(2)}, u32[]{:S(2)}) async-start(bf16[16,24,128]{2,1,0:T(8,128)(2,1)} %get-tuple-element.350), calls=%async_computation | async-start | bytes 196608 | tf_op jit(solution)/shard_map/while/body/eval_jaxpr/all_to_all | solution.py:313
  163.4 10.1 %all-to-all-start = ((bf16[16,24,128]{2,1,0:T(8,128)(2,1)}), bf16[16,24,128]{2,1,0:T(8,128)(2,1)S(1)}, u32[]{:S(2)}, u32[]{:S(2)}) async-start(bf16[16,24,128]{2,1,0:T(8,128)(2,1)} %get-tuple-element.350), calls=%async_computation | async-start | bytes 196608 | tf_op jit(solution)/shard_map/while/body/eval_jaxpr/all_to_all | solution.py:313
  175.1 10.1 %all-to-all-start = ((bf16[16,24,128]{2,1,0:T(8,128)(2,1)}), bf16[16,24,128]{2,1,0:T(8,128)(2,1)S(1)}, u32[]{:S(2)}, u32[]{:S(2)}) async-start(bf16[16,24,128]{2,1,0:T(8,128)(2,1)} %get-tuple-element.350), calls=%async_computation | async-start | bytes 196608 | tf_op jit(solution)/shard_map/while/body/eval_jaxpr/all_to_all | solution.py:313
  186.7 10.1 %all-to-all-start = ((bf16[16,24,128]{2,1,0:T(8,128)(2,1)}), bf16[16,24,128]{2,1,0:T(8,128)(2,1)S(1)}, u32[]{:S(2)}, u32[]{:S(2)}) async-start(bf16[16,24,128]{2,1,0:T(8,128)(2,1)} %get-tuple-element.350), calls=%async_computation | async-start | bytes 196608 | tf_op jit(solution)/shard_map/while/body/eval_jaxpr/all_to_all | solution.py:313
  198.3 10.1 %all-to-all-start = ((bf16[16,24,128]{2,1,0:T(8,128)(2,1)}), bf16[16,24,128]{2,1,0:T(8,128)(2,1)S(1)}, u32[]{:S(2)}, u32[]{:S(2)}) async-start(bf16[16,24,128]{2,1,0:T(8,128)(2,1)} %get-tuple-element.350), calls=%async_computation | async-start | bytes 196608 | tf_op jit(solution)/shard_map/while/body/eval_jaxpr/all_to_all | solution.py:313
  209.9 10.1 %all-to-all-start = ((bf16[16,24,128]{2,1,0:T(8,128)(2,1)}), bf16[16,24,128]{2,1,0:T(8,128)(2,1)S(1)}, u32[]{:S(2)}, u32[]{:S(2)}) async-start(bf16[16,24,128]{2,1,0:T(8,128)(2,1)} %get-tuple-element.350), calls=%async_computation | async-start | bytes 196608 | tf_op jit(solution)/shard_map/while/body/eval_jaxpr/all_to_all | solution.py:313
  221.5 10.1 %all-to-all-start = ((bf16[16,24,128]{2,1,0:T(8,128)(2,1)}), bf16[16,24,128]{2,1,0:T(8,128)(2,1)S(1)}, u32[]{:S(2)}, u32[]{:S(2)}) async-start(bf16[16,24,128]{2,1,0:T(8,128)(2,1)} %get-tuple-element.350), calls=%async_computation | async-start | bytes 196608 | tf_op jit(solution)/shard_map/while/body/eval_jaxpr/all_to_all | solution.py:313
  233.1 10.1 %all-to-all-start = ((bf16[16,24,128]{2,1,0:T(8,128)(2,1)}), bf16[16,24,128]{2,1,0:T(8,128)(2,1)S(1)}, u32[]{:S(2)}, u32[]{:S(2)}) async-start(bf16[16,24,128]{2,1,0:T(8,128)(2,1)} %get-tuple-element.350), calls=%async_computation | async-start | bytes 196608 | tf_op jit(solution)/shard_map/while/body/eval_jaxpr/all_to_all | solution.py:313
  244.8 10.1 %all-to-all-start = ((bf16[16,24,128]{2,1,0:T(8,128)(2,1)}), bf16[16,24,128]{2,1,0:T(8,128)(2,1)S(1)}, u32[]{:S(2)}, u32[]{:S(2)}) async-start(bf16[16,24,128]{2,1,0:T(8,128)(2,1)} %get-tuple-element.350), calls=%async_computation | async-start | bytes 196608 | tf_op jit(solution)/shard_map/while/body/eval_jaxpr/all_to_all | solution.py:313
  256.4 10.5 %all-to-all-start = ((bf16[16,24,128]{2,1,0:T(8,128)(2,1)}), bf16[16,24,128]{2,1,0:T(8,128)(2,1)S(1)}, u32[]{:S(2)}, u32[]{:S(2)}) async-start(bf16[16,24,128]{2,1,0:T(8,128)(2,1)} %get-tuple-element.350), calls=%async_computation | async-start | bytes 196608 | tf_op jit(solution)/shard_map/while/body/eval_jaxpr/all_to_all | solution.py:313
  268.4 10.1 %all-to-all-start = ((bf16[16,24,128]{2,1,0:T(8,128)(2,1)}), bf16[16,24,128]{2,1,0:T(8,128)(2,1)S(1)}, u32[]{:S(2)}, u32[]{:S(2)}) async-start(bf16[16,24,128]{2,1,0:T(8,128)(2,1)} %get-tuple-element.350), calls=%async_computation | async-start | bytes 196608 | tf_op jit(solution)/shard_map/while/body/eval_jaxpr/all_to_all | solution.py:313
  280.0 10.1 %all-to-all-start = ((bf16[16,24,128]{2,1,0:T(8,128)(2,1)}), bf16[16,24,128]{2,1,0:T(8,128)(2,1)S(1)}, u32[]{:S(2)}, u32[]{:S(2)}) async-start(bf16[16,24,128]{2,1,0:T(8,128)(2,1)} %get-tuple-element.350), calls=%async_computation | async-start | bytes 196608 | tf_op jit(solution)/shard_map/while/body/eval_jaxpr/all_to_all | solution.py:313
  291.6 10.1 %all-to-all-start = ((bf16[16,24,128]{2,1,0:T(8,128)(2,1)}), bf16[16,24,128]{2,1,0:T(8,128)(2,1)S(1)}, u32[]{:S(2)}, u32[]{:S(2)}) async-start(bf16[16,24,128]{2,1,0:T(8,128)(2,1)} %get-tuple-element.350), calls=%async_computation | async-start | bytes 196608 | tf_op jit(solution)/shard_map/while/body/eval_jaxpr/all_to_all | solution.py:313
  303.2 10.1 %all-to-all-start = ((bf16[16,24,128]{2,1,0:T(8,128)(2,1)}), bf16[16,24,128]{2,1,0:T(8,128)(2,1)S(1)}, u32[]{:S(2)}, u32[]{:S(2)}) async-start(bf16[16,24,128]{2,1,0:T(8,128)(2,1)} %get-tuple-element.350), calls=%async_computation | async-start | bytes 196608 | tf_op jit(solution)/shard_map/while/body/eval_jaxpr/all_to_all | solution.py:313
  382.4 29.9 %all-to-all-start.5 = ((bf16[16,4,2,24,256]{4,3,2,1,0:T(8,128)(2,1)}), bf16[16,4,2,24,256]{4,3,2,1,0:T(8,128)(2,1)}, u32[]{:S(2)}, u32[]{:S(2)}) async-start(bf16[16,4,2,24,256]{4,3,2,1,0:T(8,128)(2,1)} %owner_send.1), calls=%async_computation.5 | async-start | bytes 3145728 | tf_op jit(solution)/shard_map/all_to_all | solution.py:343
  386.8 25.5 %copy-start.1 = (bf16[768,768]{1,0:T(8,128)(2,1)S(1)}, bf16[768,768]{1,0:T(8,128)(2,1)}, u32[]{:S(2)}) copy-start(bf16[768,768]{1,0:T(8,128)(2,1)} %get-tuple-element.226.pick1_ref) | copy-start | bytes 3538948
  386.8 25.4 %copy-start.3 = (bf16[1,1,6,128,128]{4,3,2,1,0:T(8,128)(2,1)S(1)}, bf16[1,1,6,128,128]{4,3,2,1,0:T(8,128)(2,1)}, u32[]{:S(2)}) copy-start(bf16[1,1,6,128,128]{4,3,2,1,0:T(8,128)(2,1)} %param.10) | copy-start | bytes 589828
  (3 other events, 4.1 us)

commit v9 on v8

--- a/solution.py
+++ b/solution.py
@@ -145,9 +145,9 @@
     last = table_ref[table_ref.shape[0] - 1]
     for place, place_ref in enumerate(place_refs):
 
-        @pl.when(last // 2 == place)
+        @pl.when(last == place)
         def _():
-            copy = pltpu.make_async_copy(place_ref.at[last % 2], packed_ref, sem)
+            copy = pltpu.make_async_copy(place_ref, packed_ref, sem)
             copy.start()
             copy.wait()
 
@@ -209,8 +209,6 @@
     square = sds((feats, feats), bf16)
     pack_rows = 2 * LANES + IDS
 
-    xs = lax.all_to_all(x.reshape(sections, share, feats), "pipe", 0, 0, tiled=True)
-
     packed, w1d, w2d, pick1, pick2 = pl.pallas_call(
         prep_kernel,
         in_specs=[whole(pltpu.SMEM), whole(pltpu.SMEM), whole(), whole(), whole()],
@@ -225,14 +223,15 @@
     onward = [(2 * z, 2 * ((z + 1) % chips)) for z in range(chips)]
     onward += [(2 * z + 1, 2 * ((z - 1) % chips) + 1) for z in range(chips)]
     other = lax.ppermute(packed, "pipe", swap)
-    current = jnp.stack([jnp.where(core == 0, packed, other), jnp.where(core == 0, other, packed)])
-    places = [current] + [None] * (chips - 1)
-    for distance in range(1, chips // 2 + 1):
-        current = lax.ppermute(current, "pipe", onward)
-        places[chips - distance] = current
-        if 2 * distance < chips:
-            places[distance] = lax.ppermute(current, "pipe", swap)
-    packed = jnp.stack(places).reshape(sections, pack_rows, feats)
+    places = [None] * sections
+    for which in range(2):
+        current = jnp.where(core == which, packed, other)
+        places[which] = current
+        for distance in range(1, chips // 2 + 1):
+            current = lax.ppermute(current, "pipe", onward)
+            places[2 * (chips - distance) + which] = current
+            if 2 * distance < chips:
+                places[2 * distance + which] = lax.ppermute(current, "pipe", swap)
     index = jnp.arange(sections, dtype=i32)
     table = ((1 - 2 * core) * (index // 2 - chip)) % chips * 2 + index % 2
 
@@ -255,9 +254,13 @@
     mixed_shape = sds((groups, half, 2 * share), bf16)
     value_shape = sds((share, feats), bf16)
     g = lax.dynamic_index_in_dim(out_grad.reshape(sections, share, feats), row, 0, keepdims=False)
+    z = lax.all_to_all(hidden, "tensor", 0, 0, tiled=True)
+    to_share, z, places = lax.optimization_barrier((x, z, places))
+    xs = lax.all_to_all(to_share.reshape(sections, share, feats), "pipe", 0, 0, tiled=True)
+    packed = jnp.stack(places)
     mixed = pl.pallas_call(
         start_kernel,
-        in_specs=[whole(pltpu.SMEM), whole()] + [whole(pl.ANY)] * chips,
+        in_specs=[whole(pltpu.SMEM), whole()] + [whole(pl.ANY)] * sections,
         out_specs=whole(),
         out_shape=mixed_shape,
         scratch_shapes=[
@@ -268,9 +271,7 @@
         compiler_params=params,
         name="start",
     )(table, g, *places)
-    hidden, xs = lax.optimization_barrier((hidden, xs))
-    z = lax.all_to_all(hidden, "tensor", 0, 0, tiled=True)
-    mixed, z = lax.optimization_barrier((mixed, z))
+    mixed, xs = lax.optimization_barrier((mixed, xs))
     returned = lax.all_to_all(mixed, "tensor", 0, 0, tiled=True)
 
     expand = pl.pallas_call(

time: 423 us -> 399 us (0.943)
  waiting for transfers between devices: 148 us -> 108 us
  local copies, waits for them, and re-layouts: 28.8 us -> 41.6 us
  starting transfers between devices: 88.1 us -> 95.1 us
    ppermute x4 -> x8, waiting for transfers between devices: 60.2 us -> 15.4 us  [on_device(): current = lax.ppermute(current, 'pipe', onward)]
    all_to_all x1, waiting for transfers between devices: 0.01 us -> 13.1 us  [on_device(): lax.all_to_all(to_share.reshape(sections, share, feats), 'pipe', 0, 0, ti...]
    unnamed x24 -> x39, local copies, waits for them, and re-layouts: 14.8 us -> 27.8 us
    all_to_all x1, waiting for transfers between devices: 9.95 us -> 0.01 us  [on_device(): z = lax.all_to_all(hidden, 'tensor', 0, 0, tiled=True)]
    ppermute x4 -> x8, starting transfers between devices: 5.46 us -> 12.2 us  [on_device(): current = lax.ppermute(current, 'pipe', onward)]
  transfers between devices with their start and end apart: 26 -> 33, of which waited for: 21 -> 23; matrix products, arithmetic and copies ran while one was open for 7% -> 9% of each run, Pallas kernels for 11% -> 12%
where the time goes in v9:
time: 399 us; the launch traced here: 396 us
  waiting for transfers between devices  108 us (27%)
  starting transfers between devices  95.1 us (24%)
  Pallas kernels  86.7 us (22%)
  blocking collectives  60.7 us (15%)
  local copies, waits for them, and re-layouts  41.6 us (10%)
    all_to_all x1, blocking collectives, on_device(): cotangent = lax.all_to_all(stored, 'pipe', 0, 0, tiled=True)  60.7 us
    all_to_all x14, waiting for transfers between devices, advance(): returned = lax.all_to_all(mixed, 'tensor', 0, 0, tiled=True)  54 us
    all_to_all x14, starting transfers between devices, advance(): returned = lax.all_to_all(mixed, 'tensor', 0, 0, tiled=True)  49.1 us
    pallas_call x15, Pallas kernels, prepare(): return expand(jnp.full((1,), s, i32), table, packed, packed, xs)  31.7 us
    unnamed x39, local copies, waits for them, and re-layouts  27.8 us
    all_to_all x2, waiting for transfers between devices, on_device(): returned = lax.all_to_all(mixed, 'tensor', 0, 0, tiled=True)  23.4 us
    pallas_call x14, Pallas kernels, advance(): g, mixed = relay(returned, g, scale, w1, w2)  20.6 us
    ppermute x8, waiting for transfers between devices, on_device(): current = lax.ppermute(current, 'pipe', onward)  15.4 us
  transfers between devices with their start and end apart: 33, of which 23 were waited for; matrix products, arithmetic and copies ran while one was open for 9% of the time, Pallas kernels for 12%

profile of v9, /device:TPU:1, one launch (start us, length us, event | category | flops | bytes accessed | tf_op | source)
XLA Modules:
  0.0 396.5 jit_solution(9324173738445640108)
XLA Ops:
  1.4 5.2 %prep.1 = (bf16[272,768]{1,0:T(8,128)(2,1)}, bf16[768,768]{1,0:T(8,128)(2,1)}, bf16[768,768]{1,0:T(8,128)(2,1)}, bf16[768,768]{1,0:T(8,128)(2,1)}, bf16[768,768]{1,0:T(8,128)(2,1)}) custom-call(s32[1]{0:T(128)} %bitcast.4.group_ref, s32[1]{0:T(128)} %bitcast.55.drop_ref, s32[1,12288]{1,0:T(1,128)} %bitcast.67, bf16[6,128,128]{2,1,0:T(8,128)(2,1)} %bitcast.59, ...), custom_call_target="tpu_custom_call" | custom-call | tf_op jit(solution)/shard_map/prep/pallas_call | solution.py:212
  13.3 3.9 collective-permute-start.1
  17.9 6.4 %forward.1 = (bf16[16,4,2,24,256]{4,3,2,1,0:T(8,128)(2,1)}, f32[4,768,256]{2,1,0:T(8,128)}) custom-call(bf16[4,256,768]{2,1,0:T(8,128)(2,1)} %bitcast.61, bf16[768,768]{1,0:T(8,128)(2,1)} %get-tuple-element.225.w1d_ref), custom_call_target="tpu_custom_call" | custom-call | tf_op jit(solution)/shard_map/forward/pallas_call | solution.py:245
  24.3 6.8 %all-to-all-start.1 = ((bf16[16,4,2,24,256]{4,3,2,1,0:T(8,128)(2,1)}), bf16[16,4,2,24,256]{4,3,2,1,0:T(8,128)(2,1)S(1)}, u32[]{:S(2)}, u32[]{:S(2)}) async-start(bf16[16,4,2,24,256]{4,3,2,1,0:T(8,128)(2,1)} %get-tuple-element.226), calls=%async_computation.1 | async-start | bytes 3145728 | tf_op jit(solution)/shard_map/all_to_all | solution.py:257
  34.4 4.3 %collective-permute-done.5.refs_12_ = bf16[272,768]{1,0:T(8,128)(2,1)S(1)} collective-permute-done((bf16[272,768]{1,0:T(8,128)(2,1)}, bf16[272,768]{1,0:T(8,128)(2,1)S(1)}, u32[]{:S(2)}, u32[]{:S(2)}) %collective-permute-start.5) | collective-permute-done | bytes 417824 | tf_op jit(solution)/shard_map/ppermute | solution.py:231
  57.2 4.1 %collective-permute-done.14.refs_9_ = bf16[272,768]{1,0:T(8,128)(2,1)} collective-permute-done((bf16[272,768]{1,0:T(8,128)(2,1)}, bf16[272,768]{1,0:T(8,128)(2,1)}, u32[]{:S(2)}, u32[]{:S(2)}) %collective-permute-start.14) | collective-permute-done | bytes 417824 | tf_op jit(solution)/shard_map/ppermute | solution.py:231
  64.8 8.8 %all-to-all-start.2 = ((bf16[16,64,768]{2,1,0:T(8,128)(2,1)}), bf16[16,64,768]{2,1,0:T(8,128)(2,1)S(1)}, u32[]{:S(2)}, u32[]{:S(2)}) async-start(bf16[16,64,768]{2,1,0:T(8,128)(2,1)} %bitcast.62), calls=%async_computation.2 | async-start | bytes 3145728 | tf_op jit(solution)/shard_map/all_to_all | solution.py:259
  99.0 13.1 %all-to-all-done.2.x_ref = bf16[16,64,768]{2,1,0:T(8,128)(2,1)S(1)} async-done(((bf16[16,64,768]{2,1,0:T(8,128)(2,1)}), bf16[16,64,768]{2,1,0:T(8,128)(2,1)S(1)}, u32[]{:S(2)}, u32[]{:S(2)}) %all-to-all-start.2) | async-done | bytes 1572896 | tf_op jit(solution)/shard_map/all_to_all | solution.py:259
  113.3 6.9 %all-to-all-start.3 = ((bf16[16,24,128]{2,1,0:T(8,128)(2,1)}), bf16[16,24,128]{2,1,0:T(8,128)(2,1)S(1)}, u32[]{:S(2)}, u32[]{:S(2)}) async-start(bf16[16,24,128]{2,1,0:T(8,128)(2,1)} %start.1), calls=%async_computation.3 | async-start | bytes 196608 | tf_op jit(solution)/shard_map/all_to_all | solution.py:275
  128.8 163.3 %while.20 = (s32[]{:T(128)}, bf16[64,768]{1,0:T(8,128)(2,1)S(1)}, bf16[16,24,128]{2,1,0:T(8,128)(2,1)}, bf16[16,64,768]{2,1,0:T(8,128)(2,1)}, bf16[16,272,768]{2...) while((s32[]{:T(128)}, bf16[64,768]{1,0:T(8,128)(2,1)S(1)}, ...), condition=%wide.region_1.2_spmd.clone, body=%wide.region_0.1_spmd.clone.sunk | while | flops 438 | bytes 688399 | solution.py:320
  135.2 3.8 all-to-all-done.returned_ref
  140.4 3.5 all-to-all-start
  146.8 3.8 all-to-all-done.returned_ref
  152.1 3.5 all-to-all-start
  158.4 3.8 all-to-all-done.returned_ref
  170.0 3.8 all-to-all-done.returned_ref
  181.6 3.8 all-to-all-done.returned_ref
  193.3 3.8 all-to-all-done.returned_ref
  204.9 3.8 all-to-all-done.returned_ref
  216.5 3.8 all-to-all-done.returned_ref
  228.1 3.8 all-to-all-done.returned_ref
  239.7 3.8 all-to-all-done.returned_ref
  251.3 4.4 %all-to-all-done.returned_ref = bf16[16,24,128]{2,1,0:T(8,128)(2,1)S(1)} async-done(((bf16[16,24,128]{2,1,0:T(8,128)(2,1)}), bf16[16,24,128]{2,1,0:T(8,128)(2,1)S(1)}, u32[]{:S(2)}, u32[]{:S(2)}) %all-to-all-start) | async-done | bytes 98336 | tf_op jit(solution)/shard_map/while/body/eval_jaxpr/all_to_all | solution.py:314
  263.6 3.8 all-to-all-done.returned_ref
  275.2 3.8 all-to-all-done.returned_ref
  286.8 3.8 all-to-all-done.returned_ref
  292.8 60.7 %all_to_all.32 = bf16[16,64,768]{2,1,0:T(8,128)(2,1)} all-to-all(bf16[16,64,768]{2,1,0:T(8,128)(2,1)} %bitcast_dynamic-update-slice_fusion.17), channel_id=1, replica_groups=mesh['pipe'=16,'tensor'=16] {'pipe'}, dimensions={0} | all-to-all | bytes 3145728 | tf_op jit(solution)/shard_map/all_to_all | solution.py:323
  353.5 5.0 %owner_send.1 = bf16[16,4,2,24,256]{4,3,2,1,0:T(8,128)(2,1)} custom-call(bf16[4,256,768]{2,1,0:T(8,128)(2,1)} %bitcast.64, bf16[768,768]{1,0:T(8,128)(2,1)} %get-tuple-element.256.w2d_ref), custom_call_target="tpu_custom_call" | custom-call | tf_op jit(solution)/shard_map/owner_send/pallas_call | solution.py:335
  358.5 4.4 %all-to-all-start.5 = ((bf16[16,4,2,24,256]{4,3,2,1,0:T(8,128)(2,1)}), bf16[16,4,2,24,256]{4,3,2,1,0:T(8,128)(2,1)}, u32[]{:S(2)}, u32[]{:S(2)}) async-start(bf16[16,4,2,24,256]{4,3,2,1,0:T(8,128)(2,1)} %owner_send.1), calls=%async_computation.5 | async-start | bytes 3145728 | tf_op jit(solution)/shard_map/all_to_all | solution.py:344
  362.9 5.3 %settle.1 = (bf16[4,768,256]{2,1,0:T(8,128)(2,1)}, bf16[4,768,256]{2,1,0:T(8,128)(2,1)}) custom-call(bf16[16,4,2,24,256]{4,3,2,1,0:T(8,128)(2,1)} %copy-done.6, bf16[4,256,768]{2,1,0:T(8,128)(2,1)} %bitcast.63, bf16[768,768]{1,0:T(8,128)(2,1)} %get-tuple-element.260.pick2_ref), custom_call_target="tpu_custom_call" | custom-call | tf_op jit(solution)/shard_map/settle/pallas_call | solution.py:325
  368.2 20.2 %all-to-all-done.5.returned_ref = bf16[16,4,2,24,256]{4,3,2,1,0:T(8,128)(2,1)} async-done(((bf16[16,4,2,24,256]{4,3,2,1,0:T(8,128)(2,1)}), bf16[16,4,2,24,256]{4,3,2,1,0:T(8,128)(2,1)}, u32[]{:S(2)}, u32[]{:S(2)}) %all-to-all-start.5) | async-done | bytes 1572896 | tf_op jit(solution)/shard_map/all_to_all | solution.py:344
  388.4 8.0 %owner.1 = (bf16[4,256,768]{2,1,0:T(8,128)(2,1)}, f32[6,128,128]{2,1,0:T(8,128)}, f32[6,128,128]{2,1,0:T(8,128)}) custom-call(s32[1]{0:T(128)} %bitcast.56.drop_ref, bf16[16,4,2,24,256]{4,3,2,1,0:T(8,128)(2,1)} %all-to-all-done.5.returned_ref, f32[4,768,256]{2,1,0:T(8,128)} %get-tuple-element.257.slope_ref, bf16[768,768]{1,0:T(8,128)(2,1)S(1)} %copy-done.1, ...), custom_call_target="tpu_custom_call" | custom-call | tf_op jit(solution)/shard_map/owner/pallas_call | solution.py:345
  (160 shorter events, 170.4 us)
Async XLA Ops:
  13.3 17.8 %collective-permute-start.1 = (bf16[272,768]{1,0:T(8,128)(2,1)}, bf16[272,768]{1,0:T(8,128)(2,1)}, u32[]{:S(2)}, u32[]{:S(2)}) collective-permute-start(bf16[272,768]{1,0:T(8,128)(2,1)} %get-tuple-element.228.refs_0_), channel_id=1, source_target_pairs={{0,32},{32,64},{64,96},{96,128},{128,160},{160,192},{192,224},{224... | collective-permute-start | bytes 1253384 | tf_op jit(solution)/shard_map/ppermute | solution.py:231
  17.2 14.7 %collective-permute-start.3 = (bf16[272,768]{1,0:T(8,128)(2,1)}, bf16[272,768]{1,0:T(8,128)(2,1)}, u32[]{:S(2)}, u32[]{:S(2)}) collective-permute-start(bf16[272,768]{1,0:T(8,128)(2,1)} %get-tuple-element.229.refs_1_), channel_id=1, source_target_pairs={{0,32},{32,64},{64,96},{96,128},{128,160},{160,192},{192,224},{224... | collective-permute-start | bytes 1253384 | tf_op jit(solution)/shard_map/ppermute | solution.py:231
  24.3 32.8 %all-to-all-start.1 = ((bf16[16,4,2,24,256]{4,3,2,1,0:T(8,128)(2,1)}), bf16[16,4,2,24,256]{4,3,2,1,0:T(8,128)(2,1)S(1)}, u32[]{:S(2)}, u32[]{:S(2)}) async-start(bf16[16,4,2,24,256]{4,3,2,1,0:T(8,128)(2,1)} %get-tuple-element.226), calls=%async_computation.1 | async-start | bytes 3145728 | tf_op jit(solution)/shard_map/all_to_all | solution.py:257
  31.1 7.6 %collective-permute-start.5 = (bf16[272,768]{1,0:T(8,128)(2,1)}, bf16[272,768]{1,0:T(8,128)(2,1)S(1)}, u32[]{:S(2)}, u32[]{:S(2)}) collective-permute-start(bf16[272,768]{1,0:T(8,128)(2,1)} %collective-permute-done.1.refs_14_), channel_id=1, source_target_pairs={{0,32},{32,64},{64,96},{96,128},{128,160},{160,192},{192,224},{224... | collective-permute-start | bytes 1253384 | tf_op jit(solution)/shard_map/ppermute | solution.py:231
  31.9 11.1 %collective-permute-start.7 = (bf16[272,768]{1,0:T(8,128)(2,1)}, bf16[272,768]{1,0:T(8,128)(2,1)}, u32[]{:S(2)}, u32[]{:S(2)}) collective-permute-start(bf16[272,768]{1,0:T(8,128)(2,1)} %collective-permute-done.3.refs_15_), channel_id=1, source_target_pairs={{0,32},{32,64},{64,96},{96,128},{128,160},{160,192},{192,224},{224... | collective-permute-start | bytes 1253384 | tf_op jit(solution)/shard_map/ppermute | solution.py:231
  32.6 12.4 %collective-permute-start.2 = (bf16[272,768]{1,0:T(8,128)(2,1)}, bf16[272,768]{1,0:T(8,128)(2,1)S(1)}, u32[]{:S(2)}, u32[]{:S(2)}) collective-permute-start(bf16[272,768]{1,0:T(8,128)(2,1)} %collective-permute-done.1.refs_14_), channel_id=1, source_target_pairs={{0,16},{16,0},{32,48},{48,32},{64,80},{80,64},{96,112},{112,96},{1... | collective-permute-start | bytes 1253384 | tf_op jit(solution)/shard_map/ppermute | solution.py:234
  38.7 9.0 %collective-permute-start.9 = (bf16[272,768]{1,0:T(8,128)(2,1)S(1)}, bf16[272,768]{1,0:T(8,128)(2,1)}, u32[]{:S(2)}, u32[]{:S(2)}) collective-permute-start(bf16[272,768]{1,0:T(8,128)(2,1)S(1)} %collective-permute-done.5.refs_12_), channel_id=1, source_target_pairs={{0,32},{32,64},{64,96},{96,128},{128,160},{160,192},{192,224},{224... | collective-permute-start | bytes 1253384 | tf_op jit(solution)/shard_map/ppermute | solution.py:231
  40.5 7.7 %collective-permute-start.4 = (bf16[272,768]{1,0:T(8,128)(2,1)}, bf16[272,768]{1,0:T(8,128)(2,1)S(1)}, u32[]{:S(2)}, u32[]{:S(2)}) collective-permute-start(bf16[272,768]{1,0:T(8,128)(2,1)} %collective-permute-done.3.refs_15_), channel_id=1, source_target_pairs={{0,16},{16,0},{32,48},{48,32},{64,80},{80,64},{96,112},{112,96},{1... | collective-permute-start | bytes 1253384 | tf_op jit(solution)/shard_map/ppermute | solution.py:234
  43.0 9.1 %collective-permute-start.11 = (bf16[272,768]{1,0:T(8,128)(2,1)}, bf16[272,768]{1,0:T(8,128)(2,1)}, u32[]{:S(2)}, u32[]{:S(2)}) collective-permute-start(bf16[272,768]{1,0:T(8,128)(2,1)} %collective-permute-done.7.refs_13_), channel_id=1, source_target_pairs={{0,32},{32,64},{64,96},{96,128},{128,160},{160,192},{192,224},{224... | collective-permute-start | bytes 1253384 | tf_op jit(solution)/shard_map/ppermute | solution.py:231
  45.0 8.0 %collective-permute-start.6 = (bf16[272,768]{1,0:T(8,128)(2,1)S(1)}, bf16[272,768]{1,0:T(8,128)(2,1)S(1)}, u32[]{:S(2)}, u32[]{:S(2)}) collective-permute-start(bf16[272,768]{1,0:T(8,128)(2,1)S(1)} %collective-permute-done.5.refs_12_), channel_id=1, source_target_pairs={{0,16},{16,0},{32,48},{48,32},{64,80},{80,64},{96,112},{112,96},{1... | collective-permute-start | bytes 1253384 | tf_op jit(solution)/shard_map/ppermute | solution.py:234
  45.0 12.1 %collective-permute-start.8 = (bf16[272,768]{1,0:T(8,128)(2,1)}, bf16[272,768]{1,0:T(8,128)(2,1)}, u32[]{:S(2)}, u32[]{:S(2)}) collective-permute-start(bf16[272,768]{1,0:T(8,128)(2,1)} %collective-permute-done.7.refs_13_), channel_id=1, source_target_pairs={{0,16},{16,0},{32,48},{48,32},{64,80},{80,64},{96,112},{112,96},{1... | collective-permute-start | bytes 1253384 | tf_op jit(solution)/shard_map/ppermute | solution.py:234
  47.6 9.5 %collective-permute-start.10 = (bf16[272,768]{1,0:T(8,128)(2,1)}, bf16[272,768]{1,0:T(8,128)(2,1)}, u32[]{:S(2)}, u32[]{:S(2)}) collective-permute-start(bf16[272,768]{1,0:T(8,128)(2,1)} %collective-permute-done.9.refs_10_), channel_id=1, source_target_pairs={{0,16},{16,0},{32,48},{48,32},{64,80},{80,64},{96,112},{112,96},{1... | collective-permute-start | bytes 1253384 | tf_op jit(solution)/shard_map/ppermute | solution.py:234
  48.2 9.0 %collective-permute-start.13 = (bf16[272,768]{1,0:T(8,128)(2,1)}, bf16[272,768]{1,0:T(8,128)(2,1)}, u32[]{:S(2)}, u32[]{:S(2)}) collective-permute-start(bf16[272,768]{1,0:T(8,128)(2,1)} %collective-permute-done.9.refs_10_), channel_id=1, source_target_pairs={{0,32},{32,64},{64,96},{96,128},{128,160},{160,192},{192,224},{224... | collective-permute-start | bytes 1253384 | tf_op jit(solution)/shard_map/ppermute | solution.py:231
  52.1 5.0 %collective-permute-start.12 = (bf16[272,768]{1,0:T(8,128)(2,1)}, bf16[272,768]{1,0:T(8,128)(2,1)}, u32[]{:S(2)}, u32[]{:S(2)}) collective-permute-start(bf16[272,768]{1,0:T(8,128)(2,1)} %collective-permute-done.11.refs_11_), channel_id=1, source_target_pairs={{0,16},{16,0},{32,48},{48,32},{64,80},{80,64},{96,112},{112,96},{1... | collective-permute-start | bytes 1253384 | tf_op jit(solution)/shard_map/ppermute | solution.py:234
  53.7 7.5 %collective-permute-start.14 = (bf16[272,768]{1,0:T(8,128)(2,1)}, bf16[272,768]{1,0:T(8,128)(2,1)}, u32[]{:S(2)}, u32[]{:S(2)}) collective-permute-start(bf16[272,768]{1,0:T(8,128)(2,1)} %collective-permute-done.11.refs_11_), channel_id=1, source_target_pairs={{0,32},{32,64},{64,96},{96,128},{128,160},{160,192},{192,224},{224... | collective-permute-start | bytes 1253384 | tf_op jit(solution)/shard_map/ppermute | solution.py:231
  64.8 47.3 %all-to-all-start.2 = ((bf16[16,64,768]{2,1,0:T(8,128)(2,1)}), bf16[16,64,768]{2,1,0:T(8,128)(2,1)S(1)}, u32[]{:S(2)}, u32[]{:S(2)}) async-start(bf16[16,64,768]{2,1,0:T(8,128)(2,1)} %bitcast.62), calls=%async_computation.2 | async-start | bytes 3145728 | tf_op jit(solution)/shard_map/all_to_all | solution.py:259
  113.3 14.1 %all-to-all-start.3 = ((bf16[16,24,128]{2,1,0:T(8,128)(2,1)}), bf16[16,24,128]{2,1,0:T(8,128)(2,1)S(1)}, u32[]{:S(2)}, u32[]{:S(2)}) async-start(bf16[16,24,128]{2,1,0:T(8,128)(2,1)} %start.1), calls=%async_computation.3 | async-start | bytes 196608 | tf_op jit(solution)/shard_map/all_to_all | solution.py:275
  128.8 10.1 %all-to-all-start = ((bf16[16,24,128]{2,1,0:T(8,128)(2,1)}), bf16[16,24,128]{2,1,0:T(8,128)(2,1)S(1)}, u32[]{:S(2)}, u32[]{:S(2)}) async-start(bf16[16,24,128]{2,1,0:T(8,128)(2,1)} %get-tuple-element.382), calls=%async_computation | async-start | bytes 196608 | tf_op jit(solution)/shard_map/while/body/eval_jaxpr/all_to_all | solution.py:314
  140.4 10.1 %all-to-all-start = ((bf16[16,24,128]{2,1,0:T(8,128)(2,1)}), bf16[16,24,128]{2,1,0:T(8,128)(2,1)S(1)}, u32[]{:S(2)}, u32[]{:S(2)}) async-start(bf16[16,24,128]{2,1,0:T(8,128)(2,1)} %get-tuple-element.382), calls=%async_computation | async-start | bytes 196608 | tf_op jit(solution)/shard_map/while/body/eval_jaxpr/all_to_all | solution.py:314
  152.1 10.1 %all-to-all-start = ((bf16[16,24,128]{2,1,0:T(8,128)(2,1)}), bf16[16,24,128]{2,1,0:T(8,128)(2,1)S(1)}, u32[]{:S(2)}, u32[]{:S(2)}) async-start(bf16[16,24,128]{2,1,0:T(8,128)(2,1)} %get-tuple-element.382), calls=%async_computation | async-start | bytes 196608 | tf_op jit(solution)/shard_map/while/body/eval_jaxpr/all_to_all | solution.py:314
  163.7 10.1 %all-to-all-start = ((bf16[16,24,128]{2,1,0:T(8,128)(2,1)}), bf16[16,24,128]{2,1,0:T(8,128)(2,1)S(1)}, u32[]{:S(2)}, u32[]{:S(2)}) async-start(bf16[16,24,128]{2,1,0:T(8,128)(2,1)} %get-tuple-element.382), calls=%async_computation | async-start | bytes 196608 | tf_op jit(solution)/shard_map/while/body/eval_jaxpr/all_to_all | solution.py:314
  175.3 10.1 %all-to-all-start = ((bf16[16,24,128]{2,1,0:T(8,128)(2,1)}), bf16[16,24,128]{2,1,0:T(8,128)(2,1)S(1)}, u32[]{:S(2)}, u32[]{:S(2)}) async-start(bf16[16,24,128]{2,1,0:T(8,128)(2,1)} %get-tuple-element.382), calls=%async_computation | async-start | bytes 196608 | tf_op jit(solution)/shard_map/while/body/eval_jaxpr/all_to_all | solution.py:314
  186.9 10.1 %all-to-all-start = ((bf16[16,24,128]{2,1,0:T(8,128)(2,1)}), bf16[16,24,128]{2,1,0:T(8,128)(2,1)S(1)}, u32[]{:S(2)}, u32[]{:S(2)}) async-start(bf16[16,24,128]{2,1,0:T(8,128)(2,1)} %get-tuple-element.382), calls=%async_computation | async-start | bytes 196608 | tf_op jit(solution)/shard_map/while/body/eval_jaxpr/all_to_all | solution.py:314
  198.5 10.1 %all-to-all-start = ((bf16[16,24,128]{2,1,0:T(8,128)(2,1)}), bf16[16,24,128]{2,1,0:T(8,128)(2,1)S(1)}, u32[]{:S(2)}, u32[]{:S(2)}) async-start(bf16[16,24,128]{2,1,0:T(8,128)(2,1)} %get-tuple-element.382), calls=%async_computation | async-start | bytes 196608 | tf_op jit(solution)/shard_map/while/body/eval_jaxpr/all_to_all | solution.py:314
  210.1 10.1 %all-to-all-start = ((bf16[16,24,128]{2,1,0:T(8,128)(2,1)}), bf16[16,24,128]{2,1,0:T(8,128)(2,1)S(1)}, u32[]{:S(2)}, u32[]{:S(2)}) async-start(bf16[16,24,128]{2,1,0:T(8,128)(2,1)} %get-tuple-element.382), calls=%async_computation | async-start | bytes 196608 | tf_op jit(solution)/shard_map/while/body/eval_jaxpr/all_to_all | solution.py:314
  221.8 10.1 %all-to-all-start = ((bf16[16,24,128]{2,1,0:T(8,128)(2,1)}), bf16[16,24,128]{2,1,0:T(8,128)(2,1)S(1)}, u32[]{:S(2)}, u32[]{:S(2)}) async-start(bf16[16,24,128]{2,1,0:T(8,128)(2,1)} %get-tuple-element.382), calls=%async_computation | async-start | bytes 196608 | tf_op jit(solution)/shard_map/while/body/eval_jaxpr/all_to_all | solution.py:314
  233.4 10.1 %all-to-all-start = ((bf16[16,24,128]{2,1,0:T(8,128)(2,1)}), bf16[16,24,128]{2,1,0:T(8,128)(2,1)S(1)}, u32[]{:S(2)}, u32[]{:S(2)}) async-start(bf16[16,24,128]{2,1,0:T(8,128)(2,1)} %get-tuple-element.382), calls=%async_computation | async-start | bytes 196608 | tf_op jit(solution)/shard_map/while/body/eval_jaxpr/all_to_all | solution.py:314
  245.0 10.8 %all-to-all-start = ((bf16[16,24,128]{2,1,0:T(8,128)(2,1)}), bf16[16,24,128]{2,1,0:T(8,128)(2,1)S(1)}, u32[]{:S(2)}, u32[]{:S(2)}) async-start(bf16[16,24,128]{2,1,0:T(8,128)(2,1)} %get-tuple-element.382), calls=%async_computation | async-start | bytes 196608 | tf_op jit(solution)/shard_map/while/body/eval_jaxpr/all_to_all | solution.py:314
  257.3 10.1 %all-to-all-start = ((bf16[16,24,128]{2,1,0:T(8,128)(2,1)}), bf16[16,24,128]{2,1,0:T(8,128)(2,1)S(1)}, u32[]{:S(2)}, u32[]{:S(2)}) async-start(bf16[16,24,128]{2,1,0:T(8,128)(2,1)} %get-tuple-element.382), calls=%async_computation | async-start | bytes 196608 | tf_op jit(solution)/shard_map/while/body/eval_jaxpr/all_to_all | solution.py:314
  268.9 10.1 %all-to-all-start = ((bf16[16,24,128]{2,1,0:T(8,128)(2,1)}), bf16[16,24,128]{2,1,0:T(8,128)(2,1)S(1)}, u32[]{:S(2)}, u32[]{:S(2)}) async-start(bf16[16,24,128]{2,1,0:T(8,128)(2,1)} %get-tuple-element.382), calls=%async_computation | async-start | bytes 196608 | tf_op jit(solution)/shard_map/while/body/eval_jaxpr/all_to_all | solution.py:314
  280.5 10.1 %all-to-all-start = ((bf16[16,24,128]{2,1,0:T(8,128)(2,1)}), bf16[16,24,128]{2,1,0:T(8,128)(2,1)S(1)}, u32[]{:S(2)}, u32[]{:S(2)}) async-start(bf16[16,24,128]{2,1,0:T(8,128)(2,1)} %get-tuple-element.382), calls=%async_computation | async-start | bytes 196608 | tf_op jit(solution)/shard_map/while/body/eval_jaxpr/all_to_all | solution.py:314
  358.5 29.9 %all-to-all-start.5 = ((bf16[16,4,2,24,256]{4,3,2,1,0:T(8,128)(2,1)}), bf16[16,4,2,24,256]{4,3,2,1,0:T(8,128)(2,1)}, u32[]{:S(2)}, u32[]{:S(2)}) async-start(bf16[16,4,2,24,256]{4,3,2,1,0:T(8,128)(2,1)} %owner_send.1), calls=%async_computation.5 | async-start | bytes 3145728 | tf_op jit(solution)/shard_map/all_to_all | solution.py:344
  (13 other events, 225.3 us)
